TPU v7x, 128 devices: a whole 4x4x4 slice. The times are simulated.
128 devices in a mesh: row: 8 (over z, core), col: 16 (over x, y).
Axes of the slice: x: 4, y: 4, z: 4, core: 2. Of those that a mesh axis runs over, the one named last changes fastest.
Arguments:
- covariance: float32 [9216, 9216], P('row', 'col'), as said below
- features: float32 [2, 9216, 128], P(None, ('row', 'col')), may hold values from -6 to 6
- noise: float32 [2, 128], replicated, may hold values from 2304 to 36864
Outputs:
- updated: float32 [9216, 9216], P('row', 'col')
Inputs may be any that keep to these rules, and one draw needn't show every extreme that they name: covariance is symmetric and positive definite.
All inputs are finite; a program needn't handle non-finite values.
Results may differ from a plain program's by a relative error of at most 0.0001.
Values sent between devices are 32-bit elements; how exact they have to be, the bound alone decides.
No kernel may reach another device: no remote copies, remote signals or barrier semaphores. Data moves between devices by JAX's collectives and lax.ppermute only.
A program may use at most 64 MiB of HBM per device.

v0:
```python
import jax
import jax.numpy as jnp
from jax import lax
from jax.experimental import pallas as pl
from jax.experimental.pallas import tpu as pltpu
from jax.sharding import PartitionSpec as P


HIGHEST = lax.Precision.HIGHEST
HIGH = lax.Precision.HIGH


def dot(a, b, dims, precision):
    return lax.dot_general(a, b, (dims, ((), ())), precision=precision, preferred_element_type=jnp.float32)


def to_xor(value, axis, bits):
    size = lax.axis_size(axis)
    return lax.ppermute(value, axis, [(i, i ^ bits) for i in range(size)])


def to_place(value, owner):
    return lax.ppermute(value, ("row", "col"), [(i, owner(i)) for i in range(128)])


def side(a, b, bit):
    first = jnp.where(bit == 0, a, b)
    second = jnp.where(bit == 0, b, a)
    return jnp.stack([first, second])


def feature_place(index):
    col, part = index // 8, index % 8
    return (2 * (part % 4) + part // 4) * 16 + col


def product_place(index):
    row, col = index // 16, index % 16
    return 8 * col + 4 * (row % 2) + row // 2


def to_plane(block):
    devices = lax.axis_size("col")
    sent = jnp.broadcast_to(block[None], (devices, *block.shape))
    return lax.all_to_all(sent, "col", 0, 0, tiled=True).reshape(-1, block.shape[-1])


def halves(a):
    high = a.astype(jnp.bfloat16)
    return high, (a - high.astype(jnp.float32)).astype(jnp.bfloat16)


def near_full(a, b, dims):
    (ah, al), (bh, bl) = a, b
    dims = (dims, ((), ()))

    def one(p, q):
        return lax.dot_general(p, q, dims, preferred_element_type=jnp.float32)

    return one(ah, bh) + (one(ah, bl) + one(al, bh))


def products_kernel(core_ref, cov_ref, rows_ref, cols_ref, kept_ref, given_ref, t_ref, m_ref):
    core = core_ref[0]
    block, share = t_ref.shape[0] // 8, m_ref.shape[0] // 8
    part = near_full(halves(cov_ref[...]), halves(rows_ref[...]), ((1,), (0,)))
    t_ref[...] = part
    m_ref[...] = near_full(halves(cols_ref[...]), halves(part), ((0,), (0,)))
    for ref, at in ((kept_ref, core), (given_ref, 1 - core)):
        for i in range(4):
            ref[i, :block, :] = t_ref[pl.ds(pl.multiple_of((4 * at + i) * block, 8), block), :]
            ref[i, block:, :] = m_ref[pl.ds(pl.multiple_of((4 * at + i) * share, 8), share), :]


def products(core, cov, rows, cols):
    n, width = cols.shape
    depth = n // 8 + width // 8
    exchange = jax.ShapeDtypeStruct((4, depth, width), jnp.float32)
    return pl.pallas_call(
        products_kernel,
        out_shape=(exchange, exchange),
        in_specs=[pl.BlockSpec(memory_space=pltpu.SMEM)] + [pl.BlockSpec(memory_space=pltpu.VMEM)] * 3,
        scratch_shapes=[pltpu.VMEM((n, width), jnp.float32), pltpu.VMEM((width, width), jnp.float32)],
        cost_estimate=pl.CostEstimate(
            flops=6 * n * width * (rows.shape[0] + width), bytes_accessed=4 * cov.size, transcendentals=0
        ),
        compiler_params=pltpu.CompilerParams(vmem_limit_bytes=16 << 20),
    )(core.reshape(1), cov, rows, cols)


def invert_kernel(m_ref, noise_ref, out_ref):
    n = m_ref.shape[0]
    eye = lax.broadcasted_iota(jnp.int32, (n, n), 0) == lax.broadcasted_iota(jnp.int32, (n, n), 1)
    one = jnp.where(eye, 1.0, 0.0).astype(jnp.float32)
    system = m_ref[...] + jnp.where(eye, noise_ref[...], 0.0)
    diag = jnp.where(eye, system, 0.0)
    across = lax.rsqrt(jnp.sum(diag, axis=0, keepdims=True))
    down = lax.rsqrt(jnp.sum(diag, axis=1, keepdims=True))
    scaled = system * down * across
    bound = jnp.max(jnp.sum(jnp.abs(scaled), axis=1, keepdims=True), axis=0, keepdims=True)
    alpha = 2.0 / (1.0 + bound)
    err = one - alpha * scaled
    start = alpha * (one + err)

    def fast(a, b):
        return jnp.dot(a.astype(jnp.bfloat16), b.astype(jnp.bfloat16), preferred_element_type=jnp.float32)

    def full(a, b):
        return jnp.dot(a, b, precision=HIGHEST, preferred_element_type=jnp.float32)

    err2 = fast(err, err)
    err4 = fast(err2, err2)
    guess = start + fast(start, err2)
    guess = guess + fast(guess, err4)

    def norm(r):
        return jnp.max(jnp.sum(jnp.abs(r), axis=0, keepdims=True))

    rest = one - full(scaled, guess)
    size = norm(rest)
    bad = size >= 0.5
    guess = jnp.where(bad, start, guess)

    def go_on(state):
        return jnp.logical_and(state[1] >= 1e-3, state[2] < 60)

    def refine(state):
        y = state[0]
        r = one - full(scaled, y)
        return y + full(y, r), norm(r), state[2] + 1

    guess, _, _ = lax.while_loop(go_on, refine, (guess, jnp.float32(1.0), jnp.int32(0)))
    out_ref[...] = guess * down * across


def inverse_of(m, noise):
    n = m.shape[0]
    return pl.pallas_call(
        invert_kernel,
        out_shape=jax.ShapeDtypeStruct((n, n), jnp.float32),
        cost_estimate=pl.CostEstimate(flops=2 * n**3 * 40, bytes_accessed=4 * n * n * 3, transcendentals=n),
        compiler_params=pltpu.CompilerParams(vmem_limit_bytes=4 << 20),
    )(m, noise)


def step(covariance, features, noise):
    r = lax.axis_index("row")
    z, core = r >> 1, r & 1
    steps, block, batch = features.shape
    width = steps * batch
    own = jnp.moveaxis(features, 0, 1).reshape(block, width)
    turned = covariance.T

    row_features = to_plane(own)
    apart = to_place(own, feature_place)
    za = side(apart, to_xor(apart, "row", 2), z & 1)
    zb = side(za, to_xor(za, "row", 6), z >> 1)
    column_features = side(zb, to_xor(zb, "row", 1), core).reshape(8 * block, width)

    kept, given = products(core, turned, row_features, column_features)
    mate = to_xor(given, "row", 1)

    def part(d):
        return lax.dynamic_index_in_dim(kept, z ^ d, 0, keepdims=False) + lax.dynamic_index_in_dim(
            mate, z ^ d, 0, keepdims=False
        )

    arrived = [to_xor(part(d), "row", 2 * d) for d in (2, 1, 3)]
    total = (part(0) + arrived[0]) + (arrived[1] + arrived[2])
    product, share = total[:block], total[block:]

    for bits in (1, 3, 4, 12):
        share = share + to_xor(share, "col", bits)
    shares = side(share, to_xor(share, "row", 2), z & 1)
    shares = side(shares, to_xor(shares, "row", 6), z >> 1)
    matrix = side(shares, to_xor(shares, "row", 1), core).reshape(width, width)

    cols = side(product, to_xor(product, "row", 2), z & 1)
    cols = side(cols, to_xor(cols, "row", 6), z >> 1)
    product_cols = side(cols, to_xor(cols, "row", 1), core).reshape(8 * block, width)

    product_rows = to_plane(to_place(product, product_place))

    inverse = inverse_of(matrix, noise.reshape(1, width))
    gain = dot(product_cols, inverse, ((1,), (0,)), HIGH)
    return (turned - dot(gain, product_rows, ((1,), (1,)), HIGH)).T


def solution(mesh):
    specs = (P("row", "col"), P(None, ("row", "col"), None), P())
    return jax.shard_map(step, mesh=mesh, in_specs=specs, out_specs=P("row", "col"), check_vma=False)
```

profile of v0, /device:TPU:0, one launch (start us, length us, event | category | flops | bytes accessed | tf_op | source)
XLA Modules:
  0.0 117.7 jit_solution(964833902105746437)
XLA Ops:
  0.0 0.9 copy-done
  1.6 9.3 %collective-permute-start.1 = (f32[72,256]{1,0:T(8,128)S(1)}, f32[72,256]{1,0:T(8,128)S(1)}, u32[]{:S(2)}, u32[]{:S(2)}) collective-permute-start(f32[72,256]{1,0:T(8,128)S(1)} %collective-permute-done), channel_id=1, source_target_pairs={{0,32},{16,48},{32,0},{48,16},{64,96},{80,112},{96,64},{112,80},{1... | collective-permute-start | bytes 221192 | tf_op jit(solution)/shard_map/ppermute | solution.py:19
  10.8 3.0 %collective-permute-done.1 = f32[72,256]{1,0:T(8,128)S(1)} collective-permute-done((f32[72,256]{1,0:T(8,128)S(1)}, f32[72,256]{1,0:T(8,128)S(1)}, u32[]{:S(2)}, u32[]{:S(2)}) %collective-permute-start.1) | collective-permute-done | bytes 73760 | tf_op jit(solution)/shard_map/ppermute | solution.py:19
  13.9 7.5 %collective-permute-start.2 = (f32[2,72,256]{2,1,0:T(8,128)S(1)}, f32[2,72,256]{2,1,0:T(8,128)S(1)}, u32[]{:S(2)}, u32[]{:S(2)}) collective-permute-start(f32[2,72,256]{2,1,0:T(8,128)S(1)} %pad_maximum_fusion.5), channel_id=1, source_target_pairs={{0,96},{16,112},{32,64},{48,80},{64,32},{80,48},{96,0},{112,16},{1... | collective-permute-start | bytes 442376 | tf_op jit(solution)/shard_map/ppermute | solution.py:19
  21.4 1.1 broadcast_in_dim.14
  22.5 4.9 %all-to-all-start = ((f32[16,72,256]{2,1,0:T(8,128)}), f32[16,72,256]{2,1,0:T(8,128)}, u32[]{:S(2)}, u32[]{:S(2)}) async-start(f32[16,72,256]{2,1,0:T(8,128)} %broadcast_in_dim.14), calls=%async_computation | async-start | bytes 2359296 | tf_op jit(solution)/shard_map/all_to_all | solution.py:45
  27.6 1.7 %collective-permute-done.3 = f32[2,2,72,256]{3,2,1,0:T(8,128)} collective-permute-done((f32[2,2,72,256]{3,2,1,0:T(8,128)S(1)}, f32[2,2,72,256]{3,2,1,0:T(8,128)}, u32[]{:S(2)}, u32[]{:S(2)}) %collective-permute-start.3) | collective-permute-done | bytes 294944 | tf_op jit(solution)/shard_map/ppermute | solution.py:19
  29.3 1.0 select_bitcast_fusion.3
  30.4 13.4 %all-to-all-done = f32[16,72,256]{2,1,0:T(8,128)} async-done(((f32[16,72,256]{2,1,0:T(8,128)}), f32[16,72,256]{2,1,0:T(8,128)}, u32[]{:S(2)}, u32[]{:S(2)}) %all-to-all-start) | async-done | bytes 1179680 | tf_op jit(solution)/shard_map/all_to_all | solution.py:45
  43.8 4.3 %shard_map.37 = (f32[4,104,256]{2,1,0:T(8,128)S(1)}, f32[4,104,256]{2,1,0:T(8,128)}) custom-call(s32[1]{0:T(128)} %bitcast.core_ref, f32[576,1152]{1,0:T(8,128)S(1)} %bitcast.64, f32[1152,256]{1,0:T(8,128)} %bitcast.3.rows_ref, f32[576,256]{1,0:T(8,128)S(1)} %bitcast.65), custom_call_target="tpu_custom_call" | custom-call | flops 1245708288 | bytes 2654208 | tf_op jit(solution)/shard_map/pallas_call | solution.py:79
  48.9 2.0 %collective-permute-done.4 = f32[4,104,256]{2,1,0:T(8,128)S(1)} collective-permute-done((f32[4,104,256]{2,1,0:T(8,128)}, f32[4,104,256]{2,1,0:T(8,128)S(1)}, u32[]{:S(2)}, u32[]{:S(2)}) %collective-permute-start.4) | collective-permute-done | bytes 426016 | tf_op jit(solution)/shard_map/ppermute | solution.py:19
  50.9 1.7 %add_bitcast_fusion = (f32[104,256]{1,0:T(8,128)}, f32[104,256]{1,0:T(8,128)}, f32[104,256]{1,0:T(8,128)}) fusion(f32[4,104,256]{2,1,0:T(8,128)S(1)} %collective-permute-done.4, s32[]{:T(128)S(6)} %select_n.125, f32[4,104,256]{2,1,0:T(8,128)} %copy-done.2, s32[]{:T(128)S(6)} %select_n.124, s32[]{:T(128)S(6)} %select_n.123), kind=kLoop, calls=%fused_computation.21 | loop fusion | flops 79872 | bytes 958476 | tf_op jit(solution)/shard_map/add | solution.py:164
  52.6 2.4 %collective-permute-start.7 = (f32[104,256]{1,0:T(8,128)}, f32[104,256]{1,0:T(8,128)S(1)}, u32[]{:S(2)}, u32[]{:S(2)}) collective-permute-start(f32[104,256]{1,0:T(8,128)} %get-tuple-element.9), channel_id=1, source_target_pairs={{0,96},{16,112},{32,64},{48,80},{64,32},{80,48},{96,0},{112,16},{1... | collective-permute-start | bytes 319496 | tf_op jit(solution)/shard_map/ppermute | solution.py:19
  54.9 2.3 %collective-permute-start.5 = (f32[104,256]{1,0:T(8,128)}, f32[104,256]{1,0:T(8,128)S(1)}, u32[]{:S(2)}, u32[]{:S(2)}) collective-permute-start(f32[104,256]{1,0:T(8,128)} %get-tuple-element.11), channel_id=1, source_target_pairs={{0,64},{16,80},{32,96},{48,112},{64,0},{80,16},{96,32},{112,48},{1... | collective-permute-start | bytes 319496 | tf_op jit(solution)/shard_map/ppermute | solution.py:19
  57.3 1.7 %collective-permute-done.7 = f32[104,256]{1,0:T(8,128)S(1)} collective-permute-done((f32[104,256]{1,0:T(8,128)}, f32[104,256]{1,0:T(8,128)S(1)}, u32[]{:S(2)}, u32[]{:S(2)}) %collective-permute-start.7) | collective-permute-done | bytes 106528 | tf_op jit(solution)/shard_map/ppermute | solution.py:19
  59.0 2.0 %collective-permute-done.6 = f32[104,256]{1,0:T(8,128)S(1)} collective-permute-done((f32[104,256]{1,0:T(8,128)}, f32[104,256]{1,0:T(8,128)S(1)}, u32[]{:S(2)}, u32[]{:S(2)}) %collective-permute-start.6) | collective-permute-done | bytes 106528 | tf_op jit(solution)/shard_map/ppermute | solution.py:19
  61.0 1.5 %collective-permute-done.5 = f32[104,256]{1,0:T(8,128)S(1)} collective-permute-done((f32[104,256]{1,0:T(8,128)}, f32[104,256]{1,0:T(8,128)S(1)}, u32[]{:S(2)}, u32[]{:S(2)}) %collective-permute-start.5) | collective-permute-done | bytes 106528 | tf_op jit(solution)/shard_map/ppermute | solution.py:19
  62.5 1.0 fusion
  64.1 3.3 %collective-permute-done.12 = f32[32,256]{1,0:T(8,128)S(1)} collective-permute-done((f32[32,256]{1,0:T(8,128)S(1)}, f32[32,256]{1,0:T(8,128)S(1)}, u32[]{:S(2)}, u32[]{:S(2)}) %collective-permute-start.12) | collective-permute-done | bytes 32800 | tf_op jit(solution)/shard_map/ppermute | solution.py:19
  68.8 3.8 %collective-permute-done.13 = f32[32,256]{1,0:T(8,128)S(1)} collective-permute-done((f32[32,256]{1,0:T(8,128)S(1)}, f32[32,256]{1,0:T(8,128)S(1)}, u32[]{:S(2)}, u32[]{:S(2)}) %collective-permute-start.13) | collective-permute-done | bytes 32800 | tf_op jit(solution)/shard_map/ppermute | solution.py:19
  72.8 3.7 %collective-permute-done.14 = f32[32,256]{1,0:T(8,128)S(1)} collective-permute-done((f32[32,256]{1,0:T(8,128)S(1)}, f32[32,256]{1,0:T(8,128)S(1)}, u32[]{:S(2)}, u32[]{:S(2)}) %collective-permute-start.14) | collective-permute-done | bytes 32800 | tf_op jit(solution)/shard_map/ppermute | solution.py:19
  76.5 1.3 %collective-permute-start.15 = (f32[32,256]{1,0:T(8,128)S(1)}, f32[32,256]{1,0:T(8,128)S(1)}, u32[]{:S(2)}, u32[]{:S(2)}) collective-permute-start(f32[32,256]{1,0:T(8,128)S(1)} %add.79), channel_id=1, source_target_pairs={{0,12},{1,13},{2,14},{3,15},{4,8},{5,9},{6,10},{7,11},{8,4},{9,5},... | collective-permute-start | bytes 98312 | tf_op jit(solution)/shard_map/ppermute | solution.py:19
  78.5 3.1 %collective-permute-done.15 = f32[32,256]{1,0:T(8,128)S(1)} collective-permute-done((f32[32,256]{1,0:T(8,128)S(1)}, f32[32,256]{1,0:T(8,128)S(1)}, u32[]{:S(2)}, u32[]{:S(2)}) %collective-permute-start.15) | collective-permute-done | bytes 32800 | tf_op jit(solution)/shard_map/ppermute | solution.py:19
  81.6 0.9 collective-permute-start.16
  82.6 3.0 %collective-permute-done.16 = f32[32,256]{1,0:T(8,128)S(1)} collective-permute-done((f32[32,256]{1,0:T(8,128)S(1)}, f32[32,256]{1,0:T(8,128)S(1)}, u32[]{:S(2)}, u32[]{:S(2)}) %collective-permute-start.16) | collective-permute-done | bytes 32800 | tf_op jit(solution)/shard_map/ppermute | solution.py:19
  85.6 2.4 %collective-permute-start.17 = (f32[2,32,256]{2,1,0:T(8,128)S(1)}, f32[2,32,256]{2,1,0:T(8,128)S(1)}, u32[]{:S(2)}, u32[]{:S(2)}) collective-permute-start(f32[2,32,256]{2,1,0:T(8,128)S(1)} %pad_maximum_fusion.8), channel_id=1, source_target_pairs={{0,96},{16,112},{32,64},{48,80},{64,32},{80,48},{96,0},{112,16},{1... | collective-permute-start | bytes 196616 | tf_op jit(solution)/shard_map/ppermute | solution.py:19
  88.0 1.0 collective-permute-start.10
  89.0 1.1 broadcast_in_dim.15
  90.1 4.7 %all-to-all-start.1 = ((f32[16,72,256]{2,1,0:T(8,128)}), f32[16,72,256]{2,1,0:T(8,128)}, u32[]{:S(2)}, u32[]{:S(2)}) async-start(f32[16,72,256]{2,1,0:T(8,128)} %broadcast_in_dim.15), calls=%async_computation.1 | async-start | bytes 2359296 | tf_op jit(solution)/shard_map/all_to_all | solution.py:45
  96.3 9.2 %shard_map.38 = f32[256,256]{1,0:T(8,128)S(1)} custom-call(f32[256,256]{1,0:T(8,128)S(1)} %bitcast.66, f32[1,256]{1,0:T(1,128)S(1)} %bitcast.67), custom_call_target="tpu_custom_call" | custom-call | flops 1342177280 | bytes 786432 | tf_op jit(solution)/shard_map/pallas_call | solution.py:138
  106.1 7.4 %all-to-all-done.1 = f32[16,72,256]{2,1,0:T(8,128)} async-done(((f32[16,72,256]{2,1,0:T(8,128)}), f32[16,72,256]{2,1,0:T(8,128)}, u32[]{:S(2)}, u32[]{:S(2)}) %all-to-all-start.1) | async-done | bytes 1179680 | tf_op jit(solution)/shard_map/all_to_all | solution.py:45
  113.5 4.2 %convolution_subtract_fusion = f32[1152,576]{0,1:T(8,128)} fusion(f32[1152,576]{0,1:T(8,128)S(1)} %copy-done.1, f32[1152,256]{1,0:T(8,128)} %bitcast.15, f32[576,256]{1,0:T(8,128)S(1)} %fusion.1), kind=kOutput, calls=%fused_computation | convolution fusion | flops 1019879424 | bytes 7077888 | tf_op jit(solution)/shard_map/dot_general | solution.py:14
  (51 shorter events, 6.6 us)
Async XLA Ops:
  0.0 0.9 copy-start
  0.9 0.7 collective-permute-start
  1.6 12.3 %collective-permute-start.1 = (f32[72,256]{1,0:T(8,128)S(1)}, f32[72,256]{1,0:T(8,128)S(1)}, u32[]{:S(2)}, u32[]{:S(2)}) collective-permute-start(f32[72,256]{1,0:T(8,128)S(1)} %collective-permute-done), channel_id=1, source_target_pairs={{0,32},{16,48},{32,0},{48,16},{64,96},{80,112},{96,64},{112,80},{1... | collective-permute-start | bytes 221192 | tf_op jit(solution)/shard_map/ppermute | solution.py:19
  13.9 13.5 %collective-permute-start.2 = (f32[2,72,256]{2,1,0:T(8,128)S(1)}, f32[2,72,256]{2,1,0:T(8,128)S(1)}, u32[]{:S(2)}, u32[]{:S(2)}) collective-permute-start(f32[2,72,256]{2,1,0:T(8,128)S(1)} %pad_maximum_fusion.5), channel_id=1, source_target_pairs={{0,96},{16,112},{32,64},{48,80},{64,32},{80,48},{96,0},{112,16},{1... | collective-permute-start | bytes 442376 | tf_op jit(solution)/shard_map/ppermute | solution.py:19
  22.5 21.3 %all-to-all-start = ((f32[16,72,256]{2,1,0:T(8,128)}), f32[16,72,256]{2,1,0:T(8,128)}, u32[]{:S(2)}, u32[]{:S(2)}) async-start(f32[16,72,256]{2,1,0:T(8,128)} %broadcast_in_dim.14), calls=%async_computation | async-start | bytes 2359296 | tf_op jit(solution)/shard_map/all_to_all | solution.py:45
  27.4 16.3 %copy-start.1 = (f32[1152,576]{0,1:T(8,128)S(1)}, f32[1152,576]{0,1:T(8,128)}, u32[]{:S(2)}) copy-start(f32[1152,576]{0,1:T(8,128)} %param.3) | copy-start | bytes 7962628
  27.5 1.8 %collective-permute-start.3 = (f32[2,2,72,256]{3,2,1,0:T(8,128)S(1)}, f32[2,2,72,256]{3,2,1,0:T(8,128)}, u32[]{:S(2)}, u32[]{:S(2)}) collective-permute-start(f32[2,2,72,256]{3,2,1,0:T(8,128)S(1)} %pad_maximum_fusion.2), channel_id=1, source_target_pairs={{0,16},{16,0},{32,48},{48,32},{64,80},{80,64},{96,112},{112,96},{1... | collective-permute-start | bytes 884744 | tf_op jit(solution)/shard_map/ppermute | solution.py:19
  48.1 0.8 copy-start.2
  48.9 2.0 %collective-permute-start.4 = (f32[4,104,256]{2,1,0:T(8,128)}, f32[4,104,256]{2,1,0:T(8,128)S(1)}, u32[]{:S(2)}, u32[]{:S(2)}) collective-permute-start(f32[4,104,256]{2,1,0:T(8,128)} %get-tuple-element.8), channel_id=1, source_target_pairs={{0,16},{16,0},{32,48},{48,32},{64,80},{80,64},{96,112},{112,96},{1... | collective-permute-start | bytes 1277960 | tf_op jit(solution)/shard_map/ppermute | solution.py:19
  52.6 6.4 %collective-permute-start.7 = (f32[104,256]{1,0:T(8,128)}, f32[104,256]{1,0:T(8,128)S(1)}, u32[]{:S(2)}, u32[]{:S(2)}) collective-permute-start(f32[104,256]{1,0:T(8,128)} %get-tuple-element.9), channel_id=1, source_target_pairs={{0,96},{16,112},{32,64},{48,80},{64,32},{80,48},{96,0},{112,16},{1... | collective-permute-start | bytes 319496 | tf_op jit(solution)/shard_map/ppermute | solution.py:19
  54.9 6.1 %collective-permute-start.6 = (f32[104,256]{1,0:T(8,128)}, f32[104,256]{1,0:T(8,128)S(1)}, u32[]{:S(2)}, u32[]{:S(2)}) collective-permute-start(f32[104,256]{1,0:T(8,128)} %get-tuple-element.10), channel_id=1, source_target_pairs={{0,32},{16,48},{32,0},{48,16},{64,96},{80,112},{96,64},{112,80},{1... | collective-permute-start | bytes 319496 | tf_op jit(solution)/shard_map/ppermute | solution.py:19
  54.9 7.5 %collective-permute-start.5 = (f32[104,256]{1,0:T(8,128)}, f32[104,256]{1,0:T(8,128)S(1)}, u32[]{:S(2)}, u32[]{:S(2)}) collective-permute-start(f32[104,256]{1,0:T(8,128)} %get-tuple-element.11), channel_id=1, source_target_pairs={{0,64},{16,80},{32,96},{48,112},{64,0},{80,16},{96,32},{112,48},{1... | collective-permute-start | bytes 319496 | tf_op jit(solution)/shard_map/ppermute | solution.py:19
  63.4 4.0 %collective-permute-start.12 = (f32[32,256]{1,0:T(8,128)S(1)}, f32[32,256]{1,0:T(8,128)S(1)}, u32[]{:S(2)}, u32[]{:S(2)}) collective-permute-start(f32[32,256]{1,0:T(8,128)S(1)} %slice.9), channel_id=1, source_target_pairs={{0,1},{1,0},{2,3},{3,2},{4,5},{5,4},{6,7},{7,6},{8,9},{9,8},{10,11... | collective-permute-start | bytes 98312 | tf_op jit(solution)/shard_map/ppermute | solution.py:19
  67.4 5.1 %collective-permute-start.13 = (f32[32,256]{1,0:T(8,128)S(1)}, f32[32,256]{1,0:T(8,128)S(1)}, u32[]{:S(2)}, u32[]{:S(2)}) collective-permute-start(f32[32,256]{1,0:T(8,128)S(1)} %slice_add_fusion), channel_id=1, source_target_pairs={{0,3},{1,2},{2,1},{3,0},{4,7},{5,6},{6,5},{7,4},{8,11},{9,10},{10,... | collective-permute-start | bytes 98312 | tf_op jit(solution)/shard_map/ppermute | solution.py:19
  68.3 14.3 %collective-permute-start.9 = (f32[72,256]{1,0:T(8,128)S(1)}, f32[72,256]{1,0:T(8,128)S(1)}, u32[]{:S(2)}, u32[]{:S(2)}) collective-permute-start(f32[72,256]{1,0:T(8,128)S(1)} %slice.8), channel_id=1, source_target_pairs={{0,32},{16,48},{32,0},{48,16},{64,96},{80,112},{96,64},{112,80},{1... | collective-permute-start | bytes 221192 | tf_op jit(solution)/shard_map/ppermute | solution.py:19
  72.6 3.9 %collective-permute-start.14 = (f32[32,256]{1,0:T(8,128)S(1)}, f32[32,256]{1,0:T(8,128)S(1)}, u32[]{:S(2)}, u32[]{:S(2)}) collective-permute-start(f32[32,256]{1,0:T(8,128)S(1)} %add.78), channel_id=1, source_target_pairs={{0,4},{1,5},{2,6},{3,7},{4,0},{5,1},{6,2},{7,3},{8,12},{9,13},{10,... | collective-permute-start | bytes 98312 | tf_op jit(solution)/shard_map/ppermute | solution.py:19
  76.5 5.1 %collective-permute-start.15 = (f32[32,256]{1,0:T(8,128)S(1)}, f32[32,256]{1,0:T(8,128)S(1)}, u32[]{:S(2)}, u32[]{:S(2)}) collective-permute-start(f32[32,256]{1,0:T(8,128)S(1)} %add.79), channel_id=1, source_target_pairs={{0,12},{1,13},{2,14},{3,15},{4,8},{5,9},{6,10},{7,11},{8,4},{9,5},... | collective-permute-start | bytes 98312 | tf_op jit(solution)/shard_map/ppermute | solution.py:19
  77.8 11.2 %collective-permute-start.8 = (f32[72,256]{1,0:T(8,128)S(1)}, f32[72,256]{1,0:T(8,128)S(1)}, u32[]{:S(2)}, u32[]{:S(2)}) collective-permute-start(f32[72,256]{1,0:T(8,128)S(1)} %slice.8), channel_id=1, source_target_pairs={{0,0},{1,8},{2,16},{3,24},{4,32},{5,40},{6,48},{7,56},{8,64},{9,72... | collective-permute-start | bytes 221192 | tf_op jit(solution)/shard_map/ppermute | solution.py:23
  81.6 3.9 %collective-permute-start.16 = (f32[32,256]{1,0:T(8,128)S(1)}, f32[32,256]{1,0:T(8,128)S(1)}, u32[]{:S(2)}, u32[]{:S(2)}) collective-permute-start(f32[32,256]{1,0:T(8,128)S(1)} %add.80), channel_id=1, source_target_pairs={{0,32},{16,48},{32,0},{48,16},{64,96},{80,112},{96,64},{112,80},{1... | collective-permute-start | bytes 98312 | tf_op jit(solution)/shard_map/ppermute | solution.py:19
  85.6 9.2 %collective-permute-start.17 = (f32[2,32,256]{2,1,0:T(8,128)S(1)}, f32[2,32,256]{2,1,0:T(8,128)S(1)}, u32[]{:S(2)}, u32[]{:S(2)}) collective-permute-start(f32[2,32,256]{2,1,0:T(8,128)S(1)} %pad_maximum_fusion.8), channel_id=1, source_target_pairs={{0,96},{16,112},{32,64},{48,80},{64,32},{80,48},{96,0},{112,16},{1... | collective-permute-start | bytes 196616 | tf_op jit(solution)/shard_map/ppermute | solution.py:19
  88.0 6.9 %collective-permute-start.10 = (f32[2,72,256]{2,1,0:T(8,128)S(1)}, f32[2,72,256]{2,1,0:T(8,128)S(1)}, u32[]{:S(2)}, u32[]{:S(2)}) collective-permute-start(f32[2,72,256]{2,1,0:T(8,128)S(1)} %pad_maximum_fusion.6), channel_id=1, source_target_pairs={{0,96},{16,112},{32,64},{48,80},{64,32},{80,48},{96,0},{112,16},{1... | collective-permute-start | bytes 442376 | tf_op jit(solution)/shard_map/ppermute | solution.py:19
  90.1 23.4 %all-to-all-start.1 = ((f32[16,72,256]{2,1,0:T(8,128)}), f32[16,72,256]{2,1,0:T(8,128)}, u32[]{:S(2)}, u32[]{:S(2)}) async-start(f32[16,72,256]{2,1,0:T(8,128)} %broadcast_in_dim.15), calls=%async_computation.1 | async-start | bytes 2359296 | tf_op jit(solution)/shard_map/all_to_all | solution.py:45
  94.8 1.5 %copy-start.3 = (f32[2,128]{1,0:T(2,128)S(1)}, f32[2,128]{1,0:T(2,128)}, u32[]{:S(2)}) copy-start(f32[2,128]{1,0:T(2,128)} %param.5) | copy-start | bytes 3076
  94.8 1.4 %collective-permute-start.18 = (f32[2,2,32,256]{3,2,1,0:T(8,128)S(1)}, f32[2,2,32,256]{3,2,1,0:T(8,128)S(1)}, u32[]{:S(2)}, u32[]{:S(2)}) collective-permute-start(f32[2,2,32,256]{3,2,1,0:T(8,128)S(1)} %pad_maximum_fusion.7), channel_id=1, source_target_pairs={{0,16},{16,0},{32,48},{48,32},{64,80},{80,64},{96,112},{112,96},{1... | collective-permute-start | bytes 393224 | tf_op jit(solution)/shard_map/ppermute | solution.py:19
  95.0 10.6 %collective-permute-start.11 = (f32[2,2,72,256]{3,2,1,0:T(8,128)S(1)}, f32[2,2,72,256]{3,2,1,0:T(8,128)S(1)}, u32[]{:S(2)}, u32[]{:S(2)}) collective-permute-start(f32[2,2,72,256]{3,2,1,0:T(8,128)S(1)} %pad_maximum_fusion.3), channel_id=1, source_target_pairs={{0,16},{16,0},{32,48},{48,32},{64,80},{80,64},{96,112},{112,96},{1... | collective-permute-start | bytes 884744 | tf_op jit(solution)/shard_map/ppermute | solution.py:19
where the time goes:
time: 118 us
  waiting for transfers between devices  50.4 us (43%)
  starting transfers between devices  40.9 us (35%)
  Pallas kernels  13.6 us (12%)
  matrix products  4.58 us (4%)
  other arithmetic  4.11 us (3%)
  local copies, waits for them, and re-layouts  3.86 us (3%)
    ppermute x17, starting transfers between devices, to_xor(): return lax.ppermute(value, axis, [(i, i ^ bits) for i in range(size)])  30.1 us
    ppermute x17, waiting for transfers between devices, to_xor(): return lax.ppermute(value, axis, [(i, i ^ bits) for i in range(size)])  29.5 us
    all_to_all x2, waiting for transfers between devices, to_plane(): lax.all_to_all(sent, 'col', 0, 0, tiled=True).reshape(-1, block.shape[-1])  20.9 us
    all_to_all x2, starting transfers between devices, to_plane(): lax.all_to_all(sent, 'col', 0, 0, tiled=True).reshape(-1, block.shape[-1])  9.51 us
    pallas_call x1, Pallas kernels, inverse_of(): pl.pallas_call(invert_kernel, out_shape=jax.ShapeDtypeStruct((n, n), jnp....  9.24 us
    dot_general x2, matrix products, dot(): lax.dot_general(a, b, (dims, ((), ())), precision=precision, preferred_el...  4.58 us
    pallas_call x1, Pallas kernels, products(): pl.pallas_call(products_kernel, out_shape=(exchange, exchange), in_specs=...  4.33 us
  transfers between devices with their start and end apart: 21, of which 14 were waited for; matrix products, arithmetic and copies ran while one was open for 3% of the time, Pallas kernels for 8%

commit v1 on v0

--- a/solution.py
+++ b/solution.py
@@ -10,10 +10,6 @@
 HIGH = lax.Precision.HIGH
 
 
-def dot(a, b, dims, precision):
-    return lax.dot_general(a, b, (dims, ((), ())), precision=precision, preferred_element_type=jnp.float32)
-
-
 def to_xor(value, axis, bits):
     size = lax.axis_size(axis)
     return lax.ppermute(value, axis, [(i, i ^ bits) for i in range(size)])
@@ -60,32 +56,120 @@
     return one(ah, bh) + (one(ah, bl) + one(al, bh))
 
 
-def products_kernel(core_ref, cov_ref, rows_ref, cols_ref, kept_ref, given_ref, t_ref, m_ref):
+def products_kernel(core_ref, cov_ref, rows_ref, own_ref, other_ref, kept_ref, given_ref, t_ref, m_ref, cols_ref):
     core = core_ref[0]
     block, share = t_ref.shape[0] // 8, m_ref.shape[0] // 8
-    part = near_full(halves(cov_ref[...]), halves(rows_ref[...]), ((1,), (0,)))
-    t_ref[...] = part
-    m_ref[...] = near_full(halves(cols_ref[...]), halves(part), ((0,), (0,)))
+    cut = 2 * block
+    right = halves(rows_ref[...])
+    cols_ref[pl.ds(pl.multiple_of(core * 4 * block, 8), 4 * block), :] = own_ref[...]
+    cols_ref[pl.ds(pl.multiple_of((1 - core) * 4 * block, 8), 4 * block), :] = other_ref[...]
+    for i in range(4):
+        t_ref[pl.ds(i * cut, cut), :] = near_full(halves(cov_ref[pl.ds(i * cut, cut), :]), right, ((1,), (0,)))
+    m_ref[...] = near_full(halves(cols_ref[...]), halves(t_ref[...]), ((0,), (0,)))
     for ref, at in ((kept_ref, core), (given_ref, 1 - core)):
         for i in range(4):
             ref[i, :block, :] = t_ref[pl.ds(pl.multiple_of((4 * at + i) * block, 8), block), :]
             ref[i, block:, :] = m_ref[pl.ds(pl.multiple_of((4 * at + i) * share, 8), share), :]
 
 
-def products(core, cov, rows, cols):
-    n, width = cols.shape
+SCALAR = pl.BlockSpec(memory_space=pltpu.SMEM)
+VMEM = pl.BlockSpec(memory_space=pltpu.VMEM)
+
+
+def products(core, cov, rows, own, other):
+    n, width = 2 * own.shape[0], own.shape[1]
     depth = n // 8 + width // 8
-    exchange = jax.ShapeDtypeStruct((4, depth, width), jnp.float32)
+    exchange = pltpu.VMEM((4, depth, width), jnp.float32)
     return pl.pallas_call(
         products_kernel,
         out_shape=(exchange, exchange),
-        in_specs=[pl.BlockSpec(memory_space=pltpu.SMEM)] + [pl.BlockSpec(memory_space=pltpu.VMEM)] * 3,
-        scratch_shapes=[pltpu.VMEM((n, width), jnp.float32), pltpu.VMEM((width, width), jnp.float32)],
+        in_specs=[SCALAR, VMEM, VMEM, VMEM, VMEM],
+        out_specs=(VMEM, VMEM),
+        scratch_shapes=[
+            pltpu.VMEM((n, width), jnp.float32),
+            pltpu.VMEM((width, width), jnp.float32),
+            pltpu.VMEM((n, width), jnp.float32),
+        ],
         cost_estimate=pl.CostEstimate(
             flops=6 * n * width * (rows.shape[0] + width), bytes_accessed=4 * cov.size, transcendentals=0
         ),
-        compiler_params=pltpu.CompilerParams(vmem_limit_bytes=16 << 20),
-    )(core.reshape(1), cov, rows, cols)
+        compiler_params=pltpu.CompilerParams(vmem_limit_bytes=20 << 20),
+    )(core.reshape(1), cov, rows, own, other)
+
+
+def pieces_kernel(z_ref, kept_ref, mate_ref, *out_refs):
+    for d, ref in enumerate(out_refs):
+        at = z_ref[0] ^ d
+        ref[...] = kept_ref[at] + mate_ref[at]
+
+
+def pieces(z, kept, mate):
+    piece = pltpu.VMEM(kept.shape[1:], jnp.float32)
+    return pl.pallas_call(
+        pieces_kernel,
+        out_shape=(piece,) * 4,
+        in_specs=[SCALAR, VMEM, VMEM],
+        out_specs=(VMEM,) * 4,
+        compiler_params=pltpu.CompilerParams(vmem_limit_bytes=4 << 20),
+    )(z.reshape(1), kept, mate)
+
+
+def total_kernel(a_ref, b_ref, c_ref, d_ref, product_ref, share_ref):
+    total = (a_ref[...] + b_ref[...]) + (c_ref[...] + d_ref[...])
+    product_ref[...] = total[: product_ref.shape[0]]
+    share_ref[...] = total[product_ref.shape[0] :]
+
+
+def totals(terms, block):
+    depth, width = terms[0].shape
+    return pl.pallas_call(
+        total_kernel,
+        out_shape=(pltpu.VMEM((block, width), jnp.float32), pltpu.VMEM((depth - block, width), jnp.float32)),
+        in_specs=[VMEM] * 4,
+        out_specs=(VMEM, VMEM),
+        compiler_params=pltpu.CompilerParams(vmem_limit_bytes=4 << 20),
+    )(*terms)
+
+
+def gain_kernel(core_ref, own_ref, other_ref, inv_ref, out_ref):
+    core, half = core_ref[0], own_ref.shape[0]
+    inverse = halves(inv_ref[...])
+    for ref, at in ((own_ref, core), (other_ref, 1 - core)):
+        out_ref[pl.ds(pl.multiple_of(at * half, 8), half), :] = near_full(halves(ref[...]), inverse, ((1,), (0,)))
+
+
+def gain_of(core, own, other, inverse):
+    return pl.pallas_call(
+        gain_kernel,
+        out_shape=pltpu.VMEM((2 * own.shape[0], own.shape[1]), jnp.float32),
+        in_specs=[SCALAR, VMEM, VMEM, VMEM],
+        out_specs=VMEM,
+        compiler_params=pltpu.CompilerParams(vmem_limit_bytes=6 << 20),
+    )(core.reshape(1), own, other, inverse)
+
+
+def hold_kernel(far_ref, near_ref, sems):
+    cut = near_ref.shape[0] // 4
+    copies = [
+        pltpu.make_async_copy(far_ref.at[pl.ds(i * cut, cut)], near_ref.at[pl.ds(i * cut, cut)], sems.at[i])
+        for i in range(4)
+    ]
+    for copy in copies:
+        copy.start()
+    for copy in copies:
+        copy.wait()
+
+
+def hold(cov):
+    cov = pltpu.with_memory_space_constraint(cov, pltpu.HBM)
+    return pl.pallas_call(
+        hold_kernel,
+        out_shape=pltpu.VMEM(cov.shape, jnp.float32),
+        in_specs=[pl.BlockSpec(memory_space=pltpu.HBM)],
+        out_specs=VMEM,
+        scratch_shapes=[pltpu.SemaphoreType.DMA((4,))],
+        compiler_params=pltpu.CompilerParams(vmem_limit_bytes=4 << 20),
+    )(cov)
 
 
 def invert_kernel(m_ref, noise_ref, out_ref):
@@ -118,18 +202,22 @@
 
     rest = one - full(scaled, guess)
     size = norm(rest)
-    bad = size >= 0.5
-    guess = jnp.where(bad, start, guess)
+    slow = size >= 0.5
 
     def go_on(state):
-        return jnp.logical_and(state[1] >= 1e-3, state[2] < 60)
+        return jnp.logical_and(state[2] >= 1e-3, state[3] < 60)
 
     def refine(state):
-        y = state[0]
+        y, r, _, count = state
+        y = y + full(y, r)
         r = one - full(scaled, y)
-        return y + full(y, r), norm(r), state[2] + 1
-
-    guess, _, _ = lax.while_loop(go_on, refine, (guess, jnp.float32(1.0), jnp.int32(0)))
+        return y, r, norm(r), count + 1
+
+    guess, rest = lax.cond(
+        slow, lambda: (start, one - full(scaled, start)), lambda: (guess, rest)
+    )
+    guess, rest, _, _ = lax.while_loop(go_on, refine, (guess, rest, size, jnp.int32(0)))
+    guess = guess + full(guess, rest)
     out_ref[...] = guess * down * across
 
 
@@ -149,25 +237,17 @@
     steps, block, batch = features.shape
     width = steps * batch
     own = jnp.moveaxis(features, 0, 1).reshape(block, width)
-    turned = covariance.T
+    turned = hold(covariance.T)
 
     row_features = to_plane(own)
     apart = to_place(own, feature_place)
     za = side(apart, to_xor(apart, "row", 2), z & 1)
     zb = side(za, to_xor(za, "row", 6), z >> 1)
-    column_features = side(zb, to_xor(zb, "row", 1), core).reshape(8 * block, width)
-
-    kept, given = products(core, turned, row_features, column_features)
-    mate = to_xor(given, "row", 1)
-
-    def part(d):
-        return lax.dynamic_index_in_dim(kept, z ^ d, 0, keepdims=False) + lax.dynamic_index_in_dim(
-            mate, z ^ d, 0, keepdims=False
-        )
-
-    arrived = [to_xor(part(d), "row", 2 * d) for d in (2, 1, 3)]
-    total = (part(0) + arrived[0]) + (arrived[1] + arrived[2])
-    product, share = total[:block], total[block:]
+    quad = zb.reshape(4 * block, width)
+
+    kept, given = products(core, turned, row_features, quad, to_xor(quad, "row", 1))
+    terms = pieces(z, kept, to_xor(given, "row", 1))
+    product, share = totals([terms[0]] + [to_xor(terms[d], "row", 2 * d) for d in (1, 2, 3)], block)
 
     for bits in (1, 3, 4, 12):
         share = share + to_xor(share, "col", bits)
@@ -176,14 +256,18 @@
     matrix = side(shares, to_xor(shares, "row", 1), core).reshape(width, width)
 
     cols = side(product, to_xor(product, "row", 2), z & 1)
-    cols = side(cols, to_xor(cols, "row", 6), z >> 1)
-    product_cols = side(cols, to_xor(cols, "row", 1), core).reshape(8 * block, width)
+    cols = side(cols, to_xor(cols, "row", 6), z >> 1).reshape(4 * block, width)
+    other_cols = to_xor(cols, "row", 1)
 
     product_rows = to_plane(to_place(product, product_place))
 
     inverse = inverse_of(matrix, noise.reshape(1, width))
-    gain = dot(product_cols, inverse, ((1,), (0,)), HIGH)
-    return (turned - dot(gain, product_rows, ((1,), (1,)), HIGH)).T
+    gain = gain_of(core, cols, other_cols, inverse)
+    product_rows = hold(product_rows)
+    change = lax.dot_general(
+        gain, product_rows, (((1,), (1,)), ((), ())), precision=HIGH, preferred_element_type=jnp.float32
+    )
+    return (turned - change).T
 
 
 def solution(mesh):

time: 118 us -> 110 us (0.932)
  other arithmetic: 4.11 us -> 0.28 us
  starting transfers between devices: 40.9 us -> 37.6 us
  Pallas kernels: 13.6 us -> 16.5 us
  waiting for transfers between devices: 50.4 us -> 48.6 us
  matrix products: 4.58 us -> 2.98 us
    ppermute x17, starting transfers between devices: 30.1 us -> 20.6 us  [to_xor(): return lax.ppermute(value, axis, [(i, i ^ bits) for i in range(size)])]
    all_to_all x2, starting transfers between devices: 9.51 us -> 15.7 us  [to_plane(): lax.all_to_all(sent, 'col', 0, 0, tiled=True).reshape(-1, block.shape[-1])]
    all_to_all x2, waiting for transfers between devices: 20.9 us -> 14.9 us  [to_plane(): lax.all_to_all(sent, 'col', 0, 0, tiled=True).reshape(-1, block.shape[-1])]
    ppermute x17, waiting for transfers between devices: 29.5 us -> 33.6 us  [to_xor(): return lax.ppermute(value, axis, [(i, i ^ bits) for i in range(size)])]
    pallas_call x0 -> x5, Pallas kernels: none -> 3.49 us  [the longest x2 2.99 us: hold(): pl.pallas_call(hold_kernel, out_shape=pltpu.VMEM(cov.shape, jnp.float32),...]
    add x2 -> x0, other arithmetic: 2.67 us -> none  [the longest x1 1.72 us: part(): lax.dynamic_index_in_dim(kept, z ^ d, 0, keepdims=False)]
    dot_general x2 -> x1, matrix products: 4.58 us -> 2.98 us  [step(): lax.dot_general(gain, product_rows, (((1,), (1,)), ((), ())), precision=H...]
  transfers between devices with their start and end apart: 21 -> 21, of which waited for: 14 -> 13; matrix products, arithmetic and copies ran while one was open for 3% -> 2% of each run, Pallas kernels for 8% -> 11%
where the time goes in v1:
time: 110 us; the launch traced here: 109 us
  waiting for transfers between devices  48.6 us (44%)
  starting transfers between devices  37.6 us (34%)
  Pallas kernels  16.5 us (15%)
  local copies, waits for them, and re-layouts  3.08 us (3%)
  matrix products  2.98 us (3%)
    ppermute x17, waiting for transfers between devices, to_xor(): return lax.ppermute(value, axis, [(i, i ^ bits) for i in range(size)])  33.6 us
    ppermute x17, starting transfers between devices, to_xor(): return lax.ppermute(value, axis, [(i, i ^ bits) for i in range(size)])  20.6 us
    all_to_all x2, starting transfers between devices, to_plane(): lax.all_to_all(sent, 'col', 0, 0, tiled=True).reshape(-1, block.shape[-1])  15.7 us
    all_to_all x2, waiting for transfers between devices, to_plane(): lax.all_to_all(sent, 'col', 0, 0, tiled=True).reshape(-1, block.shape[-1])  14.9 us
    pallas_call x1, Pallas kernels, inverse_of(): pl.pallas_call(invert_kernel, out_shape=jax.ShapeDtypeStruct((n, n), jnp....  9.77 us
    pallas_call x1, Pallas kernels, products(): pl.pallas_call(products_kernel, out_shape=(exchange, exchange), in_specs=...  3.19 us
    pallas_call x2, Pallas kernels, hold(): pl.pallas_call(hold_kernel, out_shape=pltpu.VMEM(cov.shape, jnp.float32),...  2.99 us
    dot_general x1, matrix products, step(): lax.dot_general(gain, product_rows, (((1,), (1,)), ((), ())), precision=H...  2.98 us
  transfers between devices with their start and end apart: 21, of which 13 were waited for; matrix products, arithmetic and copies ran while one was open for 2% of the time, Pallas kernels for 11%

profile of v1, /device:TPU:0, one launch (start us, length us, event | category | flops | bytes accessed | tf_op | source)
XLA Modules:
  0.0 109.2 jit_solution(15716996166125223840)
XLA Ops:
  0.0 0.9 copy-done
  0.9 0.7 collective-permute-start
  1.6 9.3 %collective-permute-start.1 = (f32[72,256]{1,0:T(8,128)S(1)}, f32[72,256]{1,0:T(8,128)S(1)}, u32[]{:S(2)}, u32[]{:S(2)}) collective-permute-start(f32[72,256]{1,0:T(8,128)S(1)} %collective-permute-done), channel_id=1, source_target_pairs={{0,32},{16,48},{32,0},{48,16},{64,96},{80,112},{96,64},{112,80},{1... | collective-permute-start | bytes 221192 | tf_op jit(solution)/shard_map/ppermute | solution.py:15
  10.8 1.1 broadcast_in_dim.14
  11.9 11.3 %all-to-all-start = ((f32[16,72,256]{2,1,0:T(8,128)}), f32[16,72,256]{2,1,0:T(8,128)}, u32[]{:S(2)}, u32[]{:S(2)}) async-start(f32[16,72,256]{2,1,0:T(8,128)} %broadcast_in_dim.14), calls=%async_computation | async-start | bytes 2359296 | tf_op jit(solution)/shard_map/all_to_all | solution.py:41
  23.7 6.1 %collective-permute-done.2 = f32[2,72,256]{2,1,0:T(8,128)S(1)} collective-permute-done((f32[2,72,256]{2,1,0:T(8,128)S(1)}, f32[2,72,256]{2,1,0:T(8,128)S(1)}, u32[]{:S(2)}, u32[]{:S(2)}) %collective-permute-start.2) | collective-permute-done | bytes 147488 | tf_op jit(solution)/shard_map/ppermute | solution.py:15
  29.9 1.7 %shard_map.37.cov_ref = f32[576,1152]{1,0:T(8,128)S(1)} custom-call(f32[576,1152]{1,0:T(8,128)} %bitcast.53), custom_call_target="tpu_custom_call" | custom-call | tf_op jit(solution)/shard_map/pallas_call | solution.py:165
  31.6 8.5 %all-to-all-done = f32[16,72,256]{2,1,0:T(8,128)} async-done(((f32[16,72,256]{2,1,0:T(8,128)}), f32[16,72,256]{2,1,0:T(8,128)}, u32[]{:S(2)}, u32[]{:S(2)}) %all-to-all-start) | async-done | bytes 1179680 | tf_op jit(solution)/shard_map/all_to_all | solution.py:41
  40.1 3.2 %shard_map.38 = (f32[4,104,256]{2,1,0:T(8,128)S(1)}, f32[4,104,256]{2,1,0:T(8,128)S(1)}) custom-call(s32[1]{0:T(128)} %bitcast.1.core_ref, f32[576,1152]{1,0:T(8,128)S(1)} %shard_map.37.cov_ref, f32[1152,256]{1,0:T(8,128)} %bitcast.4.rows_ref, f32[288,256]{1,0:T(8,128)S(1)} %bitcast.50, f32[288,256]{1,0:T(8,128)S(1)} %collective-permute-done.3.other_ref), custom_call_target="tpu_custom_call" | custom-call | flops 1245708288 | bytes 2654208 | tf_op jit(solution)/shard_map/pallas_call | solution.py:83
  43.4 1.8 %collective-permute-done.4.mate_ref = f32[4,104,256]{2,1,0:T(8,128)S(1)} collective-permute-done((f32[4,104,256]{2,1,0:T(8,128)S(1)}, f32[4,104,256]{2,1,0:T(8,128)S(1)}, u32[]{:S(2)}, u32[]{:S(2)}) %collective-permute-start.4) | collective-permute-done | bytes 426016 | tf_op jit(solution)/shard_map/ppermute | solution.py:15
  45.2 1.0 collective-permute-start.5
  46.2 2.2 %collective-permute-start.6 = (f32[104,256]{1,0:T(8,128)S(1)}, f32[104,256]{1,0:T(8,128)S(1)}, u32[]{:S(2)}, u32[]{:S(2)}) collective-permute-start(f32[104,256]{1,0:T(8,128)S(1)} %get-tuple-element.17), channel_id=1, source_target_pairs={{0,64},{16,80},{32,96},{48,112},{64,0},{80,16},{96,32},{112,48},{1... | collective-permute-start | bytes 319496 | tf_op jit(solution)/shard_map/ppermute | solution.py:15
  48.4 1.6 %collective-permute-start.7 = (f32[104,256]{1,0:T(8,128)S(1)}, f32[104,256]{1,0:T(8,128)S(1)}, u32[]{:S(2)}, u32[]{:S(2)}) collective-permute-start(f32[104,256]{1,0:T(8,128)S(1)} %get-tuple-element.18), channel_id=1, source_target_pairs={{0,96},{16,112},{32,64},{48,80},{64,32},{80,48},{96,0},{112,16},{1... | collective-permute-start | bytes 319496 | tf_op jit(solution)/shard_map/ppermute | solution.py:15
  50.0 1.1 %collective-permute-done.5.b_ref = f32[104,256]{1,0:T(8,128)S(1)} collective-permute-done((f32[104,256]{1,0:T(8,128)S(1)}, f32[104,256]{1,0:T(8,128)S(1)}, u32[]{:S(2)}, u32[]{:S(2)}) %collective-permute-start.5) | collective-permute-done | bytes 106528 | tf_op jit(solution)/shard_map/ppermute | solution.py:15
  51.2 2.6 %collective-permute-done.6.c_ref = f32[104,256]{1,0:T(8,128)S(1)} collective-permute-done((f32[104,256]{1,0:T(8,128)S(1)}, f32[104,256]{1,0:T(8,128)S(1)}, u32[]{:S(2)}, u32[]{:S(2)}) %collective-permute-start.6) | collective-permute-done | bytes 106528 | tf_op jit(solution)/shard_map/ppermute | solution.py:15
  53.8 2.0 %collective-permute-done.7.d_ref = f32[104,256]{1,0:T(8,128)S(1)} collective-permute-done((f32[104,256]{1,0:T(8,128)S(1)}, f32[104,256]{1,0:T(8,128)S(1)}, u32[]{:S(2)}, u32[]{:S(2)}) %collective-permute-start.7) | collective-permute-done | bytes 106528 | tf_op jit(solution)/shard_map/ppermute | solution.py:15
  56.4 3.3 %collective-permute-done.11 = f32[32,256]{1,0:T(8,128)S(1)} collective-permute-done((f32[32,256]{1,0:T(8,128)S(1)}, f32[32,256]{1,0:T(8,128)S(1)}, u32[]{:S(2)}, u32[]{:S(2)}) %collective-permute-start.11) | collective-permute-done | bytes 32800 | tf_op jit(solution)/shard_map/ppermute | solution.py:15
  60.2 4.7 %collective-permute-done.12 = f32[32,256]{1,0:T(8,128)S(1)} collective-permute-done((f32[32,256]{1,0:T(8,128)S(1)}, f32[32,256]{1,0:T(8,128)S(1)}, u32[]{:S(2)}, u32[]{:S(2)}) %collective-permute-start.12) | collective-permute-done | bytes 32800 | tf_op jit(solution)/shard_map/ppermute | solution.py:15
  64.9 3.9 %collective-permute-done.13 = f32[32,256]{1,0:T(8,128)S(1)} collective-permute-done((f32[32,256]{1,0:T(8,128)S(1)}, f32[32,256]{1,0:T(8,128)S(1)}, u32[]{:S(2)}, u32[]{:S(2)}) %collective-permute-start.13) | collective-permute-done | bytes 32800 | tf_op jit(solution)/shard_map/ppermute | solution.py:15
  68.8 0.9 collective-permute-start.14
  69.7 0.7 collective-permute-start.18
  70.4 3.5 %collective-permute-done.14 = f32[32,256]{1,0:T(8,128)S(1)} collective-permute-done((f32[32,256]{1,0:T(8,128)S(1)}, f32[32,256]{1,0:T(8,128)S(1)}, u32[]{:S(2)}, u32[]{:S(2)}) %collective-permute-start.14) | collective-permute-done | bytes 32800 | tf_op jit(solution)/shard_map/ppermute | solution.py:15
  74.0 3.9 %collective-permute-done.15 = f32[32,256]{1,0:T(8,128)S(1)} collective-permute-done((f32[32,256]{1,0:T(8,128)S(1)}, f32[32,256]{1,0:T(8,128)S(1)}, u32[]{:S(2)}, u32[]{:S(2)}) %collective-permute-start.15) | collective-permute-done | bytes 32800 | tf_op jit(solution)/shard_map/ppermute | solution.py:15
  77.9 1.7 %collective-permute-start.16 = (f32[2,32,256]{2,1,0:T(8,128)S(1)}, f32[2,32,256]{2,1,0:T(8,128)S(1)}, u32[]{:S(2)}, u32[]{:S(2)}) collective-permute-start(f32[2,32,256]{2,1,0:T(8,128)S(1)} %pad_maximum_fusion.6), channel_id=1, source_target_pairs={{0,96},{16,112},{32,64},{48,80},{64,32},{80,48},{96,0},{112,16},{1... | collective-permute-start | bytes 196616 | tf_op jit(solution)/shard_map/ppermute | solution.py:15
  79.6 1.7 %collective-permute-start.9 = (f32[2,72,256]{2,1,0:T(8,128)S(1)}, f32[2,72,256]{2,1,0:T(8,128)S(1)}, u32[]{:S(2)}, u32[]{:S(2)}) collective-permute-start(f32[2,72,256]{2,1,0:T(8,128)S(1)} %pad_maximum_fusion.4), channel_id=1, source_target_pairs={{0,96},{16,112},{32,64},{48,80},{64,32},{80,48},{96,0},{112,16},{1... | collective-permute-start | bytes 442376 | tf_op jit(solution)/shard_map/ppermute | solution.py:15
  81.3 1.1 broadcast_in_dim.15
  82.4 4.4 %all-to-all-start.1 = ((f32[16,72,256]{2,1,0:T(8,128)}), f32[16,72,256]{2,1,0:T(8,128)}, u32[]{:S(2)}, u32[]{:S(2)}) async-start(f32[16,72,256]{2,1,0:T(8,128)} %broadcast_in_dim.15), calls=%async_computation.1 | async-start | bytes 2359296 | tf_op jit(solution)/shard_map/all_to_all | solution.py:41
  87.6 0.7 collective-permute-done.17
  88.3 9.8 %shard_map.41.inv_ref = f32[256,256]{1,0:T(8,128)S(1)} custom-call(f32[256,256]{1,0:T(8,128)S(1)} %bitcast.51, f32[1,256]{1,0:T(1,128)S(1)} %bitcast.52), custom_call_target="tpu_custom_call" | custom-call | flops 1342177280 | bytes 786432 | tf_op jit(solution)/shard_map/pallas_call | solution.py:226
  98.6 6.4 %all-to-all-done.1 = f32[16,72,256]{2,1,0:T(8,128)} async-done(((f32[16,72,256]{2,1,0:T(8,128)}), f32[16,72,256]{2,1,0:T(8,128)}, u32[]{:S(2)}, u32[]{:S(2)}) %all-to-all-start.1) | async-done | bytes 1179680 | tf_op jit(solution)/shard_map/all_to_all | solution.py:41
  105.0 1.3 %shard_map.43 = f32[1152,256]{1,0:T(8,128)S(1)} custom-call(f32[1152,256]{1,0:T(8,128)} %bitcast.23.far_ref), custom_call_target="tpu_custom_call" | custom-call | tf_op jit(solution)/shard_map/pallas_call | solution.py:165
  106.3 3.0 %fusion = f32[1152,576]{0,1:T(8,128)} fusion(f32[576,1152]{1,0:T(8,128)S(1)} %shard_map.37.cov_ref, f32[576,256]{1,0:T(8,128)S(1)} %shard_map.42, f32[1152,256]{1,0:T(8,128)S(1)} %shard_map.43), kind=kOutput, calls=%fused_computation.1 | convolution fusion | flops 1019879424 | bytes 7077888 | tf_op jit(solution)/shard_map/dot_general | solution.py:267
  (43 shorter events, 3.0 us)
Async XLA Ops:
  0.0 0.9 copy-start
  0.9 0.7 collective-permute-start
  1.6 21.7 %collective-permute-start.1 = (f32[72,256]{1,0:T(8,128)S(1)}, f32[72,256]{1,0:T(8,128)S(1)}, u32[]{:S(2)}, u32[]{:S(2)}) collective-permute-start(f32[72,256]{1,0:T(8,128)S(1)} %collective-permute-done), channel_id=1, source_target_pairs={{0,32},{16,48},{32,0},{48,16},{64,96},{80,112},{96,64},{112,80},{1... | collective-permute-start | bytes 221192 | tf_op jit(solution)/shard_map/ppermute | solution.py:15
  11.9 28.2 %all-to-all-start = ((f32[16,72,256]{2,1,0:T(8,128)}), f32[16,72,256]{2,1,0:T(8,128)}, u32[]{:S(2)}, u32[]{:S(2)}) async-start(f32[16,72,256]{2,1,0:T(8,128)} %broadcast_in_dim.14), calls=%async_computation | async-start | bytes 2359296 | tf_op jit(solution)/shard_map/all_to_all | solution.py:41
  23.3 6.4 %collective-permute-start.2 = (f32[2,72,256]{2,1,0:T(8,128)S(1)}, f32[2,72,256]{2,1,0:T(8,128)S(1)}, u32[]{:S(2)}, u32[]{:S(2)}) collective-permute-start(f32[2,72,256]{2,1,0:T(8,128)S(1)} %pad_maximum_fusion.3), channel_id=1, source_target_pairs={{0,96},{16,112},{32,64},{48,80},{64,32},{80,48},{96,0},{112,16},{1... | collective-permute-start | bytes 442376 | tf_op jit(solution)/shard_map/ppermute | solution.py:15
  29.8 1.8 %collective-permute-start.3 = (f32[288,256]{1,0:T(8,128)S(1)}, f32[288,256]{1,0:T(8,128)S(1)}, u32[]{:S(2)}, u32[]{:S(2)}) collective-permute-start(f32[288,256]{1,0:T(8,128)S(1)} %bitcast.49), channel_id=1, source_target_pairs={{0,16},{16,0},{32,48},{48,32},{64,80},{80,64},{96,112},{112,96},{1... | collective-permute-start | bytes 884744 | tf_op jit(solution)/shard_map/ppermute | solution.py:15
  43.3 1.8 %collective-permute-start.4 = (f32[4,104,256]{2,1,0:T(8,128)S(1)}, f32[4,104,256]{2,1,0:T(8,128)S(1)}, u32[]{:S(2)}, u32[]{:S(2)}) collective-permute-start(f32[4,104,256]{2,1,0:T(8,128)S(1)} %get-tuple-element.14), channel_id=1, source_target_pairs={{0,16},{16,0},{32,48},{48,32},{64,80},{80,64},{96,112},{112,96},{1... | collective-permute-start | bytes 1277960 | tf_op jit(solution)/shard_map/ppermute | solution.py:15
  45.2 5.9 %collective-permute-start.5 = (f32[104,256]{1,0:T(8,128)S(1)}, f32[104,256]{1,0:T(8,128)S(1)}, u32[]{:S(2)}, u32[]{:S(2)}) collective-permute-start(f32[104,256]{1,0:T(8,128)S(1)} %get-tuple-element.16), channel_id=1, source_target_pairs={{0,32},{16,48},{32,0},{48,16},{64,96},{80,112},{96,64},{112,80},{1... | collective-permute-start | bytes 319496 | tf_op jit(solution)/shard_map/ppermute | solution.py:15
  46.2 7.5 %collective-permute-start.6 = (f32[104,256]{1,0:T(8,128)S(1)}, f32[104,256]{1,0:T(8,128)S(1)}, u32[]{:S(2)}, u32[]{:S(2)}) collective-permute-start(f32[104,256]{1,0:T(8,128)S(1)} %get-tuple-element.17), channel_id=1, source_target_pairs={{0,64},{16,80},{32,96},{48,112},{64,0},{80,16},{96,32},{112,48},{1... | collective-permute-start | bytes 319496 | tf_op jit(solution)/shard_map/ppermute | solution.py:15
  48.4 7.3 %collective-permute-start.7 = (f32[104,256]{1,0:T(8,128)S(1)}, f32[104,256]{1,0:T(8,128)S(1)}, u32[]{:S(2)}, u32[]{:S(2)}) collective-permute-start(f32[104,256]{1,0:T(8,128)S(1)} %get-tuple-element.18), channel_id=1, source_target_pairs={{0,96},{16,112},{32,64},{48,80},{64,32},{80,48},{96,0},{112,16},{1... | collective-permute-start | bytes 319496 | tf_op jit(solution)/shard_map/ppermute | solution.py:15
  55.8 4.0 %collective-permute-start.11 = (f32[32,256]{1,0:T(8,128)S(1)}, f32[32,256]{1,0:T(8,128)S(1)}, u32[]{:S(2)}, u32[]{:S(2)}) collective-permute-start(f32[32,256]{1,0:T(8,128)S(1)} %get-tuple-element.20), channel_id=1, source_target_pairs={{0,1},{1,0},{2,3},{3,2},{4,5},{5,4},{6,7},{7,6},{8,9},{9,8},{10,11... | collective-permute-start | bytes 98312 | tf_op jit(solution)/shard_map/ppermute | solution.py:15
  59.8 5.1 %collective-permute-start.12 = (f32[32,256]{1,0:T(8,128)S(1)}, f32[32,256]{1,0:T(8,128)S(1)}, u32[]{:S(2)}, u32[]{:S(2)}) collective-permute-start(f32[32,256]{1,0:T(8,128)S(1)} %add.12), channel_id=1, source_target_pairs={{0,3},{1,2},{2,1},{3,0},{4,7},{5,6},{6,5},{7,4},{8,11},{9,10},{10,... | collective-permute-start | bytes 98312 | tf_op jit(solution)/shard_map/ppermute | solution.py:15
  60.1 13.8 %collective-permute-start.8 = (f32[72,256]{1,0:T(8,128)S(1)}, f32[72,256]{1,0:T(8,128)S(1)}, u32[]{:S(2)}, u32[]{:S(2)}) collective-permute-start(f32[72,256]{1,0:T(8,128)S(1)} %get-tuple-element.19), channel_id=1, source_target_pairs={{0,32},{16,48},{32,0},{48,16},{64,96},{80,112},{96,64},{112,80},{1... | collective-permute-start | bytes 221192 | tf_op jit(solution)/shard_map/ppermute | solution.py:15
  64.9 3.9 %collective-permute-start.13 = (f32[32,256]{1,0:T(8,128)S(1)}, f32[32,256]{1,0:T(8,128)S(1)}, u32[]{:S(2)}, u32[]{:S(2)}) collective-permute-start(f32[32,256]{1,0:T(8,128)S(1)} %add.13), channel_id=1, source_target_pairs={{0,4},{1,5},{2,6},{3,7},{4,0},{5,1},{6,2},{7,3},{8,12},{9,13},{10,... | collective-permute-start | bytes 98312 | tf_op jit(solution)/shard_map/ppermute | solution.py:15
  68.8 5.1 %collective-permute-start.14 = (f32[32,256]{1,0:T(8,128)S(1)}, f32[32,256]{1,0:T(8,128)S(1)}, u32[]{:S(2)}, u32[]{:S(2)}) collective-permute-start(f32[32,256]{1,0:T(8,128)S(1)} %add.14), channel_id=1, source_target_pairs={{0,12},{1,13},{2,14},{3,15},{4,8},{5,9},{6,10},{7,11},{8,4},{9,5},... | collective-permute-start | bytes 98312 | tf_op jit(solution)/shard_map/ppermute | solution.py:15
  69.7 11.6 %collective-permute-start.18 = (f32[72,256]{1,0:T(8,128)S(1)}, f32[72,256]{1,0:T(8,128)S(1)}, u32[]{:S(2)}, u32[]{:S(2)}) collective-permute-start(f32[72,256]{1,0:T(8,128)S(1)} %get-tuple-element.19), channel_id=1, source_target_pairs={{0,0},{1,8},{2,16},{3,24},{4,32},{5,40},{6,48},{7,56},{8,64},{9,72... | collective-permute-start | bytes 221192 | tf_op jit(solution)/shard_map/ppermute | solution.py:19
  73.9 3.9 %collective-permute-start.15 = (f32[32,256]{1,0:T(8,128)S(1)}, f32[32,256]{1,0:T(8,128)S(1)}, u32[]{:S(2)}, u32[]{:S(2)}) collective-permute-start(f32[32,256]{1,0:T(8,128)S(1)} %add.15), channel_id=1, source_target_pairs={{0,32},{16,48},{32,0},{48,16},{64,96},{80,112},{96,64},{112,80},{1... | collective-permute-start | bytes 98312 | tf_op jit(solution)/shard_map/ppermute | solution.py:15
  77.9 8.9 %collective-permute-start.16 = (f32[2,32,256]{2,1,0:T(8,128)S(1)}, f32[2,32,256]{2,1,0:T(8,128)S(1)}, u32[]{:S(2)}, u32[]{:S(2)}) collective-permute-start(f32[2,32,256]{2,1,0:T(8,128)S(1)} %pad_maximum_fusion.6), channel_id=1, source_target_pairs={{0,96},{16,112},{32,64},{48,80},{64,32},{80,48},{96,0},{112,16},{1... | collective-permute-start | bytes 196616 | tf_op jit(solution)/shard_map/ppermute | solution.py:15
  79.6 7.3 %collective-permute-start.9 = (f32[2,72,256]{2,1,0:T(8,128)S(1)}, f32[2,72,256]{2,1,0:T(8,128)S(1)}, u32[]{:S(2)}, u32[]{:S(2)}) collective-permute-start(f32[2,72,256]{2,1,0:T(8,128)S(1)} %pad_maximum_fusion.4), channel_id=1, source_target_pairs={{0,96},{16,112},{32,64},{48,80},{64,32},{80,48},{96,0},{112,16},{1... | collective-permute-start | bytes 442376 | tf_op jit(solution)/shard_map/ppermute | solution.py:15
  82.4 22.6 %all-to-all-start.1 = ((f32[16,72,256]{2,1,0:T(8,128)}), f32[16,72,256]{2,1,0:T(8,128)}, u32[]{:S(2)}, u32[]{:S(2)}) async-start(f32[16,72,256]{2,1,0:T(8,128)} %broadcast_in_dim.15), calls=%async_computation.1 | async-start | bytes 2359296 | tf_op jit(solution)/shard_map/all_to_all | solution.py:41
  86.8 1.5 %copy-start.1 = (f32[2,128]{1,0:T(2,128)S(1)}, f32[2,128]{1,0:T(2,128)}, u32[]{:S(2)}) copy-start(f32[2,128]{1,0:T(2,128)} %param.5) | copy-start | bytes 3076
  86.8 1.4 %collective-permute-start.17 = (f32[2,2,32,256]{3,2,1,0:T(8,128)S(1)}, f32[2,2,32,256]{3,2,1,0:T(8,128)S(1)}, u32[]{:S(2)}, u32[]{:S(2)}) collective-permute-start(f32[2,2,32,256]{3,2,1,0:T(8,128)S(1)} %pad_maximum_fusion.5), channel_id=1, source_target_pairs={{0,16},{16,0},{32,48},{48,32},{64,80},{80,64},{96,112},{112,96},{1... | collective-permute-start | bytes 393224 | tf_op jit(solution)/shard_map/ppermute | solution.py:15
  87.0 11.1 %collective-permute-start.10 = (f32[288,256]{1,0:T(8,128)S(1)}, f32[288,256]{1,0:T(8,128)S(1)}, u32[]{:S(2)}, u32[]{:S(2)}) collective-permute-start(f32[288,256]{1,0:T(8,128)S(1)} %bitcast.47), channel_id=1, source_target_pairs={{0,16},{16,0},{32,48},{48,32},{64,80},{80,64},{96,112},{112,96},{1... | collective-permute-start | bytes 884744 | tf_op jit(solution)/shard_map/ppermute | solution.py:15

commit v2 on v1

--- a/solution.py
+++ b/solution.py
@@ -131,17 +131,41 @@
     )(*terms)
 
 
+def pack_kernel(z_ref, cols_ref, far_cols_ref, *refs):
+    out_ref = refs[-1]
+    z = z_ref[0]
+    block = cols_ref.shape[1]
+    for half, cols in ((0, cols_ref), (1, far_cols_ref)):
+        for j in range(2):
+            out_ref[2 * ((z >> 1) ^ half) + j, :block, :] = cols[j]
+    for d, share in enumerate(refs[:-1]):
+        out_ref[z ^ d, block:, :] = share[...]
+
+
+def pack(z, cols, far_cols, shares):
+    depth = cols.shape[1] + shares[0].shape[0]
+    return pl.pallas_call(
+        pack_kernel,
+        out_shape=pltpu.VMEM((4, depth, cols.shape[2]), jnp.float32),
+        in_specs=[SCALAR] + [VMEM] * 6,
+        out_specs=VMEM,
+        compiler_params=pltpu.CompilerParams(vmem_limit_bytes=4 << 20),
+    )(z.reshape(1), cols, far_cols, *shares)
+
+
 def gain_kernel(core_ref, own_ref, other_ref, inv_ref, out_ref):
-    core, half = core_ref[0], own_ref.shape[0]
+    block = out_ref.shape[0] // 8
     inverse = halves(inv_ref[...])
-    for ref, at in ((own_ref, core), (other_ref, 1 - core)):
-        out_ref[pl.ds(pl.multiple_of(at * half, 8), half), :] = near_full(halves(ref[...]), inverse, ((1,), (0,)))
-
-
-def gain_of(core, own, other, inverse):
+    for ref, at in ((own_ref, core_ref[0]), (other_ref, 1 - core_ref[0])):
+        for j in range(4):
+            out_ref[pl.ds(pl.multiple_of((4 * at + j) * block, 8), block), :] = ref[j, :block, :]
+    out_ref[...] = near_full(halves(out_ref[...]), inverse, ((1,), (0,)))
+
+
+def gain_of(core, own, other, inverse, block):
     return pl.pallas_call(
         gain_kernel,
-        out_shape=pltpu.VMEM((2 * own.shape[0], own.shape[1]), jnp.float32),
+        out_shape=pltpu.VMEM((8 * block, own.shape[2]), jnp.float32),
         in_specs=[SCALAR, VMEM, VMEM, VMEM],
         out_specs=VMEM,
         compiler_params=pltpu.CompilerParams(vmem_limit_bytes=6 << 20),
@@ -172,8 +196,12 @@
     )(cov)
 
 
-def invert_kernel(m_ref, noise_ref, out_ref):
+def invert_kernel(core_ref, own_ref, other_ref, noise_ref, out_ref, m_ref):
     n = m_ref.shape[0]
+    share = n // 8
+    for ref, at in ((own_ref, core_ref[0]), (other_ref, 1 - core_ref[0])):
+        for j in range(4):
+            m_ref[pl.ds(pl.multiple_of((4 * at + j) * share, 8), share), :] = ref[j, ref.shape[1] - share :, :]
     eye = lax.broadcasted_iota(jnp.int32, (n, n), 0) == lax.broadcasted_iota(jnp.int32, (n, n), 1)
     one = jnp.where(eye, 1.0, 0.0).astype(jnp.float32)
     system = m_ref[...] + jnp.where(eye, noise_ref[...], 0.0)
@@ -202,33 +230,39 @@
 
     rest = one - full(scaled, guess)
     size = norm(rest)
-    slow = size >= 0.5
 
     def go_on(state):
         return jnp.logical_and(state[2] >= 1e-3, state[3] < 60)
 
-    def refine(state):
-        y, r, _, count = state
-        y = y + full(y, r)
-        r = one - full(scaled, y)
-        return y, r, norm(r), count + 1
-
-    guess, rest = lax.cond(
-        slow, lambda: (start, one - full(scaled, start)), lambda: (guess, rest)
+    def finished(multiply, y, r, bound):
+        def refine(state):
+            y, r, _, count = state
+            y = y + multiply(y, r)
+            r = one - full(scaled, y)
+            return y, r, norm(r), count + 1
+
+        y, r, _, _ = lax.while_loop(go_on, refine, (y, r, bound, jnp.int32(0)))
+        return y + multiply(y, r)
+
+    guess = lax.cond(
+        size < 0.5,
+        lambda: finished(fast, guess, rest, size),
+        lambda: finished(full, start, one - full(scaled, start), jnp.float32(1.0)),
     )
-    guess, rest, _, _ = lax.while_loop(go_on, refine, (guess, rest, size, jnp.int32(0)))
-    guess = guess + full(guess, rest)
     out_ref[...] = guess * down * across
 
 
-def inverse_of(m, noise):
-    n = m.shape[0]
+def inverse_of(core, own, other, noise):
+    n = noise.shape[1]
     return pl.pallas_call(
         invert_kernel,
-        out_shape=jax.ShapeDtypeStruct((n, n), jnp.float32),
+        out_shape=pltpu.VMEM((n, n), jnp.float32),
+        in_specs=[SCALAR, VMEM, VMEM, VMEM],
+        out_specs=VMEM,
+        scratch_shapes=[pltpu.VMEM((n, n), jnp.float32)],
         cost_estimate=pl.CostEstimate(flops=2 * n**3 * 40, bytes_accessed=4 * n * n * 3, transcendentals=n),
-        compiler_params=pltpu.CompilerParams(vmem_limit_bytes=4 << 20),
-    )(m, noise)
+        compiler_params=pltpu.CompilerParams(vmem_limit_bytes=12 << 20),
+    )(core.reshape(1), own, other, noise)
 
 
 def step(covariance, features, noise):
@@ -249,20 +283,18 @@
     terms = pieces(z, kept, to_xor(given, "row", 1))
     product, share = totals([terms[0]] + [to_xor(terms[d], "row", 2 * d) for d in (1, 2, 3)], block)
 
-    for bits in (1, 3, 4, 12):
-        share = share + to_xor(share, "col", bits)
-    shares = side(share, to_xor(share, "row", 2), z & 1)
-    shares = side(shares, to_xor(shares, "row", 6), z >> 1)
-    matrix = side(shares, to_xor(shares, "row", 1), core).reshape(width, width)
-
+    for unit in (1, 4):
+        a, b, c = (to_xor(share, "col", d * unit) for d in (2, 1, 3))
+        share = (share + a) + (b + c)
+    shares = [share] + [to_xor(share, "row", 2 * d) for d in (1, 2, 3)]
     cols = side(product, to_xor(product, "row", 2), z & 1)
-    cols = side(cols, to_xor(cols, "row", 6), z >> 1).reshape(4 * block, width)
-    other_cols = to_xor(cols, "row", 1)
+    packed = pack(z, cols, to_xor(cols, "row", 6), shares)
+    mate = to_xor(packed, "row", 1)
 
     product_rows = to_plane(to_place(product, product_place))
 
-    inverse = inverse_of(matrix, noise.reshape(1, width))
-    gain = gain_of(core, cols, other_cols, inverse)
+    inverse = inverse_of(core, packed, mate, noise.reshape(1, width))
+    gain = gain_of(core, packed, mate, inverse, block)
     product_rows = hold(product_rows)
     change = lax.dot_general(
         gain, product_rows, (((1,), (1,)), ((), ())), precision=HIGH, preferred_element_type=jnp.float32

time: 110 us -> 104 us (0.945)
  the two profiles are of different devices: /device:TPU:0 before, /device:TPU:1 now
where the time goes in v2:
time: 104 us; the launch traced here: 103 us
  starting transfers between devices  56.7 us (55%)
  waiting for transfers between devices  23.8 us (23%)
  Pallas kernels  16.6 us (16%)
  local copies, waits for them, and re-layouts  3.08 us (3%)
  matrix products  2.98 us (3%)
    ppermute x19, starting transfers between devices, to_xor(): return lax.ppermute(value, axis, [(i, i ^ bits) for i in range(size)])  32.9 us
    ppermute x19, waiting for transfers between devices, to_xor(): return lax.ppermute(value, axis, [(i, i ^ bits) for i in range(size)])  15.4 us
    all_to_all x2, starting transfers between devices, to_plane(): lax.all_to_all(sent, 'col', 0, 0, tiled=True).reshape(-1, block.shape[-1])  14.7 us
    pallas_call x1, Pallas kernels, inverse_of(): pl.pallas_call(invert_kernel, out_shape=pltpu.VMEM((n, n), jnp.float32),...  9.88 us
    ppermute x2, starting transfers between devices, to_place(): lax.ppermute(value, ('row', 'col'), [(i, owner(i)) for i in range(128)])  9.07 us
    all_to_all x2, waiting for transfers between devices, to_plane(): lax.all_to_all(sent, 'col', 0, 0, tiled=True).reshape(-1, block.shape[-1])  4.76 us
    ppermute x2, waiting for transfers between devices, to_place(): lax.ppermute(value, ('row', 'col'), [(i, owner(i)) for i in range(128)])  3.65 us
    pallas_call x1, Pallas kernels, products(): pl.pallas_call(products_kernel, out_shape=(exchange, exchange), in_specs=...  3.19 us
  transfers between devices with their start and end apart: 23, of which 10 were waited for; matrix products, arithmetic and copies ran while one was open for 2% of the time, Pallas kernels for 12%

profile of v2, /device:TPU:1, one launch (start us, length us, event | category | flops | bytes accessed | tf_op | source)
XLA Modules:
  0.0 103.4 jit_solution(13076935193904028918)
XLA Ops:
  0.0 0.9 copy-done
  0.9 6.2 %collective-permute-start = (f32[72,256]{1,0:T(8,128)S(1)}, f32[72,256]{1,0:T(8,128)S(1)}, u32[]{:S(2)}, u32[]{:S(2)}) collective-permute-start(f32[72,256]{1,0:T(8,128)S(1)} %copy_bitcast_fusion), channel_id=1, source_target_pairs={{0,0},{1,32},{2,64},{3,96},{4,16},{5,48},{6,80},{7,112},{8,1},{9,3... | collective-permute-start | bytes 221192 | tf_op jit(solution)/shard_map/ppermute | solution.py:19
  7.1 3.6 %collective-permute-done = f32[72,256]{1,0:T(8,128)S(1)} collective-permute-done((f32[72,256]{1,0:T(8,128)S(1)}, f32[72,256]{1,0:T(8,128)S(1)}, u32[]{:S(2)}, u32[]{:S(2)}) %collective-permute-start) | collective-permute-done | bytes 73760 | tf_op jit(solution)/shard_map/ppermute | solution.py:19
  11.0 1.1 %broadcast_in_dim.14 = f32[16,72,256]{2,1,0:T(8,128)} broadcast(f32[72,256]{1,0:T(8,128)S(1)} %copy_bitcast_fusion), dimensions={1,2} | broadcast | bytes 1253376 | tf_op jit(solution)/shard_map/broadcast_in_dim | solution.py:40
  12.1 9.8 %all-to-all-start = ((f32[16,72,256]{2,1,0:T(8,128)}), f32[16,72,256]{2,1,0:T(8,128)}, u32[]{:S(2)}, u32[]{:S(2)}) async-start(f32[16,72,256]{2,1,0:T(8,128)} %broadcast_in_dim.14), calls=%async_computation | async-start | bytes 2359296 | tf_op jit(solution)/shard_map/all_to_all | solution.py:41
  22.0 1.0 collective-permute-start.2
  23.0 4.3 %collective-permute-done.2 = f32[2,72,256]{2,1,0:T(8,128)S(1)} collective-permute-done((f32[2,72,256]{2,1,0:T(8,128)S(1)}, f32[2,72,256]{2,1,0:T(8,128)S(1)}, u32[]{:S(2)}, u32[]{:S(2)}) %collective-permute-start.2) | collective-permute-done | bytes 147488 | tf_op jit(solution)/shard_map/ppermute | solution.py:15
  27.3 3.9 %collective-permute-start.3 = (f32[288,256]{1,0:T(8,128)S(1)}, f32[288,256]{1,0:T(8,128)S(1)}, u32[]{:S(2)}, u32[]{:S(2)}) collective-permute-start(f32[288,256]{1,0:T(8,128)S(1)} %bitcast.29), channel_id=1, source_target_pairs={{0,16},{16,0},{32,48},{48,32},{64,80},{80,64},{96,112},{112,96},{1... | collective-permute-start | bytes 884744 | tf_op jit(solution)/shard_map/ppermute | solution.py:15
  31.3 1.7 %shard_map.37.cov_ref = f32[576,1152]{1,0:T(8,128)S(1)} custom-call(f32[576,1152]{1,0:T(8,128)} %bitcast.32), custom_call_target="tpu_custom_call" | custom-call | tf_op jit(solution)/shard_map/pallas_call | solution.py:189
  33.0 4.8 %all-to-all-done = f32[16,72,256]{2,1,0:T(8,128)} async-done(((f32[16,72,256]{2,1,0:T(8,128)}), f32[16,72,256]{2,1,0:T(8,128)}, u32[]{:S(2)}, u32[]{:S(2)}) %all-to-all-start) | async-done | bytes 1179680 | tf_op jit(solution)/shard_map/all_to_all | solution.py:41
  37.8 3.2 %shard_map.38 = (f32[4,104,256]{2,1,0:T(8,128)S(1)}, f32[4,104,256]{2,1,0:T(8,128)S(1)}) custom-call(s32[1]{0:T(128)} %bitcast.1.core_ref, f32[576,1152]{1,0:T(8,128)S(1)} %shard_map.37.cov_ref, f32[1152,256]{1,0:T(8,128)} %bitcast.4.rows_ref, f32[288,256]{1,0:T(8,128)S(1)} %bitcast.30, f32[288,256]{1,0:T(8,128)S(1)} %collective-permute-done.3.other_ref), custom_call_target="tpu_custom_call" | custom-call | flops 1245708288 | bytes 2654208 | tf_op jit(solution)/shard_map/pallas_call | solution.py:83
  41.0 3.8 %collective-permute-start.4 = (f32[4,104,256]{2,1,0:T(8,128)S(1)}, f32[4,104,256]{2,1,0:T(8,128)S(1)}, u32[]{:S(2)}, u32[]{:S(2)}) collective-permute-start(f32[4,104,256]{2,1,0:T(8,128)S(1)} %get-tuple-element.14), channel_id=1, source_target_pairs={{0,16},{16,0},{32,48},{48,32},{64,80},{80,64},{96,112},{112,96},{1... | collective-permute-start | bytes 1277960 | tf_op jit(solution)/shard_map/ppermute | solution.py:15
  44.8 1.4 %collective-permute-done.4.mate_ref = f32[4,104,256]{2,1,0:T(8,128)S(1)} collective-permute-done((f32[4,104,256]{2,1,0:T(8,128)S(1)}, f32[4,104,256]{2,1,0:T(8,128)S(1)}, u32[]{:S(2)}, u32[]{:S(2)}) %collective-permute-start.4) | collective-permute-done | bytes 426016 | tf_op jit(solution)/shard_map/ppermute | solution.py:15
  47.0 1.9 %collective-permute-start.6 = (f32[104,256]{1,0:T(8,128)S(1)}, f32[104,256]{1,0:T(8,128)S(1)}, u32[]{:S(2)}, u32[]{:S(2)}) collective-permute-start(f32[104,256]{1,0:T(8,128)S(1)} %get-tuple-element.17), channel_id=1, source_target_pairs={{0,64},{16,80},{32,96},{48,112},{64,0},{80,16},{96,32},{112,48},{1... | collective-permute-start | bytes 319496 | tf_op jit(solution)/shard_map/ppermute | solution.py:15
  48.8 1.3 %collective-permute-start.7 = (f32[104,256]{1,0:T(8,128)S(1)}, f32[104,256]{1,0:T(8,128)S(1)}, u32[]{:S(2)}, u32[]{:S(2)}) collective-permute-start(f32[104,256]{1,0:T(8,128)S(1)} %get-tuple-element.18), channel_id=1, source_target_pairs={{0,96},{16,112},{32,64},{48,80},{64,32},{80,48},{96,0},{112,16},{1... | collective-permute-start | bytes 319496 | tf_op jit(solution)/shard_map/ppermute | solution.py:15
  50.5 3.3 %collective-permute-done.6.c_ref = f32[104,256]{1,0:T(8,128)S(1)} collective-permute-done((f32[104,256]{1,0:T(8,128)S(1)}, f32[104,256]{1,0:T(8,128)S(1)}, u32[]{:S(2)}, u32[]{:S(2)}) %collective-permute-start.6) | collective-permute-done | bytes 106528 | tf_op jit(solution)/shard_map/ppermute | solution.py:15
  53.8 2.6 %collective-permute-done.7.d_ref = f32[104,256]{1,0:T(8,128)S(1)} collective-permute-done((f32[104,256]{1,0:T(8,128)S(1)}, f32[104,256]{1,0:T(8,128)S(1)}, u32[]{:S(2)}, u32[]{:S(2)}) %collective-permute-start.7) | collective-permute-done | bytes 106528 | tf_op jit(solution)/shard_map/ppermute | solution.py:15
  56.9 3.5 %collective-permute-start.10 = (f32[32,256]{1,0:T(8,128)S(1)}, f32[32,256]{1,0:T(8,128)S(1)}, u32[]{:S(2)}, u32[]{:S(2)}) collective-permute-start(f32[32,256]{1,0:T(8,128)S(1)} %get-tuple-element.20), channel_id=1, source_target_pairs={{0,2},{1,3},{2,0},{3,1},{4,6},{5,7},{6,4},{7,5},{8,10},{9,11},{10,... | collective-permute-start | bytes 98312 | tf_op jit(solution)/shard_map/ppermute | solution.py:15
  60.4 2.9 %collective-permute-start.20 = (f32[72,256]{1,0:T(8,128)S(1)}, f32[72,256]{1,0:T(8,128)S(1)}, u32[]{:S(2)}, u32[]{:S(2)}) collective-permute-start(f32[72,256]{1,0:T(8,128)S(1)} %get-tuple-element.19), channel_id=1, source_target_pairs={{0,0},{1,8},{2,16},{3,24},{4,32},{5,40},{6,48},{7,56},{8,64},{9,72... | collective-permute-start | bytes 221192 | tf_op jit(solution)/shard_map/ppermute | solution.py:19
  63.4 3.9 %collective-permute-start.15 = (f32[32,256]{1,0:T(8,128)S(1)}, f32[32,256]{1,0:T(8,128)S(1)}, u32[]{:S(2)}, u32[]{:S(2)}) collective-permute-start(f32[32,256]{1,0:T(8,128)S(1)} %add_add_fusion.1), channel_id=1, source_target_pairs={{0,12},{1,13},{2,14},{3,15},{4,8},{5,9},{6,10},{7,11},{8,4},{9,5},... | collective-permute-start | bytes 98312 | tf_op jit(solution)/shard_map/ppermute | solution.py:15
  67.3 1.3 %collective-permute-start.13 = (f32[32,256]{1,0:T(8,128)S(1)}, f32[32,256]{1,0:T(8,128)S(1)}, u32[]{:S(2)}, u32[]{:S(2)}) collective-permute-start(f32[32,256]{1,0:T(8,128)S(1)} %add_add_fusion.1), channel_id=1, source_target_pairs={{0,8},{1,9},{2,10},{3,11},{4,12},{5,13},{6,14},{7,15},{8,0},{9,1},... | collective-permute-start | bytes 98312 | tf_op jit(solution)/shard_map/ppermute | solution.py:15
  68.6 1.1 %broadcast_in_dim.15 = f32[16,72,256]{2,1,0:T(8,128)} broadcast(f32[72,256]{1,0:T(8,128)S(1)} %collective-permute-done.20), dimensions={1,2} | broadcast | bytes 1253376 | tf_op jit(solution)/shard_map/broadcast_in_dim | solution.py:40
  69.7 5.0 %all-to-all-start.1 = ((f32[16,72,256]{2,1,0:T(8,128)}), f32[16,72,256]{2,1,0:T(8,128)}, u32[]{:S(2)}, u32[]{:S(2)}) async-start(f32[16,72,256]{2,1,0:T(8,128)} %broadcast_in_dim.15), calls=%async_computation.1 | async-start | bytes 2359296 | tf_op jit(solution)/shard_map/all_to_all | solution.py:41
  74.7 4.3 %collective-permute-start.9 = (f32[2,72,256]{2,1,0:T(8,128)S(1)}, f32[2,72,256]{2,1,0:T(8,128)S(1)}, u32[]{:S(2)}, u32[]{:S(2)}) collective-permute-start(f32[2,72,256]{2,1,0:T(8,128)S(1)} %pad_maximum_fusion.2.cols_ref), channel_id=1, source_target_pairs={{0,96},{16,112},{32,64},{48,80},{64,32},{80,48},{96,0},{112,16},{1... | collective-permute-start | bytes 442376 | tf_op jit(solution)/shard_map/ppermute | solution.py:15
  79.1 0.8 collective-permute-start.17
  80.0 2.4 %collective-permute-start.16 = (f32[32,256]{1,0:T(8,128)S(1)}, f32[32,256]{1,0:T(8,128)S(1)}, u32[]{:S(2)}, u32[]{:S(2)}) collective-permute-start(f32[32,256]{1,0:T(8,128)S(1)} %add_add_fusion.refs_0_), channel_id=1, source_target_pairs={{0,32},{16,48},{32,0},{48,16},{64,96},{80,112},{96,64},{112,80},{1... | collective-permute-start | bytes 98312 | tf_op jit(solution)/shard_map/ppermute | solution.py:15
  82.4 1.8 %collective-permute-done.18.refs_3_ = f32[32,256]{1,0:T(8,128)S(1)} collective-permute-done((f32[32,256]{1,0:T(8,128)S(1)}, f32[32,256]{1,0:T(8,128)S(1)}, u32[]{:S(2)}, u32[]{:S(2)}) %collective-permute-start.18) | collective-permute-done | bytes 32800 | tf_op jit(solution)/shard_map/ppermute | solution.py:15
  84.5 3.0 %collective-permute-start.19 = (f32[4,104,256]{2,1,0:T(8,128)S(1)}, f32[4,104,256]{2,1,0:T(8,128)S(1)}, u32[]{:S(2)}, u32[]{:S(2)}) collective-permute-start(f32[4,104,256]{2,1,0:T(8,128)S(1)} %shard_map.41.own_ref), channel_id=1, source_target_pairs={{0,16},{16,0},{32,48},{48,32},{64,80},{80,64},{96,112},{112,96},{1... | collective-permute-start | bytes 1277960 | tf_op jit(solution)/shard_map/ppermute | solution.py:15
  87.4 1.4 %collective-permute-done.19.other_ref = f32[4,104,256]{2,1,0:T(8,128)S(1)} collective-permute-done((f32[4,104,256]{2,1,0:T(8,128)S(1)}, f32[4,104,256]{2,1,0:T(8,128)S(1)}, u32[]{:S(2)}, u32[]{:S(2)}) %collective-permute-start.19) | collective-permute-done | bytes 426016 | tf_op jit(solution)/shard_map/ppermute | solution.py:15
  88.8 9.9 %shard_map.42.inv_ref = f32[256,256]{1,0:T(8,128)S(1)} custom-call(s32[1]{0:T(128)} %bitcast.1.core_ref, f32[4,104,256]{2,1,0:T(8,128)S(1)} %shard_map.41.own_ref, f32[4,104,256]{2,1,0:T(8,128)S(1)} %collective-permute-done.19.other_ref, f32[1,256]{1,0:T(1,128)S(1)} %bitcast.31), custom_call_target="tpu_custom_call" | custom-call | flops 1342177280 | bytes 786432 | tf_op jit(solution)/shard_map/pallas_call | solution.py:257
  99.2 1.3 %shard_map.44 = f32[1152,256]{1,0:T(8,128)S(1)} custom-call(f32[1152,256]{1,0:T(8,128)} %bitcast.13.far_ref), custom_call_target="tpu_custom_call" | custom-call | tf_op jit(solution)/shard_map/pallas_call | solution.py:189
  100.5 3.0 %fusion = f32[1152,576]{0,1:T(8,128)} fusion(f32[576,1152]{1,0:T(8,128)S(1)} %shard_map.37.cov_ref, f32[576,256]{1,0:T(8,128)S(1)} %shard_map.43, f32[1152,256]{1,0:T(8,128)S(1)} %shard_map.44), kind=kOutput, calls=%fused_computation.1 | convolution fusion | flops 1019879424 | bytes 7077888 | tf_op jit(solution)/shard_map/dot_general | solution.py:299
  (38 shorter events, 3.0 us)
Async XLA Ops:
  0.0 0.9 copy-start
  0.9 9.8 %collective-permute-start = (f32[72,256]{1,0:T(8,128)S(1)}, f32[72,256]{1,0:T(8,128)S(1)}, u32[]{:S(2)}, u32[]{:S(2)}) collective-permute-start(f32[72,256]{1,0:T(8,128)S(1)} %copy_bitcast_fusion), channel_id=1, source_target_pairs={{0,0},{1,32},{2,64},{3,96},{4,16},{5,48},{6,80},{7,112},{8,1},{9,3... | collective-permute-start | bytes 221192 | tf_op jit(solution)/shard_map/ppermute | solution.py:19
  10.7 11.2 %collective-permute-start.1 = (f32[72,256]{1,0:T(8,128)S(1)}, f32[72,256]{1,0:T(8,128)S(1)}, u32[]{:S(2)}, u32[]{:S(2)}) collective-permute-start(f32[72,256]{1,0:T(8,128)S(1)} %collective-permute-done), channel_id=1, source_target_pairs={{0,32},{16,48},{32,0},{48,16},{64,96},{80,112},{96,64},{112,80},{1... | collective-permute-start | bytes 221192 | tf_op jit(solution)/shard_map/ppermute | solution.py:15
  12.1 25.6 %all-to-all-start = ((f32[16,72,256]{2,1,0:T(8,128)}), f32[16,72,256]{2,1,0:T(8,128)}, u32[]{:S(2)}, u32[]{:S(2)}) async-start(f32[16,72,256]{2,1,0:T(8,128)} %broadcast_in_dim.14), calls=%async_computation | async-start | bytes 2359296 | tf_op jit(solution)/shard_map/all_to_all | solution.py:41
  22.0 5.3 %collective-permute-start.2 = (f32[2,72,256]{2,1,0:T(8,128)S(1)}, f32[2,72,256]{2,1,0:T(8,128)S(1)}, u32[]{:S(2)}, u32[]{:S(2)}) collective-permute-start(f32[2,72,256]{2,1,0:T(8,128)S(1)} %pad_maximum_fusion.1), channel_id=1, source_target_pairs={{0,96},{16,112},{32,64},{48,80},{64,32},{80,48},{96,0},{112,16},{1... | collective-permute-start | bytes 442376 | tf_op jit(solution)/shard_map/ppermute | solution.py:15
  27.3 5.7 %collective-permute-start.3 = (f32[288,256]{1,0:T(8,128)S(1)}, f32[288,256]{1,0:T(8,128)S(1)}, u32[]{:S(2)}, u32[]{:S(2)}) collective-permute-start(f32[288,256]{1,0:T(8,128)S(1)} %bitcast.29), channel_id=1, source_target_pairs={{0,16},{16,0},{32,48},{48,32},{64,80},{80,64},{96,112},{112,96},{1... | collective-permute-start | bytes 884744 | tf_op jit(solution)/shard_map/ppermute | solution.py:15
  41.0 5.2 %collective-permute-start.4 = (f32[4,104,256]{2,1,0:T(8,128)S(1)}, f32[4,104,256]{2,1,0:T(8,128)S(1)}, u32[]{:S(2)}, u32[]{:S(2)}) collective-permute-start(f32[4,104,256]{2,1,0:T(8,128)S(1)} %get-tuple-element.14), channel_id=1, source_target_pairs={{0,16},{16,0},{32,48},{48,32},{64,80},{80,64},{96,112},{112,96},{1... | collective-permute-start | bytes 1277960 | tf_op jit(solution)/shard_map/ppermute | solution.py:15
  46.2 4.2 %collective-permute-start.5 = (f32[104,256]{1,0:T(8,128)S(1)}, f32[104,256]{1,0:T(8,128)S(1)}, u32[]{:S(2)}, u32[]{:S(2)}) collective-permute-start(f32[104,256]{1,0:T(8,128)S(1)} %get-tuple-element.16), channel_id=1, source_target_pairs={{0,32},{16,48},{32,0},{48,16},{64,96},{80,112},{96,64},{112,80},{1... | collective-permute-start | bytes 319496 | tf_op jit(solution)/shard_map/ppermute | solution.py:15
  47.0 6.8 %collective-permute-start.6 = (f32[104,256]{1,0:T(8,128)S(1)}, f32[104,256]{1,0:T(8,128)S(1)}, u32[]{:S(2)}, u32[]{:S(2)}) collective-permute-start(f32[104,256]{1,0:T(8,128)S(1)} %get-tuple-element.17), channel_id=1, source_target_pairs={{0,64},{16,80},{32,96},{48,112},{64,0},{80,16},{96,32},{112,48},{1... | collective-permute-start | bytes 319496 | tf_op jit(solution)/shard_map/ppermute | solution.py:15
  48.8 7.6 %collective-permute-start.7 = (f32[104,256]{1,0:T(8,128)S(1)}, f32[104,256]{1,0:T(8,128)S(1)}, u32[]{:S(2)}, u32[]{:S(2)}) collective-permute-start(f32[104,256]{1,0:T(8,128)S(1)} %get-tuple-element.18), channel_id=1, source_target_pairs={{0,96},{16,112},{32,64},{48,80},{64,32},{80,48},{96,0},{112,16},{1... | collective-permute-start | bytes 319496 | tf_op jit(solution)/shard_map/ppermute | solution.py:15
  56.4 7.0 %collective-permute-start.12 = (f32[32,256]{1,0:T(8,128)S(1)}, f32[32,256]{1,0:T(8,128)S(1)}, u32[]{:S(2)}, u32[]{:S(2)}) collective-permute-start(f32[32,256]{1,0:T(8,128)S(1)} %get-tuple-element.20), channel_id=1, source_target_pairs={{0,3},{1,2},{2,1},{3,0},{4,7},{5,6},{6,5},{7,4},{8,11},{9,10},{10,... | collective-permute-start | bytes 98312 | tf_op jit(solution)/shard_map/ppermute | solution.py:15
  56.7 6.7 %collective-permute-start.11 = (f32[32,256]{1,0:T(8,128)S(1)}, f32[32,256]{1,0:T(8,128)S(1)}, u32[]{:S(2)}, u32[]{:S(2)}) collective-permute-start(f32[32,256]{1,0:T(8,128)S(1)} %get-tuple-element.20), channel_id=1, source_target_pairs={{0,1},{1,0},{2,3},{3,2},{4,5},{5,4},{6,7},{7,6},{8,9},{9,8},{10,11... | collective-permute-start | bytes 98312 | tf_op jit(solution)/shard_map/ppermute | solution.py:15
  56.9 6.5 %collective-permute-start.10 = (f32[32,256]{1,0:T(8,128)S(1)}, f32[32,256]{1,0:T(8,128)S(1)}, u32[]{:S(2)}, u32[]{:S(2)}) collective-permute-start(f32[32,256]{1,0:T(8,128)S(1)} %get-tuple-element.20), channel_id=1, source_target_pairs={{0,2},{1,3},{2,0},{3,1},{4,6},{5,7},{6,4},{7,5},{8,10},{9,11},{10,... | collective-permute-start | bytes 98312 | tf_op jit(solution)/shard_map/ppermute | solution.py:15
  60.4 8.2 %collective-permute-start.20 = (f32[72,256]{1,0:T(8,128)S(1)}, f32[72,256]{1,0:T(8,128)S(1)}, u32[]{:S(2)}, u32[]{:S(2)}) collective-permute-start(f32[72,256]{1,0:T(8,128)S(1)} %get-tuple-element.19), channel_id=1, source_target_pairs={{0,0},{1,8},{2,16},{3,24},{4,32},{5,40},{6,48},{7,56},{8,64},{9,72... | collective-permute-start | bytes 221192 | tf_op jit(solution)/shard_map/ppermute | solution.py:19
  63.2 11.4 %collective-permute-start.8 = (f32[72,256]{1,0:T(8,128)S(1)}, f32[72,256]{1,0:T(8,128)S(1)}, u32[]{:S(2)}, u32[]{:S(2)}) collective-permute-start(f32[72,256]{1,0:T(8,128)S(1)} %get-tuple-element.19), channel_id=1, source_target_pairs={{0,32},{16,48},{32,0},{48,16},{64,96},{80,112},{96,64},{112,80},{1... | collective-permute-start | bytes 221192 | tf_op jit(solution)/shard_map/ppermute | solution.py:15
  63.4 15.6 %collective-permute-start.15 = (f32[32,256]{1,0:T(8,128)S(1)}, f32[32,256]{1,0:T(8,128)S(1)}, u32[]{:S(2)}, u32[]{:S(2)}) collective-permute-start(f32[32,256]{1,0:T(8,128)S(1)} %add_add_fusion.1), channel_id=1, source_target_pairs={{0,12},{1,13},{2,14},{3,15},{4,8},{5,9},{6,10},{7,11},{8,4},{9,5},... | collective-permute-start | bytes 98312 | tf_op jit(solution)/shard_map/ppermute | solution.py:15
  67.3 11.7 %collective-permute-start.14 = (f32[32,256]{1,0:T(8,128)S(1)}, f32[32,256]{1,0:T(8,128)S(1)}, u32[]{:S(2)}, u32[]{:S(2)}) collective-permute-start(f32[32,256]{1,0:T(8,128)S(1)} %add_add_fusion.1), channel_id=1, source_target_pairs={{0,4},{1,5},{2,6},{3,7},{4,0},{5,1},{6,2},{7,3},{8,12},{9,13},{10,... | collective-permute-start | bytes 98312 | tf_op jit(solution)/shard_map/ppermute | solution.py:15
  67.3 11.7 %collective-permute-start.13 = (f32[32,256]{1,0:T(8,128)S(1)}, f32[32,256]{1,0:T(8,128)S(1)}, u32[]{:S(2)}, u32[]{:S(2)}) collective-permute-start(f32[32,256]{1,0:T(8,128)S(1)} %add_add_fusion.1), channel_id=1, source_target_pairs={{0,8},{1,9},{2,10},{3,11},{4,12},{5,13},{6,14},{7,15},{8,0},{9,1},... | collective-permute-start | bytes 98312 | tf_op jit(solution)/shard_map/ppermute | solution.py:15
  69.7 29.5 %all-to-all-start.1 = ((f32[16,72,256]{2,1,0:T(8,128)}), f32[16,72,256]{2,1,0:T(8,128)}, u32[]{:S(2)}, u32[]{:S(2)}) async-start(f32[16,72,256]{2,1,0:T(8,128)} %broadcast_in_dim.15), calls=%async_computation.1 | async-start | bytes 2359296 | tf_op jit(solution)/shard_map/all_to_all | solution.py:41
  74.6 14.2 %copy-start.1 = (f32[2,128]{1,0:T(2,128)S(1)}, f32[2,128]{1,0:T(2,128)}, u32[]{:S(2)}) copy-start(f32[2,128]{1,0:T(2,128)} %param.5) | copy-start | bytes 3076
  74.7 9.7 %collective-permute-start.9 = (f32[2,72,256]{2,1,0:T(8,128)S(1)}, f32[2,72,256]{2,1,0:T(8,128)S(1)}, u32[]{:S(2)}, u32[]{:S(2)}) collective-permute-start(f32[2,72,256]{2,1,0:T(8,128)S(1)} %pad_maximum_fusion.2.cols_ref), channel_id=1, source_target_pairs={{0,96},{16,112},{32,64},{48,80},{64,32},{80,48},{96,0},{112,16},{1... | collective-permute-start | bytes 442376 | tf_op jit(solution)/shard_map/ppermute | solution.py:15
  79.0 5.2 %collective-permute-start.18 = (f32[32,256]{1,0:T(8,128)S(1)}, f32[32,256]{1,0:T(8,128)S(1)}, u32[]{:S(2)}, u32[]{:S(2)}) collective-permute-start(f32[32,256]{1,0:T(8,128)S(1)} %add_add_fusion.refs_0_), channel_id=1, source_target_pairs={{0,96},{16,112},{32,64},{48,80},{64,32},{80,48},{96,0},{112,16},{1... | collective-permute-start | bytes 98312 | tf_op jit(solution)/shard_map/ppermute | solution.py:15
  79.1 5.0 %collective-permute-start.17 = (f32[32,256]{1,0:T(8,128)S(1)}, f32[32,256]{1,0:T(8,128)S(1)}, u32[]{:S(2)}, u32[]{:S(2)}) collective-permute-start(f32[32,256]{1,0:T(8,128)S(1)} %add_add_fusion.refs_0_), channel_id=1, source_target_pairs={{0,64},{16,80},{32,96},{48,112},{64,0},{80,16},{96,32},{112,48},{1... | collective-permute-start | bytes 98312 | tf_op jit(solution)/shard_map/ppermute | solution.py:15
  80.0 4.4 %collective-permute-start.16 = (f32[32,256]{1,0:T(8,128)S(1)}, f32[32,256]{1,0:T(8,128)S(1)}, u32[]{:S(2)}, u32[]{:S(2)}) collective-permute-start(f32[32,256]{1,0:T(8,128)S(1)} %add_add_fusion.refs_0_), channel_id=1, source_target_pairs={{0,32},{16,48},{32,0},{48,16},{64,96},{80,112},{96,64},{112,80},{1... | collective-permute-start | bytes 98312 | tf_op jit(solution)/shard_map/ppermute | solution.py:15
  84.5 4.4 %collective-permute-start.19 = (f32[4,104,256]{2,1,0:T(8,128)S(1)}, f32[4,104,256]{2,1,0:T(8,128)S(1)}, u32[]{:S(2)}, u32[]{:S(2)}) collective-permute-start(f32[4,104,256]{2,1,0:T(8,128)S(1)} %shard_map.41.own_ref), channel_id=1, source_target_pairs={{0,16},{16,0},{32,48},{48,32},{64,80},{80,64},{96,112},{112,96},{1... | collective-permute-start | bytes 1277960 | tf_op jit(solution)/shard_map/ppermute | solution.py:15

commit v3 on v2

--- a/solution.py
+++ b/solution.py
@@ -7,7 +7,6 @@
 
 
 HIGHEST = lax.Precision.HIGHEST
-HIGH = lax.Precision.HIGH
 
 
 def to_xor(value, axis, bits):
@@ -74,6 +73,7 @@
 
 SCALAR = pl.BlockSpec(memory_space=pltpu.SMEM)
 VMEM = pl.BlockSpec(memory_space=pltpu.VMEM)
+FAR = pl.BlockSpec(memory_space=pltpu.HBM)
 
 
 def products(core, cov, rows, own, other):
@@ -94,7 +94,7 @@
             flops=6 * n * width * (rows.shape[0] + width), bytes_accessed=4 * cov.size, transcendentals=0
         ),
         compiler_params=pltpu.CompilerParams(vmem_limit_bytes=20 << 20),
-    )(core.reshape(1), cov, rows, own, other)
+    )(core.reshape(1), cov, pltpu.with_memory_space_constraint(rows, pltpu.VMEM), own, other)
 
 
 def pieces_kernel(z_ref, kept_ref, mate_ref, *out_refs):
@@ -131,26 +131,87 @@
     )(*terms)
 
 
-def pack_kernel(z_ref, cols_ref, far_cols_ref, *refs):
-    out_ref = refs[-1]
-    z = z_ref[0]
-    block = cols_ref.shape[1]
-    for half, cols in ((0, cols_ref), (1, far_cols_ref)):
-        for j in range(2):
-            out_ref[2 * ((z >> 1) ^ half) + j, :block, :] = cols[j]
-    for d, share in enumerate(refs[:-1]):
-        out_ref[z ^ d, block:, :] = share[...]
-
-
-def pack(z, cols, far_cols, shares):
-    depth = cols.shape[1] + shares[0].shape[0]
+def join_kernel(product_ref, a_ref, b_ref, c_ref, d_ref, out_ref):
+    block = product_ref.shape[0]
+    out_ref[:block, :] = product_ref[...]
+    out_ref[block:, :] = (a_ref[...] + b_ref[...]) + (c_ref[...] + d_ref[...])
+
+
+def join(product, shares):
+    depth = product.shape[0] + shares[0].shape[0]
+    return pl.pallas_call(
+        join_kernel,
+        out_shape=pltpu.VMEM((depth, product.shape[1]), jnp.float32),
+        in_specs=[VMEM] * 5,
+        out_specs=VMEM,
+        compiler_params=pltpu.CompilerParams(vmem_limit_bytes=2 << 20),
+    )(product, *shares)
+
+
+def pack_kernel(z_ref, *refs):
+    for d, piece in enumerate(refs[:-1]):
+        refs[-1][z_ref[0] ^ d] = piece[...]
+
+
+def pack(z, parts):
     return pl.pallas_call(
         pack_kernel,
-        out_shape=pltpu.VMEM((4, depth, cols.shape[2]), jnp.float32),
-        in_specs=[SCALAR] + [VMEM] * 6,
+        out_shape=pltpu.VMEM((4, *parts[0].shape), jnp.float32),
+        in_specs=[SCALAR] + [VMEM] * 4,
         out_specs=VMEM,
         compiler_params=pltpu.CompilerParams(vmem_limit_bytes=4 << 20),
-    )(z.reshape(1), cols, far_cols, *shares)
+    )(z.reshape(1), *parts)
+
+
+def columns_kernel(far_ref, own_ref, sems):
+    batch = far_ref.shape[2]
+    copies = [
+        pltpu.make_async_copy(far_ref.at[i], own_ref.at[:, pl.ds(i * batch, batch)], sems.at[i])
+        for i in range(far_ref.shape[0])
+    ]
+    for copy in copies:
+        copy.start()
+    for copy in copies:
+        copy.wait()
+
+
+def columns_of(features):
+    steps, block, batch = features.shape
+    return pl.pallas_call(
+        columns_kernel,
+        out_shape=pltpu.VMEM((block, steps * batch), jnp.float32),
+        in_specs=[FAR],
+        out_specs=VMEM,
+        scratch_shapes=[pltpu.SemaphoreType.DMA((steps,))],
+        compiler_params=pltpu.CompilerParams(vmem_limit_bytes=2 << 20),
+    )(pltpu.with_memory_space_constraint(features, pltpu.HBM))
+
+
+def update_kernel(cov_ref, rows_ref, gain_ref, far_ref, out_ref, sems):
+    cut = cov_ref.shape[0] // 2
+    rows = halves(rows_ref[...])
+    copies = []
+    for i in range(2):
+        at = pl.ds(i * cut, cut)
+        out_ref[at, :] = cov_ref[at, :] - near_full(halves(gain_ref[at, :]), rows, ((1,), (1,)))
+        copies.append(pltpu.make_async_copy(out_ref.at[at], far_ref.at[at], sems.at[i]))
+        copies[-1].start()
+    for copy in copies:
+        copy.wait()
+
+
+def update(cov, rows, gain):
+    return pl.pallas_call(
+        update_kernel,
+        out_shape=pltpu.HBM(cov.shape, jnp.float32),
+        in_specs=[VMEM, VMEM, VMEM],
+        out_specs=FAR,
+        scratch_shapes=[pltpu.VMEM(cov.shape, jnp.float32), pltpu.SemaphoreType.DMA((2,))],
+        cost_estimate=pl.CostEstimate(
+            flops=6 * cov.size * rows.shape[1], bytes_accessed=4 * cov.size, transcendentals=0
+        ),
+        compiler_params=pltpu.CompilerParams(vmem_limit_bytes=20 << 20),
+    )(cov, pltpu.with_memory_space_constraint(rows, pltpu.VMEM), gain)
 
 
 def gain_kernel(core_ref, own_ref, other_ref, inv_ref, out_ref):
@@ -270,7 +331,7 @@
     z, core = r >> 1, r & 1
     steps, block, batch = features.shape
     width = steps * batch
-    own = jnp.moveaxis(features, 0, 1).reshape(block, width)
+    own = columns_of(features)
     turned = hold(covariance.T)
 
     row_features = to_plane(own)
@@ -284,22 +345,17 @@
     product, share = totals([terms[0]] + [to_xor(terms[d], "row", 2 * d) for d in (1, 2, 3)], block)
 
     for unit in (1, 4):
-        a, b, c = (to_xor(share, "col", d * unit) for d in (2, 1, 3))
-        share = (share + a) + (b + c)
-    shares = [share] + [to_xor(share, "row", 2 * d) for d in (1, 2, 3)]
-    cols = side(product, to_xor(product, "row", 2), z & 1)
-    packed = pack(z, cols, to_xor(cols, "row", 6), shares)
+        sums = [share] + [to_xor(share, "col", d * unit) for d in (1, 2, 3)]
+        share = (sums[0] + sums[1]) + (sums[2] + sums[3])
+    joined = join(product, sums)
+    packed = pack(z, [joined] + [to_xor(joined, "row", 2 * d) for d in (1, 2, 3)])
     mate = to_xor(packed, "row", 1)
 
     product_rows = to_plane(to_place(product, product_place))
 
     inverse = inverse_of(core, packed, mate, noise.reshape(1, width))
     gain = gain_of(core, packed, mate, inverse, block)
-    product_rows = hold(product_rows)
-    change = lax.dot_general(
-        gain, product_rows, (((1,), (1,)), ((), ())), precision=HIGH, preferred_element_type=jnp.float32
-    )
-    return (turned - change).T
+    return update(turned, product_rows, gain).T
 
 
 def solution(mesh):

time: 104 us -> 123 us (1.18)
  waiting for transfers between devices: 23.8 us -> 41.3 us
  Pallas kernels: 16.6 us -> 20 us
  matrix products: 2.98 us -> 0 us
  starting transfers between devices: 56.7 us -> 58.4 us
    ppermute x19 -> x17, waiting for transfers between devices: 15.4 us -> 27.3 us  [to_xor(): return lax.ppermute(value, axis, [(i, i ^ bits) for i in range(size)])]
    ppermute x2, waiting for transfers between devices: 3.65 us -> 9.24 us  [to_place(): lax.ppermute(value, ('row', 'col'), [(i, owner(i)) for i in range(128)])]
    pallas_call x1 -> x4, Pallas kernels: 0.03 us -> 4.76 us  [the longest x1 3.91 us: update(): pl.pallas_call(update_kernel, out_shape=pltpu.HBM(cov.shape, jnp.float32)...]
    dot_general x1 -> x0, matrix products: 2.98 us -> none  [step(): lax.dot_general(gain, product_rows, (((1,), (1,)), ((), ())), precision=H...]
    ppermute x19 -> x17, starting transfers between devices: 32.9 us -> 34.1 us  [to_xor(): return lax.ppermute(value, axis, [(i, i ^ bits) for i in range(size)])]
    pallas_call x2 -> x1, Pallas kernels: 2.99 us -> 1.72 us  [hold(): pl.pallas_call(hold_kernel, out_shape=pltpu.VMEM(cov.shape, jnp.float32),...]
    all_to_all x2, starting transfers between devices: 14.7 us -> 16 us  [to_plane(): lax.all_to_all(sent, 'col', 0, 0, tiled=True).reshape(-1, block.shape[-1])]
  transfers between devices with their start and end apart: 23 -> 21, of which waited for: 10 -> 16; matrix products, arithmetic and copies ran while one was open for 2% -> 1% of each run, Pallas kernels for 12% -> 10%
where the time goes in v3:
time: 123 us; the launch traced here: 122 us
  starting transfers between devices  58.4 us (47%)
  waiting for transfers between devices  41.3 us (34%)
  Pallas kernels  20 us (16%)
  local copies, waits for them, and re-layouts  2.18 us (2%)
    ppermute x17, starting transfers between devices, to_xor(): return lax.ppermute(value, axis, [(i, i ^ bits) for i in range(size)])  34.1 us
    ppermute x17, waiting for transfers between devices, to_xor(): return lax.ppermute(value, axis, [(i, i ^ bits) for i in range(size)])  27.3 us
    all_to_all x2, starting transfers between devices, to_plane(): lax.all_to_all(sent, 'col', 0, 0, tiled=True).reshape(-1, block.shape[-1])  16 us
    pallas_call x1, Pallas kernels, inverse_of(): pl.pallas_call(invert_kernel, out_shape=pltpu.VMEM((n, n), jnp.float32),...  9.89 us
    ppermute x2, waiting for transfers between devices, to_place(): lax.ppermute(value, ('row', 'col'), [(i, owner(i)) for i in range(128)])  9.24 us
    ppermute x2, starting transfers between devices, to_place(): lax.ppermute(value, ('row', 'col'), [(i, owner(i)) for i in range(128)])  8.26 us
    all_to_all x2, waiting for transfers between devices, to_plane(): lax.all_to_all(sent, 'col', 0, 0, tiled=True).reshape(-1, block.shape[-1])  4.76 us
    pallas_call x1, Pallas kernels, update(): pl.pallas_call(update_kernel, out_shape=pltpu.HBM(cov.shape, jnp.float32)...  3.91 us
  transfers between devices with their start and end apart: 21, of which 16 were waited for; matrix products, arithmetic and copies ran while one was open for 1% of the time, Pallas kernels for 10%

profile of v3, /device:TPU:1, one launch (start us, length us, event | category | flops | bytes accessed | tf_op | source)
XLA Modules:
  0.0 122.1 jit_solution(5368956547138880939)
XLA Ops:
  0.8 6.2 %collective-permute-start = (f32[72,256]{1,0:T(8,128)S(1)}, f32[72,256]{1,0:T(8,128)S(1)}, u32[]{:S(2)}, u32[]{:S(2)}) collective-permute-start(f32[72,256]{1,0:T(8,128)S(1)} %shard_map.38), channel_id=1, source_target_pairs={{0,0},{1,32},{2,64},{3,96},{4,16},{5,48},{6,80},{7,112},{8,1},{9,3... | collective-permute-start | bytes 221192 | tf_op jit(solution)/shard_map/ppermute | solution.py:18
  7.0 3.6 %collective-permute-done = f32[72,256]{1,0:T(8,128)S(1)} collective-permute-done((f32[72,256]{1,0:T(8,128)S(1)}, f32[72,256]{1,0:T(8,128)S(1)}, u32[]{:S(2)}, u32[]{:S(2)}) %collective-permute-start) | collective-permute-done | bytes 73760 | tf_op jit(solution)/shard_map/ppermute | solution.py:18
  11.0 1.1 broadcast_in_dim.4
  12.1 9.8 %all-to-all-start = ((f32[16,72,256]{2,1,0:T(8,128)}), f32[16,72,256]{2,1,0:T(8,128)}, u32[]{:S(2)}, u32[]{:S(2)}) async-start(f32[16,72,256]{2,1,0:T(8,128)} %broadcast_in_dim.4), calls=%async_computation | async-start | bytes 2359296 | tf_op jit(solution)/shard_map/all_to_all | solution.py:40
  22.9 4.3 %collective-permute-done.2 = f32[2,72,256]{2,1,0:T(8,128)S(1)} collective-permute-done((f32[2,72,256]{2,1,0:T(8,128)S(1)}, f32[2,72,256]{2,1,0:T(8,128)S(1)}, u32[]{:S(2)}, u32[]{:S(2)}) %collective-permute-start.2) | collective-permute-done | bytes 147488 | tf_op jit(solution)/shard_map/ppermute | solution.py:14
  27.3 3.9 %collective-permute-start.3 = (f32[288,256]{1,0:T(8,128)S(1)}, f32[288,256]{1,0:T(8,128)S(1)}, u32[]{:S(2)}, u32[]{:S(2)}) collective-permute-start(f32[288,256]{1,0:T(8,128)S(1)} %bitcast.16), channel_id=1, source_target_pairs={{0,16},{16,0},{32,48},{48,32},{64,80},{80,64},{96,112},{112,96},{1... | collective-permute-start | bytes 884744 | tf_op jit(solution)/shard_map/ppermute | solution.py:14
  31.2 1.7 %shard_map.37.cov_ref = f32[576,1152]{1,0:T(8,128)S(1)} custom-call(f32[576,1152]{1,0:T(8,128)} %bitcast.19), custom_call_target="tpu_custom_call" | custom-call | tf_op jit(solution)/shard_map/pallas_call | solution.py:250
  32.9 4.8 %all-to-all-done = f32[16,72,256]{2,1,0:T(8,128)} async-done(((f32[16,72,256]{2,1,0:T(8,128)}), f32[16,72,256]{2,1,0:T(8,128)}, u32[]{:S(2)}, u32[]{:S(2)}) %all-to-all-start) | async-done | bytes 1179680 | tf_op jit(solution)/shard_map/all_to_all | solution.py:40
  37.7 3.1 %shard_map.39 = (f32[4,104,256]{2,1,0:T(8,128)S(1)}, f32[4,104,256]{2,1,0:T(8,128)S(1)}) custom-call(s32[1]{0:T(128)} %bitcast.2.core_ref, f32[576,1152]{1,0:T(8,128)S(1)} %shard_map.37.cov_ref, f32[1152,256]{1,0:T(8,128)} %bitcast.3.rows_ref, f32[288,256]{1,0:T(8,128)S(1)} %bitcast.17, f32[288,256]{1,0:T(8,128)S(1)} %collective-permute-done.3.other_ref), custom_call_target="tpu_custom_call" | custom-call | flops 1245708288 | bytes 2654208 | tf_op jit(solution)/shard_map/pallas_call | solution.py:83
  40.8 3.8 %collective-permute-start.4 = (f32[4,104,256]{2,1,0:T(8,128)S(1)}, f32[4,104,256]{2,1,0:T(8,128)S(1)}, u32[]{:S(2)}, u32[]{:S(2)}) collective-permute-start(f32[4,104,256]{2,1,0:T(8,128)S(1)} %get-tuple-element.14), channel_id=1, source_target_pairs={{0,16},{16,0},{32,48},{48,32},{64,80},{80,64},{96,112},{112,96},{1... | collective-permute-start | bytes 1277960 | tf_op jit(solution)/shard_map/ppermute | solution.py:14
  44.7 1.4 %collective-permute-done.4.mate_ref = f32[4,104,256]{2,1,0:T(8,128)S(1)} collective-permute-done((f32[4,104,256]{2,1,0:T(8,128)S(1)}, f32[4,104,256]{2,1,0:T(8,128)S(1)}, u32[]{:S(2)}, u32[]{:S(2)}) %collective-permute-start.4) | collective-permute-done | bytes 426016 | tf_op jit(solution)/shard_map/ppermute | solution.py:14
  46.8 1.9 %collective-permute-start.6 = (f32[104,256]{1,0:T(8,128)S(1)}, f32[104,256]{1,0:T(8,128)S(1)}, u32[]{:S(2)}, u32[]{:S(2)}) collective-permute-start(f32[104,256]{1,0:T(8,128)S(1)} %get-tuple-element.17), channel_id=1, source_target_pairs={{0,64},{16,80},{32,96},{48,112},{64,0},{80,16},{96,32},{112,48},{1... | collective-permute-start | bytes 319496 | tf_op jit(solution)/shard_map/ppermute | solution.py:14
  48.7 1.3 %collective-permute-start.7 = (f32[104,256]{1,0:T(8,128)S(1)}, f32[104,256]{1,0:T(8,128)S(1)}, u32[]{:S(2)}, u32[]{:S(2)}) collective-permute-start(f32[104,256]{1,0:T(8,128)S(1)} %get-tuple-element.18), channel_id=1, source_target_pairs={{0,96},{16,112},{32,64},{48,80},{64,32},{80,48},{96,0},{112,16},{1... | collective-permute-start | bytes 319496 | tf_op jit(solution)/shard_map/ppermute | solution.py:14
  50.3 3.3 %collective-permute-done.6.c_ref = f32[104,256]{1,0:T(8,128)S(1)} collective-permute-done((f32[104,256]{1,0:T(8,128)S(1)}, f32[104,256]{1,0:T(8,128)S(1)}, u32[]{:S(2)}, u32[]{:S(2)}) %collective-permute-start.6) | collective-permute-done | bytes 106528 | tf_op jit(solution)/shard_map/ppermute | solution.py:14
  53.7 2.6 %collective-permute-done.7.d_ref = f32[104,256]{1,0:T(8,128)S(1)} collective-permute-done((f32[104,256]{1,0:T(8,128)S(1)}, f32[104,256]{1,0:T(8,128)S(1)}, u32[]{:S(2)}, u32[]{:S(2)}) %collective-permute-start.7) | collective-permute-done | bytes 106528 | tf_op jit(solution)/shard_map/ppermute | solution.py:14
  56.3 2.1 %collective-permute-start.8 = (f32[72,256]{1,0:T(8,128)S(1)}, f32[72,256]{1,0:T(8,128)S(1)}, u32[]{:S(2)}, u32[]{:S(2)}) collective-permute-start(f32[72,256]{1,0:T(8,128)S(1)} %get-tuple-element.19.product_ref), channel_id=1, source_target_pairs={{0,0},{1,8},{2,16},{3,24},{4,32},{5,40},{6,48},{7,56},{8,64},{9,72... | collective-permute-start | bytes 221192 | tf_op jit(solution)/shard_map/ppermute | solution.py:18
  58.3 5.6 %collective-permute-done.8 = f32[72,256]{1,0:T(8,128)S(1)} collective-permute-done((f32[72,256]{1,0:T(8,128)S(1)}, f32[72,256]{1,0:T(8,128)S(1)}, u32[]{:S(2)}, u32[]{:S(2)}) %collective-permute-start.8) | collective-permute-done | bytes 73760 | tf_op jit(solution)/shard_map/ppermute | solution.py:18
  63.9 1.1 broadcast_in_dim.5
  65.0 6.2 %all-to-all-start.1 = ((f32[16,72,256]{2,1,0:T(8,128)}), f32[16,72,256]{2,1,0:T(8,128)}, u32[]{:S(2)}, u32[]{:S(2)}) async-start(f32[16,72,256]{2,1,0:T(8,128)} %broadcast_in_dim.5), calls=%async_computation.1 | async-start | bytes 2359296 | tf_op jit(solution)/shard_map/all_to_all | solution.py:40
  71.3 2.6 %collective-permute-start.11 = (f32[32,256]{1,0:T(8,128)S(1)}, f32[32,256]{1,0:T(8,128)S(1)}, u32[]{:S(2)}, u32[]{:S(2)}) collective-permute-start(f32[32,256]{1,0:T(8,128)S(1)} %get-tuple-element.20), channel_id=1, source_target_pairs={{0,3},{1,2},{2,1},{3,0},{4,7},{5,6},{6,5},{7,4},{8,11},{9,10},{10,... | collective-permute-start | bytes 98312 | tf_op jit(solution)/shard_map/ppermute | solution.py:14
  74.6 2.3 %collective-permute-done.11 = f32[32,256]{1,0:T(8,128)S(1)} collective-permute-done((f32[32,256]{1,0:T(8,128)S(1)}, f32[32,256]{1,0:T(8,128)S(1)}, u32[]{:S(2)}, u32[]{:S(2)}) %collective-permute-start.11) | collective-permute-done | bytes 32800 | tf_op jit(solution)/shard_map/ppermute | solution.py:14
  76.9 4.0 %collective-permute-done.10 = f32[32,256]{1,0:T(8,128)S(1)} collective-permute-done((f32[32,256]{1,0:T(8,128)S(1)}, f32[32,256]{1,0:T(8,128)S(1)}, u32[]{:S(2)}, u32[]{:S(2)}) %collective-permute-start.10) | collective-permute-done | bytes 32800 | tf_op jit(solution)/shard_map/ppermute | solution.py:14
  81.0 9.4 %collective-permute-start.14 = (f32[32,256]{1,0:T(8,128)S(1)}, f32[32,256]{1,0:T(8,128)S(1)}, u32[]{:S(2)}, u32[]{:S(2)}) collective-permute-start(f32[32,256]{1,0:T(8,128)S(1)} %add_add_fusion.a_ref), channel_id=1, source_target_pairs={{0,12},{1,13},{2,14},{3,15},{4,8},{5,9},{6,10},{7,11},{8,4},{9,5},... | collective-permute-start | bytes 98312 | tf_op jit(solution)/shard_map/ppermute | solution.py:14
  90.4 1.2 collective-permute-start.13
  91.7 3.0 %collective-permute-done.13.c_ref = f32[32,256]{1,0:T(8,128)S(1)} collective-permute-done((f32[32,256]{1,0:T(8,128)S(1)}, f32[32,256]{1,0:T(8,128)S(1)}, u32[]{:S(2)}, u32[]{:S(2)}) %collective-permute-start.13) | collective-permute-done | bytes 32800 | tf_op jit(solution)/shard_map/ppermute | solution.py:14
  94.7 3.4 %collective-permute-start.17 = (f32[104,256]{1,0:T(8,128)S(1)}, f32[104,256]{1,0:T(8,128)S(1)}, u32[]{:S(2)}, u32[]{:S(2)}) collective-permute-start(f32[104,256]{1,0:T(8,128)S(1)} %shard_map.42.refs_0_), channel_id=1, source_target_pairs={{0,96},{16,112},{32,64},{48,80},{64,32},{80,48},{96,0},{112,16},{1... | collective-permute-start | bytes 319496 | tf_op jit(solution)/shard_map/ppermute | solution.py:14
  98.8 2.1 %collective-permute-done.17.refs_3_ = f32[104,256]{1,0:T(8,128)S(1)} collective-permute-done((f32[104,256]{1,0:T(8,128)S(1)}, f32[104,256]{1,0:T(8,128)S(1)}, u32[]{:S(2)}, u32[]{:S(2)}) %collective-permute-start.17) | collective-permute-done | bytes 106528 | tf_op jit(solution)/shard_map/ppermute | solution.py:14
  100.9 2.4 %collective-permute-done.16.refs_2_ = f32[104,256]{1,0:T(8,128)S(1)} collective-permute-done((f32[104,256]{1,0:T(8,128)S(1)}, f32[104,256]{1,0:T(8,128)S(1)}, u32[]{:S(2)}, u32[]{:S(2)}) %collective-permute-start.16) | collective-permute-done | bytes 106528 | tf_op jit(solution)/shard_map/ppermute | solution.py:14
  103.3 3.2 %collective-permute-start.18 = (f32[4,104,256]{2,1,0:T(8,128)S(1)}, f32[4,104,256]{2,1,0:T(8,128)S(1)}, u32[]{:S(2)}, u32[]{:S(2)}) collective-permute-start(f32[4,104,256]{2,1,0:T(8,128)S(1)} %shard_map.43.own_ref), channel_id=1, source_target_pairs={{0,16},{16,0},{32,48},{48,32},{64,80},{80,64},{96,112},{112,96},{1... | collective-permute-start | bytes 1277960 | tf_op jit(solution)/shard_map/ppermute | solution.py:14
  106.4 1.4 %collective-permute-done.18.other_ref = f32[4,104,256]{2,1,0:T(8,128)S(1)} collective-permute-done((f32[4,104,256]{2,1,0:T(8,128)S(1)}, f32[4,104,256]{2,1,0:T(8,128)S(1)}, u32[]{:S(2)}, u32[]{:S(2)}) %collective-permute-start.18) | collective-permute-done | bytes 426016 | tf_op jit(solution)/shard_map/ppermute | solution.py:14
  107.8 9.9 %shard_map.44.inv_ref = f32[256,256]{1,0:T(8,128)S(1)} custom-call(s32[1]{0:T(128)} %bitcast.2.core_ref, f32[4,104,256]{2,1,0:T(8,128)S(1)} %shard_map.43.own_ref, f32[4,104,256]{2,1,0:T(8,128)S(1)} %collective-permute-done.18.other_ref, f32[1,256]{1,0:T(1,128)S(1)} %bitcast.18), custom_call_target="tpu_custom_call" | custom-call | flops 1342177280 | bytes 786432 | tf_op jit(solution)/shard_map/pallas_call | solution.py:318
  118.2 3.9 %shard_map.46 = f32[576,1152]{1,0:T(8,128)} custom-call(f32[576,1152]{1,0:T(8,128)S(1)} %shard_map.37.cov_ref, f32[1152,256]{1,0:T(8,128)} %bitcast.9.rows_ref, f32[576,256]{1,0:T(8,128)S(1)} %shard_map.45.gain_ref), custom_call_target="tpu_custom_call" | custom-call | flops 1019215872 | bytes 2654208 | tf_op jit(solution)/shard_map/pallas_call | solution.py:204
  (29 shorter events, 5.4 us)
Async XLA Ops:
  0.8 9.9 %collective-permute-start = (f32[72,256]{1,0:T(8,128)S(1)}, f32[72,256]{1,0:T(8,128)S(1)}, u32[]{:S(2)}, u32[]{:S(2)}) collective-permute-start(f32[72,256]{1,0:T(8,128)S(1)} %shard_map.38), channel_id=1, source_target_pairs={{0,0},{1,32},{2,64},{3,96},{4,16},{5,48},{6,80},{7,112},{8,1},{9,3... | collective-permute-start | bytes 221192 | tf_op jit(solution)/shard_map/ppermute | solution.py:18
  10.7 11.2 %collective-permute-start.1 = (f32[72,256]{1,0:T(8,128)S(1)}, f32[72,256]{1,0:T(8,128)S(1)}, u32[]{:S(2)}, u32[]{:S(2)}) collective-permute-start(f32[72,256]{1,0:T(8,128)S(1)} %collective-permute-done), channel_id=1, source_target_pairs={{0,32},{16,48},{32,0},{48,16},{64,96},{80,112},{96,64},{112,80},{1... | collective-permute-start | bytes 221192 | tf_op jit(solution)/shard_map/ppermute | solution.py:14
  12.1 25.6 %all-to-all-start = ((f32[16,72,256]{2,1,0:T(8,128)}), f32[16,72,256]{2,1,0:T(8,128)}, u32[]{:S(2)}, u32[]{:S(2)}) async-start(f32[16,72,256]{2,1,0:T(8,128)} %broadcast_in_dim.4), calls=%async_computation | async-start | bytes 2359296 | tf_op jit(solution)/shard_map/all_to_all | solution.py:40
  21.9 5.3 %collective-permute-start.2 = (f32[2,72,256]{2,1,0:T(8,128)S(1)}, f32[2,72,256]{2,1,0:T(8,128)S(1)}, u32[]{:S(2)}, u32[]{:S(2)}) collective-permute-start(f32[2,72,256]{2,1,0:T(8,128)S(1)} %pad_maximum_fusion.1), channel_id=1, source_target_pairs={{0,96},{16,112},{32,64},{48,80},{64,32},{80,48},{96,0},{112,16},{1... | collective-permute-start | bytes 442376 | tf_op jit(solution)/shard_map/ppermute | solution.py:14
  27.3 5.7 %collective-permute-start.3 = (f32[288,256]{1,0:T(8,128)S(1)}, f32[288,256]{1,0:T(8,128)S(1)}, u32[]{:S(2)}, u32[]{:S(2)}) collective-permute-start(f32[288,256]{1,0:T(8,128)S(1)} %bitcast.16), channel_id=1, source_target_pairs={{0,16},{16,0},{32,48},{48,32},{64,80},{80,64},{96,112},{112,96},{1... | collective-permute-start | bytes 884744 | tf_op jit(solution)/shard_map/ppermute | solution.py:14
  40.8 5.2 %collective-permute-start.4 = (f32[4,104,256]{2,1,0:T(8,128)S(1)}, f32[4,104,256]{2,1,0:T(8,128)S(1)}, u32[]{:S(2)}, u32[]{:S(2)}) collective-permute-start(f32[4,104,256]{2,1,0:T(8,128)S(1)} %get-tuple-element.14), channel_id=1, source_target_pairs={{0,16},{16,0},{32,48},{48,32},{64,80},{80,64},{96,112},{112,96},{1... | collective-permute-start | bytes 1277960 | tf_op jit(solution)/shard_map/ppermute | solution.py:14
  46.1 4.2 %collective-permute-start.5 = (f32[104,256]{1,0:T(8,128)S(1)}, f32[104,256]{1,0:T(8,128)S(1)}, u32[]{:S(2)}, u32[]{:S(2)}) collective-permute-start(f32[104,256]{1,0:T(8,128)S(1)} %get-tuple-element.16), channel_id=1, source_target_pairs={{0,32},{16,48},{32,0},{48,16},{64,96},{80,112},{96,64},{112,80},{1... | collective-permute-start | bytes 319496 | tf_op jit(solution)/shard_map/ppermute | solution.py:14
  46.8 6.8 %collective-permute-start.6 = (f32[104,256]{1,0:T(8,128)S(1)}, f32[104,256]{1,0:T(8,128)S(1)}, u32[]{:S(2)}, u32[]{:S(2)}) collective-permute-start(f32[104,256]{1,0:T(8,128)S(1)} %get-tuple-element.17), channel_id=1, source_target_pairs={{0,64},{16,80},{32,96},{48,112},{64,0},{80,16},{96,32},{112,48},{1... | collective-permute-start | bytes 319496 | tf_op jit(solution)/shard_map/ppermute | solution.py:14
  48.7 7.6 %collective-permute-start.7 = (f32[104,256]{1,0:T(8,128)S(1)}, f32[104,256]{1,0:T(8,128)S(1)}, u32[]{:S(2)}, u32[]{:S(2)}) collective-permute-start(f32[104,256]{1,0:T(8,128)S(1)} %get-tuple-element.18), channel_id=1, source_target_pairs={{0,96},{16,112},{32,64},{48,80},{64,32},{80,48},{96,0},{112,16},{1... | collective-permute-start | bytes 319496 | tf_op jit(solution)/shard_map/ppermute | solution.py:14
  56.3 7.7 %collective-permute-start.8 = (f32[72,256]{1,0:T(8,128)S(1)}, f32[72,256]{1,0:T(8,128)S(1)}, u32[]{:S(2)}, u32[]{:S(2)}) collective-permute-start(f32[72,256]{1,0:T(8,128)S(1)} %get-tuple-element.19.product_ref), channel_id=1, source_target_pairs={{0,0},{1,8},{2,16},{3,24},{4,32},{5,40},{6,48},{7,56},{8,64},{9,72... | collective-permute-start | bytes 221192 | tf_op jit(solution)/shard_map/ppermute | solution.py:18
  65.0 53.1 %all-to-all-start.1 = ((f32[16,72,256]{2,1,0:T(8,128)}), f32[16,72,256]{2,1,0:T(8,128)}, u32[]{:S(2)}, u32[]{:S(2)}) async-start(f32[16,72,256]{2,1,0:T(8,128)} %broadcast_in_dim.5), calls=%async_computation.1 | async-start | bytes 2359296 | tf_op jit(solution)/shard_map/all_to_all | solution.py:40
  71.3 36.6 %copy-start = (f32[2,128]{1,0:T(2,128)S(1)}, f32[2,128]{1,0:T(2,128)}, u32[]{:S(2)}) copy-start(f32[2,128]{1,0:T(2,128)} %param.5) | copy-start | bytes 3076
  71.3 5.6 %collective-permute-start.11 = (f32[32,256]{1,0:T(8,128)S(1)}, f32[32,256]{1,0:T(8,128)S(1)}, u32[]{:S(2)}, u32[]{:S(2)}) collective-permute-start(f32[32,256]{1,0:T(8,128)S(1)} %get-tuple-element.20), channel_id=1, source_target_pairs={{0,3},{1,2},{2,1},{3,0},{4,7},{5,6},{6,5},{7,4},{8,11},{9,10},{10,... | collective-permute-start | bytes 98312 | tf_op jit(solution)/shard_map/ppermute | solution.py:14
  73.9 7.0 %collective-permute-start.10 = (f32[32,256]{1,0:T(8,128)S(1)}, f32[32,256]{1,0:T(8,128)S(1)}, u32[]{:S(2)}, u32[]{:S(2)}) collective-permute-start(f32[32,256]{1,0:T(8,128)S(1)} %get-tuple-element.20), channel_id=1, source_target_pairs={{0,2},{1,3},{2,0},{3,1},{4,6},{5,7},{6,4},{7,5},{8,10},{9,11},{10,... | collective-permute-start | bytes 98312 | tf_op jit(solution)/shard_map/ppermute | solution.py:14
  74.5 6.5 %collective-permute-start.9 = (f32[32,256]{1,0:T(8,128)S(1)}, f32[32,256]{1,0:T(8,128)S(1)}, u32[]{:S(2)}, u32[]{:S(2)}) collective-permute-start(f32[32,256]{1,0:T(8,128)S(1)} %get-tuple-element.20), channel_id=1, source_target_pairs={{0,1},{1,0},{2,3},{3,2},{4,5},{5,4},{6,7},{7,6},{8,9},{9,8},{10,11... | collective-permute-start | bytes 98312 | tf_op jit(solution)/shard_map/ppermute | solution.py:14
  81.0 10.7 %collective-permute-start.14 = (f32[32,256]{1,0:T(8,128)S(1)}, f32[32,256]{1,0:T(8,128)S(1)}, u32[]{:S(2)}, u32[]{:S(2)}) collective-permute-start(f32[32,256]{1,0:T(8,128)S(1)} %add_add_fusion.a_ref), channel_id=1, source_target_pairs={{0,12},{1,13},{2,14},{3,15},{4,8},{5,9},{6,10},{7,11},{8,4},{9,5},... | collective-permute-start | bytes 98312 | tf_op jit(solution)/shard_map/ppermute | solution.py:14
  90.4 4.3 %collective-permute-start.13 = (f32[32,256]{1,0:T(8,128)S(1)}, f32[32,256]{1,0:T(8,128)S(1)}, u32[]{:S(2)}, u32[]{:S(2)}) collective-permute-start(f32[32,256]{1,0:T(8,128)S(1)} %add_add_fusion.a_ref), channel_id=1, source_target_pairs={{0,8},{1,9},{2,10},{3,11},{4,12},{5,13},{6,14},{7,15},{8,0},{9,1},... | collective-permute-start | bytes 98312 | tf_op jit(solution)/shard_map/ppermute | solution.py:14
  91.6 3.1 %collective-permute-start.12 = (f32[32,256]{1,0:T(8,128)S(1)}, f32[32,256]{1,0:T(8,128)S(1)}, u32[]{:S(2)}, u32[]{:S(2)}) collective-permute-start(f32[32,256]{1,0:T(8,128)S(1)} %add_add_fusion.a_ref), channel_id=1, source_target_pairs={{0,4},{1,5},{2,6},{3,7},{4,0},{5,1},{6,2},{7,3},{8,12},{9,13},{10,... | collective-permute-start | bytes 98312 | tf_op jit(solution)/shard_map/ppermute | solution.py:14
  94.7 6.2 %collective-permute-start.17 = (f32[104,256]{1,0:T(8,128)S(1)}, f32[104,256]{1,0:T(8,128)S(1)}, u32[]{:S(2)}, u32[]{:S(2)}) collective-permute-start(f32[104,256]{1,0:T(8,128)S(1)} %shard_map.42.refs_0_), channel_id=1, source_target_pairs={{0,96},{16,112},{32,64},{48,80},{64,32},{80,48},{96,0},{112,16},{1... | collective-permute-start | bytes 319496 | tf_op jit(solution)/shard_map/ppermute | solution.py:14
  98.1 5.2 %collective-permute-start.16 = (f32[104,256]{1,0:T(8,128)S(1)}, f32[104,256]{1,0:T(8,128)S(1)}, u32[]{:S(2)}, u32[]{:S(2)}) collective-permute-start(f32[104,256]{1,0:T(8,128)S(1)} %shard_map.42.refs_0_), channel_id=1, source_target_pairs={{0,64},{16,80},{32,96},{48,112},{64,0},{80,16},{96,32},{112,48},{1... | collective-permute-start | bytes 319496 | tf_op jit(solution)/shard_map/ppermute | solution.py:14
  98.6 4.6 %collective-permute-start.15 = (f32[104,256]{1,0:T(8,128)S(1)}, f32[104,256]{1,0:T(8,128)S(1)}, u32[]{:S(2)}, u32[]{:S(2)}) collective-permute-start(f32[104,256]{1,0:T(8,128)S(1)} %shard_map.42.refs_0_), channel_id=1, source_target_pairs={{0,32},{16,48},{32,0},{48,16},{64,96},{80,112},{96,64},{112,80},{1... | collective-permute-start | bytes 319496 | tf_op jit(solution)/shard_map/ppermute | solution.py:14
  103.3 4.6 %collective-permute-start.18 = (f32[4,104,256]{2,1,0:T(8,128)S(1)}, f32[4,104,256]{2,1,0:T(8,128)S(1)}, u32[]{:S(2)}, u32[]{:S(2)}) collective-permute-start(f32[4,104,256]{2,1,0:T(8,128)S(1)} %shard_map.43.own_ref), channel_id=1, source_target_pairs={{0,16},{16,0},{32,48},{48,32},{64,80},{80,64},{96,112},{112,96},{1... | collective-permute-start | bytes 1277960 | tf_op jit(solution)/shard_map/ppermute | solution.py:14

commit v4 on v3

--- a/solution.py
+++ b/solution.py
@@ -98,36 +98,38 @@
 
 
 def pieces_kernel(z_ref, kept_ref, mate_ref, *out_refs):
-    for d, ref in enumerate(out_refs):
+    block = out_refs[0].shape[0]
+    for d in range(4):
         at = z_ref[0] ^ d
-        ref[...] = kept_ref[at] + mate_ref[at]
-
-
-def pieces(z, kept, mate):
-    piece = pltpu.VMEM(kept.shape[1:], jnp.float32)
-    return pl.pallas_call(
+        out_refs[d][...] = kept_ref[at, :block, :] + mate_ref[at, :block, :]
+        out_refs[4 + d][...] = kept_ref[at, block:, :] + mate_ref[at, block:, :]
+
+
+def pieces(z, kept, mate, block):
+    _, depth, width = kept.shape
+    product = pltpu.VMEM((block, width), jnp.float32)
+    share = pltpu.VMEM((depth - block, width), jnp.float32)
+    out = pl.pallas_call(
         pieces_kernel,
-        out_shape=(piece,) * 4,
+        out_shape=(product,) * 4 + (share,) * 4,
         in_specs=[SCALAR, VMEM, VMEM],
-        out_specs=(VMEM,) * 4,
+        out_specs=(VMEM,) * 8,
         compiler_params=pltpu.CompilerParams(vmem_limit_bytes=4 << 20),
     )(z.reshape(1), kept, mate)
-
-
-def total_kernel(a_ref, b_ref, c_ref, d_ref, product_ref, share_ref):
-    total = (a_ref[...] + b_ref[...]) + (c_ref[...] + d_ref[...])
-    product_ref[...] = total[: product_ref.shape[0]]
-    share_ref[...] = total[product_ref.shape[0] :]
-
-
-def totals(terms, block):
-    depth, width = terms[0].shape
+    return out[:4], out[4:]
+
+
+def total_kernel(a_ref, b_ref, c_ref, d_ref, out_ref):
+    out_ref[...] = (a_ref[...] + b_ref[...]) + (c_ref[...] + d_ref[...])
+
+
+def total_of(terms):
     return pl.pallas_call(
         total_kernel,
-        out_shape=(pltpu.VMEM((block, width), jnp.float32), pltpu.VMEM((depth - block, width), jnp.float32)),
+        out_shape=pltpu.VMEM(terms[0].shape, jnp.float32),
         in_specs=[VMEM] * 4,
-        out_specs=(VMEM, VMEM),
-        compiler_params=pltpu.CompilerParams(vmem_limit_bytes=4 << 20),
+        out_specs=VMEM,
+        compiler_params=pltpu.CompilerParams(vmem_limit_bytes=2 << 20),
     )(*terms)
 
 
@@ -341,13 +343,12 @@
     quad = zb.reshape(4 * block, width)
 
     kept, given = products(core, turned, row_features, quad, to_xor(quad, "row", 1))
-    terms = pieces(z, kept, to_xor(given, "row", 1))
-    product, share = totals([terms[0]] + [to_xor(terms[d], "row", 2 * d) for d in (1, 2, 3)], block)
-
-    for unit in (1, 4):
-        sums = [share] + [to_xor(share, "col", d * unit) for d in (1, 2, 3)]
-        share = (sums[0] + sums[1]) + (sums[2] + sums[3])
-    joined = join(product, sums)
+    terms, shares = pieces(z, kept, to_xor(given, "row", 1), block)
+    share = total_of([shares[0]] + [to_xor(shares[d], "row", 2 * d) for d in (1, 2, 3)])
+    product = total_of([terms[0]] + [to_xor(terms[d], "row", 2 * d) for d in (1, 2, 3)])
+
+    share = total_of([share] + [to_xor(share, "col", d) for d in (1, 2, 3)])
+    joined = join(product, [share] + [to_xor(share, "col", 4 * d) for d in (1, 2, 3)])
     packed = pack(z, [joined] + [to_xor(joined, "row", 2 * d) for d in (1, 2, 3)])
     mate = to_xor(packed, "row", 1)
 

time: 123 us -> 123 us (level)
    ppermute x17 -> x20, starting transfers between devices: 34.1 us -> 32.6 us  [to_xor(): return lax.ppermute(value, axis, [(i, i ^ bits) for i in range(size)])]
    ppermute x2, waiting for transfers between devices: 9.24 us -> 7.8 us  [to_place(): lax.ppermute(value, ('row', 'col'), [(i, owner(i)) for i in range(128)])]
    ppermute x17 -> x20, waiting for transfers between devices: 27.3 us -> 28.4 us  [to_xor(): return lax.ppermute(value, axis, [(i, i ^ bits) for i in range(size)])]
  transfers between devices with their start and end apart: 21 -> 24, of which waited for: 16 -> 17; matrix products, arithmetic and copies ran while one was open for 1% -> 1% of each run, Pallas kernels for 10% -> 10%
where the time goes in v4:
time: 123 us; the launch traced here: 122 us
  starting transfers between devices  59 us (48%)
  waiting for transfers between devices  41 us (33%)
  Pallas kernels  20 us (16%)
  local copies, waits for them, and re-layouts  2.18 us (2%)
    ppermute x20, starting transfers between devices, to_xor(): return lax.ppermute(value, axis, [(i, i ^ bits) for i in range(size)])  32.6 us
    ppermute x20, waiting for transfers between devices, to_xor(): return lax.ppermute(value, axis, [(i, i ^ bits) for i in range(size)])  28.4 us
    all_to_all x2, starting transfers between devices, to_plane(): lax.all_to_all(sent, 'col', 0, 0, tiled=True).reshape(-1, block.shape[-1])  17.2 us
    pallas_call x1, Pallas kernels, inverse_of(): pl.pallas_call(invert_kernel, out_shape=pltpu.VMEM((n, n), jnp.float32),...  9.88 us
    ppermute x2, starting transfers between devices, to_place(): lax.ppermute(value, ('row', 'col'), [(i, owner(i)) for i in range(128)])  9.22 us
    ppermute x2, waiting for transfers between devices, to_place(): lax.ppermute(value, ('row', 'col'), [(i, owner(i)) for i in range(128)])  7.8 us
    all_to_all x2, waiting for transfers between devices, to_plane(): lax.all_to_all(sent, 'col', 0, 0, tiled=True).reshape(-1, block.shape[-1])  4.76 us
    pallas_call x1, Pallas kernels, update(): pl.pallas_call(update_kernel, out_shape=pltpu.HBM(cov.shape, jnp.float32)...  3.92 us
  transfers between devices with their start and end apart: 24, of which 17 were waited for; matrix products, arithmetic and copies ran while one was open for 1% of the time, Pallas kernels for 10%

profile of v4, /device:TPU:1, one launch (start us, length us, event | category | flops | bytes accessed | tf_op | source)
XLA Modules:
  0.0 122.4 jit_solution(9108211764818823244)
XLA Ops:
  0.8 6.2 %collective-permute-start = (f32[72,256]{1,0:T(8,128)S(1)}, f32[72,256]{1,0:T(8,128)S(1)}, u32[]{:S(2)}, u32[]{:S(2)}) collective-permute-start(f32[72,256]{1,0:T(8,128)S(1)} %shard_map.38), channel_id=1, source_target_pairs={{0,0},{1,32},{2,64},{3,96},{4,16},{5,48},{6,80},{7,112},{8,1},{9,3... | collective-permute-start | bytes 221192 | tf_op jit(solution)/shard_map/ppermute | solution.py:18
  7.0 3.6 %collective-permute-done = f32[72,256]{1,0:T(8,128)S(1)} collective-permute-done((f32[72,256]{1,0:T(8,128)S(1)}, f32[72,256]{1,0:T(8,128)S(1)}, u32[]{:S(2)}, u32[]{:S(2)}) %collective-permute-start) | collective-permute-done | bytes 73760 | tf_op jit(solution)/shard_map/ppermute | solution.py:18
  11.0 1.1 broadcast_in_dim.4
  12.1 9.8 %all-to-all-start = ((f32[16,72,256]{2,1,0:T(8,128)}), f32[16,72,256]{2,1,0:T(8,128)}, u32[]{:S(2)}, u32[]{:S(2)}) async-start(f32[16,72,256]{2,1,0:T(8,128)} %broadcast_in_dim.4), calls=%async_computation | async-start | bytes 2359296 | tf_op jit(solution)/shard_map/all_to_all | solution.py:40
  22.9 4.3 %collective-permute-done.2 = f32[2,72,256]{2,1,0:T(8,128)S(1)} collective-permute-done((f32[2,72,256]{2,1,0:T(8,128)S(1)}, f32[2,72,256]{2,1,0:T(8,128)S(1)}, u32[]{:S(2)}, u32[]{:S(2)}) %collective-permute-start.2) | collective-permute-done | bytes 147488 | tf_op jit(solution)/shard_map/ppermute | solution.py:14
  27.3 3.9 %collective-permute-start.3 = (f32[288,256]{1,0:T(8,128)S(1)}, f32[288,256]{1,0:T(8,128)S(1)}, u32[]{:S(2)}, u32[]{:S(2)}) collective-permute-start(f32[288,256]{1,0:T(8,128)S(1)} %bitcast.16), channel_id=1, source_target_pairs={{0,16},{16,0},{32,48},{48,32},{64,80},{80,64},{96,112},{112,96},{1... | collective-permute-start | bytes 884744 | tf_op jit(solution)/shard_map/ppermute | solution.py:14
  31.2 1.7 %shard_map.37.cov_ref = f32[576,1152]{1,0:T(8,128)S(1)} custom-call(f32[576,1152]{1,0:T(8,128)} %bitcast.19), custom_call_target="tpu_custom_call" | custom-call | tf_op jit(solution)/shard_map/pallas_call | solution.py:252
  32.9 4.8 %all-to-all-done = f32[16,72,256]{2,1,0:T(8,128)} async-done(((f32[16,72,256]{2,1,0:T(8,128)}), f32[16,72,256]{2,1,0:T(8,128)}, u32[]{:S(2)}, u32[]{:S(2)}) %all-to-all-start) | async-done | bytes 1179680 | tf_op jit(solution)/shard_map/all_to_all | solution.py:40
  37.7 3.1 %shard_map.39 = (f32[4,104,256]{2,1,0:T(8,128)S(1)}, f32[4,104,256]{2,1,0:T(8,128)S(1)}) custom-call(s32[1]{0:T(128)} %bitcast.2.core_ref, f32[576,1152]{1,0:T(8,128)S(1)} %shard_map.37.cov_ref, f32[1152,256]{1,0:T(8,128)} %bitcast.3.rows_ref, f32[288,256]{1,0:T(8,128)S(1)} %bitcast.17, f32[288,256]{1,0:T(8,128)S(1)} %collective-permute-done.3.other_ref), custom_call_target="tpu_custom_call" | custom-call | flops 1245708288 | bytes 2654208 | tf_op jit(solution)/shard_map/pallas_call | solution.py:83
  40.8 3.8 %collective-permute-start.4 = (f32[4,104,256]{2,1,0:T(8,128)S(1)}, f32[4,104,256]{2,1,0:T(8,128)S(1)}, u32[]{:S(2)}, u32[]{:S(2)}) collective-permute-start(f32[4,104,256]{2,1,0:T(8,128)S(1)} %get-tuple-element.16), channel_id=1, source_target_pairs={{0,16},{16,0},{32,48},{48,32},{64,80},{80,64},{96,112},{112,96},{1... | collective-permute-start | bytes 1277960 | tf_op jit(solution)/shard_map/ppermute | solution.py:14
  44.7 1.4 %collective-permute-done.4.mate_ref = f32[4,104,256]{2,1,0:T(8,128)S(1)} collective-permute-done((f32[4,104,256]{2,1,0:T(8,128)S(1)}, f32[4,104,256]{2,1,0:T(8,128)S(1)}, u32[]{:S(2)}, u32[]{:S(2)}) %collective-permute-start.4) | collective-permute-done | bytes 426016 | tf_op jit(solution)/shard_map/ppermute | solution.py:14
  46.8 1.9 %collective-permute-start.6 = (f32[72,256]{1,0:T(8,128)S(1)}, f32[72,256]{1,0:T(8,128)S(1)}, u32[]{:S(2)}, u32[]{:S(2)}) collective-permute-start(f32[72,256]{1,0:T(8,128)S(1)} %get-tuple-element.19), channel_id=1, source_target_pairs={{0,64},{16,80},{32,96},{48,112},{64,0},{80,16},{96,32},{112,48},{1... | collective-permute-start | bytes 221192 | tf_op jit(solution)/shard_map/ppermute | solution.py:14
  48.7 1.3 %collective-permute-start.7 = (f32[72,256]{1,0:T(8,128)S(1)}, f32[72,256]{1,0:T(8,128)S(1)}, u32[]{:S(2)}, u32[]{:S(2)}) collective-permute-start(f32[72,256]{1,0:T(8,128)S(1)} %get-tuple-element.20), channel_id=1, source_target_pairs={{0,96},{16,112},{32,64},{48,80},{64,32},{80,48},{96,0},{112,16},{1... | collective-permute-start | bytes 221192 | tf_op jit(solution)/shard_map/ppermute | solution.py:14
  50.1 2.5 %collective-permute-done.6.c_ref = f32[72,256]{1,0:T(8,128)S(1)} collective-permute-done((f32[72,256]{1,0:T(8,128)S(1)}, f32[72,256]{1,0:T(8,128)S(1)}, u32[]{:S(2)}, u32[]{:S(2)}) %collective-permute-start.6) | collective-permute-done | bytes 73760 | tf_op jit(solution)/shard_map/ppermute | solution.py:14
  52.6 1.1 collective-permute-done.7.d_ref
  53.7 3.0 %collective-permute-start.8 = (f32[72,256]{1,0:T(8,128)S(1)}, f32[72,256]{1,0:T(8,128)S(1)}, u32[]{:S(2)}, u32[]{:S(2)}) collective-permute-start(f32[72,256]{1,0:T(8,128)S(1)} %shard_map.41.product_ref), channel_id=1, source_target_pairs={{0,0},{1,8},{2,16},{3,24},{4,32},{5,40},{6,48},{7,56},{8,64},{9,72... | collective-permute-start | bytes 221192 | tf_op jit(solution)/shard_map/ppermute | solution.py:18
  56.7 4.2 %collective-permute-done.8 = f32[72,256]{1,0:T(8,128)S(1)} collective-permute-done((f32[72,256]{1,0:T(8,128)S(1)}, f32[72,256]{1,0:T(8,128)S(1)}, u32[]{:S(2)}, u32[]{:S(2)}) %collective-permute-start.8) | collective-permute-done | bytes 73760 | tf_op jit(solution)/shard_map/ppermute | solution.py:18
  60.8 1.1 broadcast_in_dim.5
  61.9 7.4 %all-to-all-start.1 = ((f32[16,72,256]{2,1,0:T(8,128)}), f32[16,72,256]{2,1,0:T(8,128)}, u32[]{:S(2)}, u32[]{:S(2)}) async-start(f32[16,72,256]{2,1,0:T(8,128)} %broadcast_in_dim.5), calls=%async_computation.1 | async-start | bytes 2359296 | tf_op jit(solution)/shard_map/all_to_all | solution.py:40
  69.4 4.5 %collective-permute-start.10 = (f32[32,256]{1,0:T(8,128)S(1)}, f32[32,256]{1,0:T(8,128)S(1)}, u32[]{:S(2)}, u32[]{:S(2)}) collective-permute-start(f32[32,256]{1,0:T(8,128)S(1)} %get-tuple-element.23), channel_id=1, source_target_pairs={{0,64},{16,80},{32,96},{48,112},{64,0},{80,16},{96,32},{112,48},{1... | collective-permute-start | bytes 98312 | tf_op jit(solution)/shard_map/ppermute | solution.py:14
  74.0 1.9 %collective-permute-done.10.c_ref = f32[32,256]{1,0:T(8,128)S(1)} collective-permute-done((f32[32,256]{1,0:T(8,128)S(1)}, f32[32,256]{1,0:T(8,128)S(1)}, u32[]{:S(2)}, u32[]{:S(2)}) %collective-permute-start.10) | collective-permute-done | bytes 32800 | tf_op jit(solution)/shard_map/ppermute | solution.py:14
  75.9 2.4 %collective-permute-done.11.d_ref = f32[32,256]{1,0:T(8,128)S(1)} collective-permute-done((f32[32,256]{1,0:T(8,128)S(1)}, f32[32,256]{1,0:T(8,128)S(1)}, u32[]{:S(2)}, u32[]{:S(2)}) %collective-permute-start.11) | collective-permute-done | bytes 32800 | tf_op jit(solution)/shard_map/ppermute | solution.py:14
  78.3 2.1 %collective-permute-start.14 = (f32[32,256]{1,0:T(8,128)S(1)}, f32[32,256]{1,0:T(8,128)S(1)}, u32[]{:S(2)}, u32[]{:S(2)}) collective-permute-start(f32[32,256]{1,0:T(8,128)S(1)} %shard_map.42.a_ref), channel_id=1, source_target_pairs={{0,3},{1,2},{2,1},{3,0},{4,7},{5,6},{6,5},{7,4},{8,11},{9,10},{10,... | collective-permute-start | bytes 98312 | tf_op jit(solution)/shard_map/ppermute | solution.py:14
  81.7 6.3 %collective-permute-done.14.d_ref = f32[32,256]{1,0:T(8,128)S(1)} collective-permute-done((f32[32,256]{1,0:T(8,128)S(1)}, f32[32,256]{1,0:T(8,128)S(1)}, u32[]{:S(2)}, u32[]{:S(2)}) %collective-permute-start.14) | collective-permute-done | bytes 32800 | tf_op jit(solution)/shard_map/ppermute | solution.py:14
  90.4 1.9 %collective-permute-start.15 = (f32[32,256]{1,0:T(8,128)S(1)}, f32[32,256]{1,0:T(8,128)S(1)}, u32[]{:S(2)}, u32[]{:S(2)}) collective-permute-start(f32[32,256]{1,0:T(8,128)S(1)} %shard_map.43.a_ref), channel_id=1, source_target_pairs={{0,4},{1,5},{2,6},{3,7},{4,0},{5,1},{6,2},{7,3},{8,12},{9,13},{10,... | collective-permute-start | bytes 98312 | tf_op jit(solution)/shard_map/ppermute | solution.py:14
  94.3 2.4 %collective-permute-start.20 = (f32[104,256]{1,0:T(8,128)S(1)}, f32[104,256]{1,0:T(8,128)S(1)}, u32[]{:S(2)}, u32[]{:S(2)}) collective-permute-start(f32[104,256]{1,0:T(8,128)S(1)} %shard_map.44.refs_0_), channel_id=1, source_target_pairs={{0,96},{16,112},{32,64},{48,80},{64,32},{80,48},{96,0},{112,16},{1... | collective-permute-start | bytes 319496 | tf_op jit(solution)/shard_map/ppermute | solution.py:14
  97.6 1.9 %collective-permute-done.20.refs_3_ = f32[104,256]{1,0:T(8,128)S(1)} collective-permute-done((f32[104,256]{1,0:T(8,128)S(1)}, f32[104,256]{1,0:T(8,128)S(1)}, u32[]{:S(2)}, u32[]{:S(2)}) %collective-permute-start.20) | collective-permute-done | bytes 106528 | tf_op jit(solution)/shard_map/ppermute | solution.py:14
  99.5 2.3 %collective-permute-done.19.refs_2_ = f32[104,256]{1,0:T(8,128)S(1)} collective-permute-done((f32[104,256]{1,0:T(8,128)S(1)}, f32[104,256]{1,0:T(8,128)S(1)}, u32[]{:S(2)}, u32[]{:S(2)}) %collective-permute-start.19) | collective-permute-done | bytes 106528 | tf_op jit(solution)/shard_map/ppermute | solution.py:14
  101.8 5.0 %collective-permute-start.21 = (f32[4,104,256]{2,1,0:T(8,128)S(1)}, f32[4,104,256]{2,1,0:T(8,128)S(1)}, u32[]{:S(2)}, u32[]{:S(2)}) collective-permute-start(f32[4,104,256]{2,1,0:T(8,128)S(1)} %shard_map.45.own_ref), channel_id=1, source_target_pairs={{0,16},{16,0},{32,48},{48,32},{64,80},{80,64},{96,112},{112,96},{1... | collective-permute-start | bytes 1277960 | tf_op jit(solution)/shard_map/ppermute | solution.py:14
  106.8 1.4 %collective-permute-done.21.other_ref = f32[4,104,256]{2,1,0:T(8,128)S(1)} collective-permute-done((f32[4,104,256]{2,1,0:T(8,128)S(1)}, f32[4,104,256]{2,1,0:T(8,128)S(1)}, u32[]{:S(2)}, u32[]{:S(2)}) %collective-permute-start.21) | collective-permute-done | bytes 426016 | tf_op jit(solution)/shard_map/ppermute | solution.py:14
  108.2 9.9 %shard_map.46.inv_ref = f32[256,256]{1,0:T(8,128)S(1)} custom-call(s32[1]{0:T(128)} %bitcast.2.core_ref, f32[4,104,256]{2,1,0:T(8,128)S(1)} %shard_map.45.own_ref, f32[4,104,256]{2,1,0:T(8,128)S(1)} %collective-permute-done.21.other_ref, f32[1,256]{1,0:T(1,128)S(1)} %bitcast.18), custom_call_target="tpu_custom_call" | custom-call | flops 1342177280 | bytes 786432 | tf_op jit(solution)/shard_map/pallas_call | solution.py:320
  118.5 3.9 %shard_map.48 = f32[576,1152]{1,0:T(8,128)} custom-call(f32[576,1152]{1,0:T(8,128)S(1)} %shard_map.37.cov_ref, f32[1152,256]{1,0:T(8,128)} %bitcast.9.rows_ref, f32[576,256]{1,0:T(8,128)S(1)} %shard_map.47.gain_ref), custom_call_target="tpu_custom_call" | custom-call | flops 1019215872 | bytes 2654208 | tf_op jit(solution)/shard_map/pallas_call | solution.py:206
  (36 shorter events, 10.1 us)
Async XLA Ops:
  0.8 9.9 %collective-permute-start = (f32[72,256]{1,0:T(8,128)S(1)}, f32[72,256]{1,0:T(8,128)S(1)}, u32[]{:S(2)}, u32[]{:S(2)}) collective-permute-start(f32[72,256]{1,0:T(8,128)S(1)} %shard_map.38), channel_id=1, source_target_pairs={{0,0},{1,32},{2,64},{3,96},{4,16},{5,48},{6,80},{7,112},{8,1},{9,3... | collective-permute-start | bytes 221192 | tf_op jit(solution)/shard_map/ppermute | solution.py:18
  10.7 11.2 %collective-permute-start.1 = (f32[72,256]{1,0:T(8,128)S(1)}, f32[72,256]{1,0:T(8,128)S(1)}, u32[]{:S(2)}, u32[]{:S(2)}) collective-permute-start(f32[72,256]{1,0:T(8,128)S(1)} %collective-permute-done), channel_id=1, source_target_pairs={{0,32},{16,48},{32,0},{48,16},{64,96},{80,112},{96,64},{112,80},{1... | collective-permute-start | bytes 221192 | tf_op jit(solution)/shard_map/ppermute | solution.py:14
  12.1 25.6 %all-to-all-start = ((f32[16,72,256]{2,1,0:T(8,128)}), f32[16,72,256]{2,1,0:T(8,128)}, u32[]{:S(2)}, u32[]{:S(2)}) async-start(f32[16,72,256]{2,1,0:T(8,128)} %broadcast_in_dim.4), calls=%async_computation | async-start | bytes 2359296 | tf_op jit(solution)/shard_map/all_to_all | solution.py:40
  21.9 5.3 %collective-permute-start.2 = (f32[2,72,256]{2,1,0:T(8,128)S(1)}, f32[2,72,256]{2,1,0:T(8,128)S(1)}, u32[]{:S(2)}, u32[]{:S(2)}) collective-permute-start(f32[2,72,256]{2,1,0:T(8,128)S(1)} %pad_maximum_fusion.1), channel_id=1, source_target_pairs={{0,96},{16,112},{32,64},{48,80},{64,32},{80,48},{96,0},{112,16},{1... | collective-permute-start | bytes 442376 | tf_op jit(solution)/shard_map/ppermute | solution.py:14
  27.3 5.7 %collective-permute-start.3 = (f32[288,256]{1,0:T(8,128)S(1)}, f32[288,256]{1,0:T(8,128)S(1)}, u32[]{:S(2)}, u32[]{:S(2)}) collective-permute-start(f32[288,256]{1,0:T(8,128)S(1)} %bitcast.16), channel_id=1, source_target_pairs={{0,16},{16,0},{32,48},{48,32},{64,80},{80,64},{96,112},{112,96},{1... | collective-permute-start | bytes 884744 | tf_op jit(solution)/shard_map/ppermute | solution.py:14
  40.8 5.2 %collective-permute-start.4 = (f32[4,104,256]{2,1,0:T(8,128)S(1)}, f32[4,104,256]{2,1,0:T(8,128)S(1)}, u32[]{:S(2)}, u32[]{:S(2)}) collective-permute-start(f32[4,104,256]{2,1,0:T(8,128)S(1)} %get-tuple-element.16), channel_id=1, source_target_pairs={{0,16},{16,0},{32,48},{48,32},{64,80},{80,64},{96,112},{112,96},{1... | collective-permute-start | bytes 1277960 | tf_op jit(solution)/shard_map/ppermute | solution.py:14
  46.1 3.9 %collective-permute-start.5 = (f32[72,256]{1,0:T(8,128)S(1)}, f32[72,256]{1,0:T(8,128)S(1)}, u32[]{:S(2)}, u32[]{:S(2)}) collective-permute-start(f32[72,256]{1,0:T(8,128)S(1)} %get-tuple-element.18), channel_id=1, source_target_pairs={{0,32},{16,48},{32,0},{48,16},{64,96},{80,112},{96,64},{112,80},{1... | collective-permute-start | bytes 221192 | tf_op jit(solution)/shard_map/ppermute | solution.py:14
  46.8 5.7 %collective-permute-start.6 = (f32[72,256]{1,0:T(8,128)S(1)}, f32[72,256]{1,0:T(8,128)S(1)}, u32[]{:S(2)}, u32[]{:S(2)}) collective-permute-start(f32[72,256]{1,0:T(8,128)S(1)} %get-tuple-element.19), channel_id=1, source_target_pairs={{0,64},{16,80},{32,96},{48,112},{64,0},{80,16},{96,32},{112,48},{1... | collective-permute-start | bytes 221192 | tf_op jit(solution)/shard_map/ppermute | solution.py:14
  48.7 4.9 %collective-permute-start.7 = (f32[72,256]{1,0:T(8,128)S(1)}, f32[72,256]{1,0:T(8,128)S(1)}, u32[]{:S(2)}, u32[]{:S(2)}) collective-permute-start(f32[72,256]{1,0:T(8,128)S(1)} %get-tuple-element.20), channel_id=1, source_target_pairs={{0,96},{16,112},{32,64},{48,80},{64,32},{80,48},{96,0},{112,16},{1... | collective-permute-start | bytes 221192 | tf_op jit(solution)/shard_map/ppermute | solution.py:14
  53.7 7.2 %collective-permute-start.8 = (f32[72,256]{1,0:T(8,128)S(1)}, f32[72,256]{1,0:T(8,128)S(1)}, u32[]{:S(2)}, u32[]{:S(2)}) collective-permute-start(f32[72,256]{1,0:T(8,128)S(1)} %shard_map.41.product_ref), channel_id=1, source_target_pairs={{0,0},{1,8},{2,16},{3,24},{4,32},{5,40},{6,48},{7,56},{8,64},{9,72... | collective-permute-start | bytes 221192 | tf_op jit(solution)/shard_map/ppermute | solution.py:18
  61.9 56.6 %all-to-all-start.1 = ((f32[16,72,256]{2,1,0:T(8,128)}), f32[16,72,256]{2,1,0:T(8,128)}, u32[]{:S(2)}, u32[]{:S(2)}) async-start(f32[16,72,256]{2,1,0:T(8,128)} %broadcast_in_dim.5), calls=%async_computation.1 | async-start | bytes 2359296 | tf_op jit(solution)/shard_map/all_to_all | solution.py:40
  69.3 38.8 %copy-start = (f32[2,128]{1,0:T(2,128)S(1)}, f32[2,128]{1,0:T(2,128)}, u32[]{:S(2)}) copy-start(f32[2,128]{1,0:T(2,128)} %param.5) | copy-start | bytes 3076
  69.4 4.6 %collective-permute-start.9 = (f32[32,256]{1,0:T(8,128)S(1)}, f32[32,256]{1,0:T(8,128)S(1)}, u32[]{:S(2)}, u32[]{:S(2)}) collective-permute-start(f32[32,256]{1,0:T(8,128)S(1)} %get-tuple-element.22), channel_id=1, source_target_pairs={{0,32},{16,48},{32,0},{48,16},{64,96},{80,112},{96,64},{112,80},{1... | collective-permute-start | bytes 98312 | tf_op jit(solution)/shard_map/ppermute | solution.py:14
  69.4 6.4 %collective-permute-start.10 = (f32[32,256]{1,0:T(8,128)S(1)}, f32[32,256]{1,0:T(8,128)S(1)}, u32[]{:S(2)}, u32[]{:S(2)}) collective-permute-start(f32[32,256]{1,0:T(8,128)S(1)} %get-tuple-element.23), channel_id=1, source_target_pairs={{0,64},{16,80},{32,96},{48,112},{64,0},{80,16},{96,32},{112,48},{1... | collective-permute-start | bytes 98312 | tf_op jit(solution)/shard_map/ppermute | solution.py:14
  74.0 4.4 %collective-permute-start.11 = (f32[32,256]{1,0:T(8,128)S(1)}, f32[32,256]{1,0:T(8,128)S(1)}, u32[]{:S(2)}, u32[]{:S(2)}) collective-permute-start(f32[32,256]{1,0:T(8,128)S(1)} %get-tuple-element.24), channel_id=1, source_target_pairs={{0,96},{16,112},{32,64},{48,80},{64,32},{80,48},{96,0},{112,16},{1... | collective-permute-start | bytes 98312 | tf_op jit(solution)/shard_map/ppermute | solution.py:14
  78.3 9.7 %collective-permute-start.14 = (f32[32,256]{1,0:T(8,128)S(1)}, f32[32,256]{1,0:T(8,128)S(1)}, u32[]{:S(2)}, u32[]{:S(2)}) collective-permute-start(f32[32,256]{1,0:T(8,128)S(1)} %shard_map.42.a_ref), channel_id=1, source_target_pairs={{0,3},{1,2},{2,1},{3,0},{4,7},{5,6},{6,5},{7,4},{8,11},{9,10},{10,... | collective-permute-start | bytes 98312 | tf_op jit(solution)/shard_map/ppermute | solution.py:14
  80.4 8.5 %collective-permute-start.13 = (f32[32,256]{1,0:T(8,128)S(1)}, f32[32,256]{1,0:T(8,128)S(1)}, u32[]{:S(2)}, u32[]{:S(2)}) collective-permute-start(f32[32,256]{1,0:T(8,128)S(1)} %shard_map.42.a_ref), channel_id=1, source_target_pairs={{0,2},{1,3},{2,0},{3,1},{4,6},{5,7},{6,4},{7,5},{8,10},{9,11},{10,... | collective-permute-start | bytes 98312 | tf_op jit(solution)/shard_map/ppermute | solution.py:14
  81.4 7.5 %collective-permute-start.12 = (f32[32,256]{1,0:T(8,128)S(1)}, f32[32,256]{1,0:T(8,128)S(1)}, u32[]{:S(2)}, u32[]{:S(2)}) collective-permute-start(f32[32,256]{1,0:T(8,128)S(1)} %shard_map.42.a_ref), channel_id=1, source_target_pairs={{0,1},{1,0},{2,3},{3,2},{4,5},{5,4},{6,7},{7,6},{8,9},{9,8},{10,11... | collective-permute-start | bytes 98312 | tf_op jit(solution)/shard_map/ppermute | solution.py:14
  89.0 4.1 %collective-permute-start.17 = (f32[32,256]{1,0:T(8,128)S(1)}, f32[32,256]{1,0:T(8,128)S(1)}, u32[]{:S(2)}, u32[]{:S(2)}) collective-permute-start(f32[32,256]{1,0:T(8,128)S(1)} %shard_map.43.a_ref), channel_id=1, source_target_pairs={{0,12},{1,13},{2,14},{3,15},{4,8},{5,9},{6,10},{7,11},{8,4},{9,5},... | collective-permute-start | bytes 98312 | tf_op jit(solution)/shard_map/ppermute | solution.py:14
  89.6 4.3 %collective-permute-start.16 = (f32[32,256]{1,0:T(8,128)S(1)}, f32[32,256]{1,0:T(8,128)S(1)}, u32[]{:S(2)}, u32[]{:S(2)}) collective-permute-start(f32[32,256]{1,0:T(8,128)S(1)} %shard_map.43.a_ref), channel_id=1, source_target_pairs={{0,8},{1,9},{2,10},{3,11},{4,12},{5,13},{6,14},{7,15},{8,0},{9,1},... | collective-permute-start | bytes 98312 | tf_op jit(solution)/shard_map/ppermute | solution.py:14
  90.4 3.8 %collective-permute-start.15 = (f32[32,256]{1,0:T(8,128)S(1)}, f32[32,256]{1,0:T(8,128)S(1)}, u32[]{:S(2)}, u32[]{:S(2)}) collective-permute-start(f32[32,256]{1,0:T(8,128)S(1)} %shard_map.43.a_ref), channel_id=1, source_target_pairs={{0,4},{1,5},{2,6},{3,7},{4,0},{5,1},{6,2},{7,3},{8,12},{9,13},{10,... | collective-permute-start | bytes 98312 | tf_op jit(solution)/shard_map/ppermute | solution.py:14
  94.3 5.2 %collective-permute-start.20 = (f32[104,256]{1,0:T(8,128)S(1)}, f32[104,256]{1,0:T(8,128)S(1)}, u32[]{:S(2)}, u32[]{:S(2)}) collective-permute-start(f32[104,256]{1,0:T(8,128)S(1)} %shard_map.44.refs_0_), channel_id=1, source_target_pairs={{0,96},{16,112},{32,64},{48,80},{64,32},{80,48},{96,0},{112,16},{1... | collective-permute-start | bytes 319496 | tf_op jit(solution)/shard_map/ppermute | solution.py:14
  96.7 5.1 %collective-permute-start.19 = (f32[104,256]{1,0:T(8,128)S(1)}, f32[104,256]{1,0:T(8,128)S(1)}, u32[]{:S(2)}, u32[]{:S(2)}) collective-permute-start(f32[104,256]{1,0:T(8,128)S(1)} %shard_map.44.refs_0_), channel_id=1, source_target_pairs={{0,64},{16,80},{32,96},{48,112},{64,0},{80,16},{96,32},{112,48},{1... | collective-permute-start | bytes 319496 | tf_op jit(solution)/shard_map/ppermute | solution.py:14
  96.7 5.1 %collective-permute-start.18 = (f32[104,256]{1,0:T(8,128)S(1)}, f32[104,256]{1,0:T(8,128)S(1)}, u32[]{:S(2)}, u32[]{:S(2)}) collective-permute-start(f32[104,256]{1,0:T(8,128)S(1)} %shard_map.44.refs_0_), channel_id=1, source_target_pairs={{0,32},{16,48},{32,0},{48,16},{64,96},{80,112},{96,64},{112,80},{1... | collective-permute-start | bytes 319496 | tf_op jit(solution)/shard_map/ppermute | solution.py:14
  101.8 6.4 %collective-permute-start.21 = (f32[4,104,256]{2,1,0:T(8,128)S(1)}, f32[4,104,256]{2,1,0:T(8,128)S(1)}, u32[]{:S(2)}, u32[]{:S(2)}) collective-permute-start(f32[4,104,256]{2,1,0:T(8,128)S(1)} %shard_map.45.own_ref), channel_id=1, source_target_pairs={{0,16},{16,0},{32,48},{48,32},{64,80},{80,64},{96,112},{112,96},{1... | collective-permute-start | bytes 1277960 | tf_op jit(solution)/shard_map/ppermute | solution.py:14

commit v5 on v4

--- a/solution.py
+++ b/solution.py
@@ -55,20 +55,27 @@
     return one(ah, bh) + (one(ah, bl) + one(al, bh))
 
 
-def products_kernel(core_ref, cov_ref, rows_ref, own_ref, other_ref, kept_ref, given_ref, t_ref, m_ref, cols_ref):
+def products_kernel(core_ref, cov_ref, rows_ref, kept_ref, given_ref, t_ref):
     core = core_ref[0]
-    block, share = t_ref.shape[0] // 8, m_ref.shape[0] // 8
+    block = t_ref.shape[0] // 8
     cut = 2 * block
     right = halves(rows_ref[...])
-    cols_ref[pl.ds(pl.multiple_of(core * 4 * block, 8), 4 * block), :] = own_ref[...]
-    cols_ref[pl.ds(pl.multiple_of((1 - core) * 4 * block, 8), 4 * block), :] = other_ref[...]
     for i in range(4):
         t_ref[pl.ds(i * cut, cut), :] = near_full(halves(cov_ref[pl.ds(i * cut, cut), :]), right, ((1,), (0,)))
-    m_ref[...] = near_full(halves(cols_ref[...]), halves(t_ref[...]), ((0,), (0,)))
     for ref, at in ((kept_ref, core), (given_ref, 1 - core)):
         for i in range(4):
-            ref[i, :block, :] = t_ref[pl.ds(pl.multiple_of((4 * at + i) * block, 8), block), :]
-            ref[i, block:, :] = m_ref[pl.ds(pl.multiple_of((4 * at + i) * share, 8), share), :]
+            ref[i] = t_ref[pl.ds(pl.multiple_of((4 * at + i) * block, 8), block), :]
+
+
+def inner_kernel(core_ref, kept_ref, given_ref, own_ref, other_ref, kept_out_ref, given_out_ref, m_ref):
+    share = m_ref.shape[0] // 8
+    first = ((0,), (0,))
+    m_ref[...] = near_full(halves(own_ref[...]), halves(kept_ref[...]), first) + near_full(
+        halves(other_ref[...]), halves(given_ref[...]), first
+    )
+    for ref, at in ((kept_out_ref, core_ref[0]), (given_out_ref, 1 - core_ref[0])):
+        for i in range(4):
+            ref[i] = m_ref[pl.ds(pl.multiple_of((4 * at + i) * share, 8), share), :]
 
 
 SCALAR = pl.BlockSpec(memory_space=pltpu.SMEM)
@@ -76,47 +83,53 @@
 FAR = pl.BlockSpec(memory_space=pltpu.HBM)
 
 
-def products(core, cov, rows, own, other):
-    n, width = 2 * own.shape[0], own.shape[1]
-    depth = n // 8 + width // 8
-    exchange = pltpu.VMEM((4, depth, width), jnp.float32)
+def products(core, cov, rows):
+    n, width = cov.shape[0], rows.shape[1]
+    exchange = pltpu.VMEM((4, n // 8, width), jnp.float32)
     return pl.pallas_call(
         products_kernel,
         out_shape=(exchange, exchange),
-        in_specs=[SCALAR, VMEM, VMEM, VMEM, VMEM],
+        in_specs=[SCALAR, VMEM, VMEM],
         out_specs=(VMEM, VMEM),
-        scratch_shapes=[
-            pltpu.VMEM((n, width), jnp.float32),
-            pltpu.VMEM((width, width), jnp.float32),
-            pltpu.VMEM((n, width), jnp.float32),
-        ],
+        scratch_shapes=[pltpu.VMEM((n, width), jnp.float32)],
         cost_estimate=pl.CostEstimate(
-            flops=6 * n * width * (rows.shape[0] + width), bytes_accessed=4 * cov.size, transcendentals=0
+            flops=6 * n * width * rows.shape[0], bytes_accessed=4 * cov.size, transcendentals=0
         ),
         compiler_params=pltpu.CompilerParams(vmem_limit_bytes=20 << 20),
-    )(core.reshape(1), cov, pltpu.with_memory_space_constraint(rows, pltpu.VMEM), own, other)
+    )(core.reshape(1), cov, rows)
+
+
+def inner_of(core, kept, given, own, other):
+    width = own.shape[1]
+    exchange = pltpu.VMEM((4, width // 8, width), jnp.float32)
+    tall = (own.shape[0], width)
+    return pl.pallas_call(
+        inner_kernel,
+        out_shape=(exchange, exchange),
+        in_specs=[SCALAR] + [VMEM] * 4,
+        out_specs=(VMEM, VMEM),
+        scratch_shapes=[pltpu.VMEM((width, width), jnp.float32)],
+        cost_estimate=pl.CostEstimate(
+            flops=12 * own.size * width, bytes_accessed=16 * own.size, transcendentals=0
+        ),
+        compiler_params=pltpu.CompilerParams(vmem_limit_bytes=10 << 20),
+    )(core.reshape(1), kept.reshape(tall), given.reshape(tall), own, other)
 
 
 def pieces_kernel(z_ref, kept_ref, mate_ref, *out_refs):
-    block = out_refs[0].shape[0]
-    for d in range(4):
+    for d, ref in enumerate(out_refs):
         at = z_ref[0] ^ d
-        out_refs[d][...] = kept_ref[at, :block, :] + mate_ref[at, :block, :]
-        out_refs[4 + d][...] = kept_ref[at, block:, :] + mate_ref[at, block:, :]
-
-
-def pieces(z, kept, mate, block):
-    _, depth, width = kept.shape
-    product = pltpu.VMEM((block, width), jnp.float32)
-    share = pltpu.VMEM((depth - block, width), jnp.float32)
-    out = pl.pallas_call(
+        ref[...] = kept_ref[at] + mate_ref[at]
+
+
+def pieces(z, kept, mate):
+    return pl.pallas_call(
         pieces_kernel,
-        out_shape=(product,) * 4 + (share,) * 4,
+        out_shape=(pltpu.VMEM(kept.shape[1:], jnp.float32),) * 4,
         in_specs=[SCALAR, VMEM, VMEM],
-        out_specs=(VMEM,) * 8,
+        out_specs=(VMEM,) * 4,
         compiler_params=pltpu.CompilerParams(vmem_limit_bytes=4 << 20),
     )(z.reshape(1), kept, mate)
-    return out[:4], out[4:]
 
 
 def total_kernel(a_ref, b_ref, c_ref, d_ref, out_ref):
@@ -342,8 +355,10 @@
     zb = side(za, to_xor(za, "row", 6), z >> 1)
     quad = zb.reshape(4 * block, width)
 
-    kept, given = products(core, turned, row_features, quad, to_xor(quad, "row", 1))
-    terms, shares = pieces(z, kept, to_xor(given, "row", 1), block)
+    kept, given = products(core, turned, row_features)
+    terms = pieces(z, kept, to_xor(given, "row", 1))
+    kept_inner, given_inner = inner_of(core, kept, given, quad, to_xor(quad, "row", 1))
+    shares = pieces(z, kept_inner, to_xor(given_inner, "row", 1))
     share = total_of([shares[0]] + [to_xor(shares[d], "row", 2 * d) for d in (1, 2, 3)])
     product = total_of([terms[0]] + [to_xor(terms[d], "row", 2 * d) for d in (1, 2, 3)])
 

time: 123 us -> 126 us (1.024)
  waiting for transfers between devices: 41 us -> 34.5 us
  starting transfers between devices: 59 us -> 62.7 us
  other arithmetic: 0.09 us -> 3.29 us
    ppermute x20 -> x21, waiting for transfers between devices: 28.4 us -> 20.8 us  [to_xor(): return lax.ppermute(value, axis, [(i, i ^ bits) for i in range(size)])]
    ppermute x2, waiting for transfers between devices: 7.8 us -> 13.7 us  [to_place(): lax.ppermute(value, ('row', 'col'), [(i, owner(i)) for i in range(128)])]
    all_to_all x2, waiting for transfers between devices: 4.76 us -> 0.01 us  [to_plane(): lax.all_to_all(sent, 'col', 0, 0, tiled=True).reshape(-1, block.shape[-1])]
    another operation x4, other arithmetic: 0.09 us -> 3.29 us  [side(): return jnp.stack([first, second])]
    ppermute x20 -> x21, starting transfers between devices: 32.6 us -> 35.1 us  [to_xor(): return lax.ppermute(value, axis, [(i, i ^ bits) for i in range(size)])]
    ppermute x2, starting transfers between devices: 9.22 us -> 11.5 us  [to_place(): lax.ppermute(value, ('row', 'col'), [(i, owner(i)) for i in range(128)])]
    pallas_call x1 -> x3, Pallas kernels: 0.05 us -> 1.67 us  [the longest x1 1.61 us: inner_of(): pl.pallas_call(inner_kernel, out_shape=(exchange, exchange), in_specs=[SC...]
  transfers between devices with their start and end apart: 24 -> 25, of which waited for: 17 -> 16; matrix products, arithmetic and copies ran while one was open for 1% -> 4% of each run, Pallas kernels for 10% -> 13%
where the time goes in v5:
time: 126 us; the launch traced here: 125 us
  starting transfers between devices  62.7 us (50%)
  waiting for transfers between devices  34.5 us (27%)
  Pallas kernels  21.1 us (17%)
  other arithmetic  3.29 us (3%)
  local copies, waits for them, and re-layouts  3.14 us (2%)
    ppermute x21, starting transfers between devices, to_xor(): return lax.ppermute(value, axis, [(i, i ^ bits) for i in range(size)])  35.1 us
    ppermute x21, waiting for transfers between devices, to_xor(): return lax.ppermute(value, axis, [(i, i ^ bits) for i in range(size)])  20.8 us
    all_to_all x2, starting transfers between devices, to_plane(): lax.all_to_all(sent, 'col', 0, 0, tiled=True).reshape(-1, block.shape[-1])  16.1 us
    ppermute x2, waiting for transfers between devices, to_place(): lax.ppermute(value, ('row', 'col'), [(i, owner(i)) for i in range(128)])  13.7 us
    ppermute x2, starting transfers between devices, to_place(): lax.ppermute(value, ('row', 'col'), [(i, owner(i)) for i in range(128)])  11.5 us
    pallas_call x1, Pallas kernels, inverse_of(): pl.pallas_call(invert_kernel, out_shape=pltpu.VMEM((n, n), jnp.float32),...  9.88 us
    pallas_call x1, Pallas kernels, update(): pl.pallas_call(update_kernel, out_shape=pltpu.HBM(cov.shape, jnp.float32)...  3.91 us
    another operation x4, other arithmetic, side(): return jnp.stack([first, second])  3.29 us
  transfers between devices with their start and end apart: 25, of which 16 were waited for; matrix products, arithmetic and copies ran while one was open for 4% of the time, Pallas kernels for 13%

profile of v5, /device:TPU:1, one launch (start us, length us, event | category | flops | bytes accessed | tf_op | source)
XLA Modules:
  0.0 124.9 jit_solution(4666778031405627516)
XLA Ops:
  1.9 7.6 %all-to-all-start = ((f32[16,72,256]{2,1,0:T(8,128)}), f32[16,72,256]{2,1,0:T(8,128)}, u32[]{:S(2)}, u32[]{:S(2)}) async-start(f32[16,72,256]{2,1,0:T(8,128)} %broadcast_in_dim.4), calls=%async_computation | async-start | bytes 2359296 | tf_op jit(solution)/shard_map/all_to_all | solution.py:40
  9.5 5.8 %collective-permute-start.5 = (f32[72,256]{1,0:T(8,128)S(1)}, f32[72,256]{1,0:T(8,128)S(1)}, u32[]{:S(2)}, u32[]{:S(2)}) collective-permute-start(f32[72,256]{1,0:T(8,128)S(1)} %shard_map.38), channel_id=1, source_target_pairs={{0,0},{1,32},{2,64},{3,96},{4,16},{5,48},{6,80},{7,112},{8,1},{9,3... | collective-permute-start | bytes 221192 | tf_op jit(solution)/shard_map/ppermute | solution.py:18
  15.4 11.3 %collective-permute-done.5 = f32[72,256]{1,0:T(8,128)S(1)} collective-permute-done((f32[72,256]{1,0:T(8,128)S(1)}, f32[72,256]{1,0:T(8,128)S(1)}, u32[]{:S(2)}, u32[]{:S(2)}) %collective-permute-start.5) | collective-permute-done | bytes 73760 | tf_op jit(solution)/shard_map/ppermute | solution.py:18
  26.7 2.8 %collective-permute-start.6 = (f32[72,256]{1,0:T(8,128)S(1)}, f32[72,256]{1,0:T(8,128)S(1)}, u32[]{:S(2)}, u32[]{:S(2)}) collective-permute-start(f32[72,256]{1,0:T(8,128)S(1)} %collective-permute-done.5), channel_id=1, source_target_pairs={{0,32},{16,48},{32,0},{48,16},{64,96},{80,112},{96,64},{112,80},{1... | collective-permute-start | bytes 221192 | tf_op jit(solution)/shard_map/ppermute | solution.py:14
  29.6 1.7 %shard_map.37.cov_ref = f32[576,1152]{1,0:T(8,128)S(1)} custom-call(f32[576,1152]{1,0:T(8,128)} %bitcast.23), custom_call_target="tpu_custom_call" | custom-call | tf_op jit(solution)/shard_map/pallas_call | solution.py:265
  32.5 1.6 %pad_maximum_fusion.1 = f32[2,72,256]{2,1,0:T(8,128)} fusion(f32[1,72,256]{2,1,0:T(8,128)} %get-tuple-element.32, f32[1,72,256]{2,1,0:T(8,128)} %get-tuple-element.31), kind=kLoop, calls=%fused_computation.1 | loop fusion | flops 36864 | bytes 294912 | tf_op jit(solution)/shard_map/stack | solution.py:24
  34.1 3.7 %collective-permute-start.7 = (f32[2,72,256]{2,1,0:T(8,128)}, f32[2,72,256]{2,1,0:T(8,128)}, u32[]{:S(2)}, u32[]{:S(2)}) collective-permute-start(f32[2,72,256]{2,1,0:T(8,128)} %pad_maximum_fusion.1), channel_id=1, source_target_pairs={{0,96},{16,112},{32,64},{48,80},{64,32},{80,48},{96,0},{112,16},{1... | collective-permute-start | bytes 442376 | tf_op jit(solution)/shard_map/ppermute | solution.py:14
  37.8 2.6 %shard_map.39 = (f32[4,72,256]{2,1,0:T(8,128)S(1)}, f32[4,72,256]{2,1,0:T(8,128)S(1)}) custom-call(s32[1]{0:T(128)} %bitcast.2.core_ref, f32[576,1152]{1,0:T(8,128)S(1)} %shard_map.37.cov_ref, f32[1152,256]{1,0:T(8,128)} %bitcast.3.rows_ref), custom_call_target="tpu_custom_call" | custom-call | flops 1019215872 | bytes 2654208 | tf_op jit(solution)/shard_map/pallas_call | solution.py:89
  40.5 1.6 %collective-permute-done.7 = f32[2,72,256]{2,1,0:T(8,128)} collective-permute-done((f32[2,72,256]{2,1,0:T(8,128)}, f32[2,72,256]{2,1,0:T(8,128)}, u32[]{:S(2)}, u32[]{:S(2)}) %collective-permute-start.7) | collective-permute-done | bytes 147488 | tf_op jit(solution)/shard_map/ppermute | solution.py:14
  44.2 2.4 %collective-permute-start.2 = (f32[72,256]{1,0:T(8,128)S(1)}, f32[72,256]{1,0:T(8,128)S(1)}, u32[]{:S(2)}, u32[]{:S(2)}) collective-permute-start(f32[72,256]{1,0:T(8,128)S(1)} %get-tuple-element.21), channel_id=1, source_target_pairs={{0,64},{16,80},{32,96},{48,112},{64,0},{80,16},{96,32},{112,48},{1... | collective-permute-start | bytes 221192 | tf_op jit(solution)/shard_map/ppermute | solution.py:14
  47.1 1.7 %collective-permute-start.8 = (f32[288,256]{1,0:T(8,128)S(1)}, f32[288,256]{1,0:T(8,128)}, u32[]{:S(2)}, u32[]{:S(2)}) collective-permute-start(f32[288,256]{1,0:T(8,128)S(1)} %bitcast.18), channel_id=1, source_target_pairs={{0,16},{16,0},{32,48},{48,32},{64,80},{80,64},{96,112},{112,96},{1... | collective-permute-start | bytes 884744 | tf_op jit(solution)/shard_map/ppermute | solution.py:14
  48.8 1.6 %collective-permute-done.2.c_ref = f32[72,256]{1,0:T(8,128)S(1)} collective-permute-done((f32[72,256]{1,0:T(8,128)S(1)}, f32[72,256]{1,0:T(8,128)S(1)}, u32[]{:S(2)}, u32[]{:S(2)}) %collective-permute-start.2) | collective-permute-done | bytes 73760 | tf_op jit(solution)/shard_map/ppermute | solution.py:14
  50.5 1.5 %collective-permute-done.3.d_ref = f32[72,256]{1,0:T(8,128)S(1)} collective-permute-done((f32[72,256]{1,0:T(8,128)S(1)}, f32[72,256]{1,0:T(8,128)S(1)}, u32[]{:S(2)}, u32[]{:S(2)}) %collective-permute-start.3) | collective-permute-done | bytes 73760 | tf_op jit(solution)/shard_map/ppermute | solution.py:14
  52.0 5.6 %collective-permute-start.4 = (f32[72,256]{1,0:T(8,128)S(1)}, f32[72,256]{1,0:T(8,128)S(1)}, u32[]{:S(2)}, u32[]{:S(2)}) collective-permute-start(f32[72,256]{1,0:T(8,128)S(1)} %shard_map.41.product_ref), channel_id=1, source_target_pairs={{0,0},{1,8},{2,16},{3,24},{4,32},{5,40},{6,48},{7,56},{8,64},{9,72... | collective-permute-start | bytes 221192 | tf_op jit(solution)/shard_map/ppermute | solution.py:18
  57.6 2.3 %collective-permute-done.4 = f32[72,256]{1,0:T(8,128)S(1)} collective-permute-done((f32[72,256]{1,0:T(8,128)S(1)}, f32[72,256]{1,0:T(8,128)S(1)}, u32[]{:S(2)}, u32[]{:S(2)}) %collective-permute-start.4) | collective-permute-done | bytes 73760 | tf_op jit(solution)/shard_map/ppermute | solution.py:18
  61.0 8.5 %all-to-all-start.1 = ((f32[16,72,256]{2,1,0:T(8,128)}), f32[16,72,256]{2,1,0:T(8,128)}, u32[]{:S(2)}, u32[]{:S(2)}) async-start(f32[16,72,256]{2,1,0:T(8,128)} %broadcast_in_dim.5), calls=%async_computation.1 | async-start | bytes 2359296 | tf_op jit(solution)/shard_map/all_to_all | solution.py:40
  70.5 1.6 %shard_map.42 = (f32[4,32,256]{2,1,0:T(8,128)S(1)}, f32[4,32,256]{2,1,0:T(8,128)S(1)}) custom-call(s32[1]{0:T(128)} %bitcast.2.core_ref, f32[288,256]{1,0:T(8,128)S(1)} %bitcast.20, f32[288,256]{1,0:T(8,128)S(1)} %bitcast.21, f32[288,256]{1,0:T(8,128)S(1)} %bitcast.19, f32[288,256]{1,0:T(8,128)} %collective-permute-done.8.other_ref), custom_call_target="tpu_custom_call" | custom-call | flops 226492416 | bytes 1179648 | tf_op jit(solution)/shard_map/pallas_call | solution.py:106
  72.2 2.6 %collective-permute-start.9 = (f32[4,32,256]{2,1,0:T(8,128)S(1)}, f32[4,32,256]{2,1,0:T(8,128)S(1)}, u32[]{:S(2)}, u32[]{:S(2)}) collective-permute-start(f32[4,32,256]{2,1,0:T(8,128)S(1)} %get-tuple-element.24), channel_id=1, source_target_pairs={{0,16},{16,0},{32,48},{48,32},{64,80},{80,64},{96,112},{112,96},{1... | collective-permute-start | bytes 393224 | tf_op jit(solution)/shard_map/ppermute | solution.py:14
  75.9 1.2 collective-permute-start.11
  77.1 2.6 %collective-permute-start.12 = (f32[32,256]{1,0:T(8,128)S(1)}, f32[32,256]{1,0:T(8,128)S(1)}, u32[]{:S(2)}, u32[]{:S(2)}) collective-permute-start(f32[32,256]{1,0:T(8,128)S(1)} %get-tuple-element.28), channel_id=1, source_target_pairs={{0,96},{16,112},{32,64},{48,80},{64,32},{80,48},{96,0},{112,16},{1... | collective-permute-start | bytes 98312 | tf_op jit(solution)/shard_map/ppermute | solution.py:14
  80.6 1.2 collective-permute-done.12.d_ref
  81.9 2.9 %collective-permute-start.15 = (f32[32,256]{1,0:T(8,128)S(1)}, f32[32,256]{1,0:T(8,128)S(1)}, u32[]{:S(2)}, u32[]{:S(2)}) collective-permute-start(f32[32,256]{1,0:T(8,128)S(1)} %shard_map.44.a_ref), channel_id=1, source_target_pairs={{0,3},{1,2},{2,1},{3,0},{4,7},{5,6},{6,5},{7,4},{8,11},{9,10},{10,... | collective-permute-start | bytes 98312 | tf_op jit(solution)/shard_map/ppermute | solution.py:14
  85.4 3.3 %collective-permute-done.15.d_ref = f32[32,256]{1,0:T(8,128)S(1)} collective-permute-done((f32[32,256]{1,0:T(8,128)S(1)}, f32[32,256]{1,0:T(8,128)S(1)}, u32[]{:S(2)}, u32[]{:S(2)}) %collective-permute-start.15) | collective-permute-done | bytes 32800 | tf_op jit(solution)/shard_map/ppermute | solution.py:14
  89.0 2.5 %collective-permute-start.18 = (f32[32,256]{1,0:T(8,128)S(1)}, f32[32,256]{1,0:T(8,128)S(1)}, u32[]{:S(2)}, u32[]{:S(2)}) collective-permute-start(f32[32,256]{1,0:T(8,128)S(1)} %shard_map.45.a_ref), channel_id=1, source_target_pairs={{0,12},{1,13},{2,14},{3,15},{4,8},{5,9},{6,10},{7,11},{8,4},{9,5},... | collective-permute-start | bytes 98312 | tf_op jit(solution)/shard_map/ppermute | solution.py:14
  93.1 2.7 %collective-permute-done.17.c_ref = f32[32,256]{1,0:T(8,128)S(1)} collective-permute-done((f32[32,256]{1,0:T(8,128)S(1)}, f32[32,256]{1,0:T(8,128)S(1)}, u32[]{:S(2)}, u32[]{:S(2)}) %collective-permute-start.17) | collective-permute-done | bytes 32800 | tf_op jit(solution)/shard_map/ppermute | solution.py:14
  95.8 2.3 %collective-permute-start.21 = (f32[104,256]{1,0:T(8,128)S(1)}, f32[104,256]{1,0:T(8,128)S(1)}, u32[]{:S(2)}, u32[]{:S(2)}) collective-permute-start(f32[104,256]{1,0:T(8,128)S(1)} %shard_map.46.refs_0_), channel_id=1, source_target_pairs={{0,96},{16,112},{32,64},{48,80},{64,32},{80,48},{96,0},{112,16},{1... | collective-permute-start | bytes 319496 | tf_op jit(solution)/shard_map/ppermute | solution.py:14
  99.1 1.8 %collective-permute-done.21.refs_3_ = f32[104,256]{1,0:T(8,128)S(1)} collective-permute-done((f32[104,256]{1,0:T(8,128)S(1)}, f32[104,256]{1,0:T(8,128)S(1)}, u32[]{:S(2)}, u32[]{:S(2)}) %collective-permute-start.21) | collective-permute-done | bytes 106528 | tf_op jit(solution)/shard_map/ppermute | solution.py:14
  100.9 2.3 %collective-permute-done.20.refs_2_ = f32[104,256]{1,0:T(8,128)S(1)} collective-permute-done((f32[104,256]{1,0:T(8,128)S(1)}, f32[104,256]{1,0:T(8,128)S(1)}, u32[]{:S(2)}, u32[]{:S(2)}) %collective-permute-start.20) | collective-permute-done | bytes 106528 | tf_op jit(solution)/shard_map/ppermute | solution.py:14
  103.2 6.0 %collective-permute-start.22 = (f32[4,104,256]{2,1,0:T(8,128)S(1)}, f32[4,104,256]{2,1,0:T(8,128)S(1)}, u32[]{:S(2)}, u32[]{:S(2)}) collective-permute-start(f32[4,104,256]{2,1,0:T(8,128)S(1)} %shard_map.47.own_ref), channel_id=1, source_target_pairs={{0,16},{16,0},{32,48},{48,32},{64,80},{80,64},{96,112},{112,96},{1... | collective-permute-start | bytes 1277960 | tf_op jit(solution)/shard_map/ppermute | solution.py:14
  109.3 1.4 %collective-permute-done.22.other_ref = f32[4,104,256]{2,1,0:T(8,128)S(1)} collective-permute-done((f32[4,104,256]{2,1,0:T(8,128)S(1)}, f32[4,104,256]{2,1,0:T(8,128)S(1)}, u32[]{:S(2)}, u32[]{:S(2)}) %collective-permute-start.22) | collective-permute-done | bytes 426016 | tf_op jit(solution)/shard_map/ppermute | solution.py:14
  110.7 9.9 %shard_map.48.inv_ref = f32[256,256]{1,0:T(8,128)S(1)} custom-call(s32[1]{0:T(128)} %bitcast.2.core_ref, f32[4,104,256]{2,1,0:T(8,128)S(1)} %shard_map.47.own_ref, f32[4,104,256]{2,1,0:T(8,128)S(1)} %collective-permute-done.22.other_ref, f32[1,256]{1,0:T(1,128)S(1)} %bitcast.22), custom_call_target="tpu_custom_call" | custom-call | flops 1342177280 | bytes 786432 | tf_op jit(solution)/shard_map/pallas_call | solution.py:333
  121.0 3.9 %shard_map.50 = f32[576,1152]{1,0:T(8,128)} custom-call(f32[576,1152]{1,0:T(8,128)S(1)} %shard_map.37.cov_ref, f32[1152,256]{1,0:T(8,128)} %bitcast.4.rows_ref, f32[576,256]{1,0:T(8,128)S(1)} %shard_map.49.gain_ref), custom_call_target="tpu_custom_call" | custom-call | flops 1019215872 | bytes 2654208 | tf_op jit(solution)/shard_map/pallas_call | solution.py:219
  (44 shorter events, 13.9 us)
Async XLA Ops:
  1.9 35.9 %all-to-all-start = ((f32[16,72,256]{2,1,0:T(8,128)}), f32[16,72,256]{2,1,0:T(8,128)}, u32[]{:S(2)}, u32[]{:S(2)}) async-start(f32[16,72,256]{2,1,0:T(8,128)} %broadcast_in_dim.4), calls=%async_computation | async-start | bytes 2359296 | tf_op jit(solution)/shard_map/all_to_all | solution.py:40
  9.5 17.2 %collective-permute-start.5 = (f32[72,256]{1,0:T(8,128)S(1)}, f32[72,256]{1,0:T(8,128)S(1)}, u32[]{:S(2)}, u32[]{:S(2)}) collective-permute-start(f32[72,256]{1,0:T(8,128)S(1)} %shard_map.38), channel_id=1, source_target_pairs={{0,0},{1,32},{2,64},{3,96},{4,16},{5,48},{6,80},{7,112},{8,1},{9,3... | collective-permute-start | bytes 221192 | tf_op jit(solution)/shard_map/ppermute | solution.py:18
  26.7 5.1 %collective-permute-start.6 = (f32[72,256]{1,0:T(8,128)S(1)}, f32[72,256]{1,0:T(8,128)S(1)}, u32[]{:S(2)}, u32[]{:S(2)}) collective-permute-start(f32[72,256]{1,0:T(8,128)S(1)} %collective-permute-done.5), channel_id=1, source_target_pairs={{0,32},{16,48},{32,0},{48,16},{64,96},{80,112},{96,64},{112,80},{1... | collective-permute-start | bytes 221192 | tf_op jit(solution)/shard_map/ppermute | solution.py:14
  34.1 8.0 %collective-permute-start.7 = (f32[2,72,256]{2,1,0:T(8,128)}, f32[2,72,256]{2,1,0:T(8,128)}, u32[]{:S(2)}, u32[]{:S(2)}) collective-permute-start(f32[2,72,256]{2,1,0:T(8,128)} %pad_maximum_fusion.1), channel_id=1, source_target_pairs={{0,96},{16,112},{32,64},{48,80},{64,32},{80,48},{96,0},{112,16},{1... | collective-permute-start | bytes 442376 | tf_op jit(solution)/shard_map/ppermute | solution.py:14
  40.4 11.6 %copy-start = (f32[4,72,256]{2,1,0:T(8,128)}, f32[4,72,256]{2,1,0:T(8,128)S(1)}, u32[]{:S(2)}) copy-start(f32[4,72,256]{2,1,0:T(8,128)S(1)} %get-tuple-element.18) | copy-start | bytes 884740
  40.4 2.7 %collective-permute-start = (f32[4,72,256]{2,1,0:T(8,128)S(1)}, f32[4,72,256]{2,1,0:T(8,128)S(1)}, u32[]{:S(2)}, u32[]{:S(2)}) collective-permute-start(f32[4,72,256]{2,1,0:T(8,128)S(1)} %get-tuple-element.18), channel_id=1, source_target_pairs={{0,16},{16,0},{32,48},{48,32},{64,80},{80,64},{96,112},{112,96},{1... | collective-permute-start | bytes 884744 | tf_op jit(solution)/shard_map/ppermute | solution.py:14
  43.2 5.7 %collective-permute-start.1 = (f32[72,256]{1,0:T(8,128)S(1)}, f32[72,256]{1,0:T(8,128)S(1)}, u32[]{:S(2)}, u32[]{:S(2)}) collective-permute-start(f32[72,256]{1,0:T(8,128)S(1)} %get-tuple-element.20), channel_id=1, source_target_pairs={{0,32},{16,48},{32,0},{48,16},{64,96},{80,112},{96,64},{112,80},{1... | collective-permute-start | bytes 221192 | tf_op jit(solution)/shard_map/ppermute | solution.py:14
  44.2 6.3 %collective-permute-start.2 = (f32[72,256]{1,0:T(8,128)S(1)}, f32[72,256]{1,0:T(8,128)S(1)}, u32[]{:S(2)}, u32[]{:S(2)}) collective-permute-start(f32[72,256]{1,0:T(8,128)S(1)} %get-tuple-element.21), channel_id=1, source_target_pairs={{0,64},{16,80},{32,96},{48,112},{64,0},{80,16},{96,32},{112,48},{1... | collective-permute-start | bytes 221192 | tf_op jit(solution)/shard_map/ppermute | solution.py:14
  46.6 5.4 %collective-permute-start.3 = (f32[72,256]{1,0:T(8,128)S(1)}, f32[72,256]{1,0:T(8,128)S(1)}, u32[]{:S(2)}, u32[]{:S(2)}) collective-permute-start(f32[72,256]{1,0:T(8,128)S(1)} %get-tuple-element.22), channel_id=1, source_target_pairs={{0,96},{16,112},{32,64},{48,80},{64,32},{80,48},{96,0},{112,16},{1... | collective-permute-start | bytes 221192 | tf_op jit(solution)/shard_map/ppermute | solution.py:14
  47.1 22.4 %collective-permute-start.8 = (f32[288,256]{1,0:T(8,128)S(1)}, f32[288,256]{1,0:T(8,128)}, u32[]{:S(2)}, u32[]{:S(2)}) collective-permute-start(f32[288,256]{1,0:T(8,128)S(1)} %bitcast.18), channel_id=1, source_target_pairs={{0,16},{16,0},{32,48},{48,32},{64,80},{80,64},{96,112},{112,96},{1... | collective-permute-start | bytes 884744 | tf_op jit(solution)/shard_map/ppermute | solution.py:14
  52.0 8.0 %collective-permute-start.4 = (f32[72,256]{1,0:T(8,128)S(1)}, f32[72,256]{1,0:T(8,128)S(1)}, u32[]{:S(2)}, u32[]{:S(2)}) collective-permute-start(f32[72,256]{1,0:T(8,128)S(1)} %shard_map.41.product_ref), channel_id=1, source_target_pairs={{0,0},{1,8},{2,16},{3,24},{4,32},{5,40},{6,48},{7,56},{8,64},{9,72... | collective-permute-start | bytes 221192 | tf_op jit(solution)/shard_map/ppermute | solution.py:18
  61.0 60.0 %all-to-all-start.1 = ((f32[16,72,256]{2,1,0:T(8,128)}), f32[16,72,256]{2,1,0:T(8,128)}, u32[]{:S(2)}, u32[]{:S(2)}) async-start(f32[16,72,256]{2,1,0:T(8,128)} %broadcast_in_dim.5), calls=%async_computation.1 | async-start | bytes 2359296 | tf_op jit(solution)/shard_map/all_to_all | solution.py:40
  69.6 1.0 copy-start.1
  70.5 40.2 %copy-start.2 = (f32[2,128]{1,0:T(2,128)S(1)}, f32[2,128]{1,0:T(2,128)}, u32[]{:S(2)}) copy-start(f32[2,128]{1,0:T(2,128)} %param.5) | copy-start | bytes 3076
  72.2 3.6 %collective-permute-start.9 = (f32[4,32,256]{2,1,0:T(8,128)S(1)}, f32[4,32,256]{2,1,0:T(8,128)S(1)}, u32[]{:S(2)}, u32[]{:S(2)}) collective-permute-start(f32[4,32,256]{2,1,0:T(8,128)S(1)} %get-tuple-element.24), channel_id=1, source_target_pairs={{0,16},{16,0},{32,48},{48,32},{64,80},{80,64},{96,112},{112,96},{1... | collective-permute-start | bytes 393224 | tf_op jit(solution)/shard_map/ppermute | solution.py:14
  75.8 3.9 %collective-permute-start.10 = (f32[32,256]{1,0:T(8,128)S(1)}, f32[32,256]{1,0:T(8,128)S(1)}, u32[]{:S(2)}, u32[]{:S(2)}) collective-permute-start(f32[32,256]{1,0:T(8,128)S(1)} %get-tuple-element.26), channel_id=1, source_target_pairs={{0,32},{16,48},{32,0},{48,16},{64,96},{80,112},{96,64},{112,80},{1... | collective-permute-start | bytes 98312 | tf_op jit(solution)/shard_map/ppermute | solution.py:14
  75.9 4.7 %collective-permute-start.11 = (f32[32,256]{1,0:T(8,128)S(1)}, f32[32,256]{1,0:T(8,128)S(1)}, u32[]{:S(2)}, u32[]{:S(2)}) collective-permute-start(f32[32,256]{1,0:T(8,128)S(1)} %get-tuple-element.27), channel_id=1, source_target_pairs={{0,64},{16,80},{32,96},{48,112},{64,0},{80,16},{96,32},{112,48},{1... | collective-permute-start | bytes 98312 | tf_op jit(solution)/shard_map/ppermute | solution.py:14
  77.1 4.7 %collective-permute-start.12 = (f32[32,256]{1,0:T(8,128)S(1)}, f32[32,256]{1,0:T(8,128)S(1)}, u32[]{:S(2)}, u32[]{:S(2)}) collective-permute-start(f32[32,256]{1,0:T(8,128)S(1)} %get-tuple-element.28), channel_id=1, source_target_pairs={{0,96},{16,112},{32,64},{48,80},{64,32},{80,48},{96,0},{112,16},{1... | collective-permute-start | bytes 98312 | tf_op jit(solution)/shard_map/ppermute | solution.py:14
  81.9 6.8 %collective-permute-start.15 = (f32[32,256]{1,0:T(8,128)S(1)}, f32[32,256]{1,0:T(8,128)S(1)}, u32[]{:S(2)}, u32[]{:S(2)}) collective-permute-start(f32[32,256]{1,0:T(8,128)S(1)} %shard_map.44.a_ref), channel_id=1, source_target_pairs={{0,3},{1,2},{2,1},{3,0},{4,7},{5,6},{6,5},{7,4},{8,11},{9,10},{10,... | collective-permute-start | bytes 98312 | tf_op jit(solution)/shard_map/ppermute | solution.py:14
  84.8 4.3 %collective-permute-start.14 = (f32[32,256]{1,0:T(8,128)S(1)}, f32[32,256]{1,0:T(8,128)S(1)}, u32[]{:S(2)}, u32[]{:S(2)}) collective-permute-start(f32[32,256]{1,0:T(8,128)S(1)} %shard_map.44.a_ref), channel_id=1, source_target_pairs={{0,2},{1,3},{2,0},{3,1},{4,6},{5,7},{6,4},{7,5},{8,10},{9,11},{10,... | collective-permute-start | bytes 98312 | tf_op jit(solution)/shard_map/ppermute | solution.py:14
  85.4 3.6 %collective-permute-start.13 = (f32[32,256]{1,0:T(8,128)S(1)}, f32[32,256]{1,0:T(8,128)S(1)}, u32[]{:S(2)}, u32[]{:S(2)}) collective-permute-start(f32[32,256]{1,0:T(8,128)S(1)} %shard_map.44.a_ref), channel_id=1, source_target_pairs={{0,1},{1,0},{2,3},{3,2},{4,5},{5,4},{6,7},{7,6},{8,9},{9,8},{10,11... | collective-permute-start | bytes 98312 | tf_op jit(solution)/shard_map/ppermute | solution.py:14
  89.0 4.1 %collective-permute-start.18 = (f32[32,256]{1,0:T(8,128)S(1)}, f32[32,256]{1,0:T(8,128)S(1)}, u32[]{:S(2)}, u32[]{:S(2)}) collective-permute-start(f32[32,256]{1,0:T(8,128)S(1)} %shard_map.45.a_ref), channel_id=1, source_target_pairs={{0,12},{1,13},{2,14},{3,15},{4,8},{5,9},{6,10},{7,11},{8,4},{9,5},... | collective-permute-start | bytes 98312 | tf_op jit(solution)/shard_map/ppermute | solution.py:14
  91.5 4.3 %collective-permute-start.17 = (f32[32,256]{1,0:T(8,128)S(1)}, f32[32,256]{1,0:T(8,128)S(1)}, u32[]{:S(2)}, u32[]{:S(2)}) collective-permute-start(f32[32,256]{1,0:T(8,128)S(1)} %shard_map.45.a_ref), channel_id=1, source_target_pairs={{0,8},{1,9},{2,10},{3,11},{4,12},{5,13},{6,14},{7,15},{8,0},{9,1},... | collective-permute-start | bytes 98312 | tf_op jit(solution)/shard_map/ppermute | solution.py:14
  92.1 3.7 %collective-permute-start.16 = (f32[32,256]{1,0:T(8,128)S(1)}, f32[32,256]{1,0:T(8,128)S(1)}, u32[]{:S(2)}, u32[]{:S(2)}) collective-permute-start(f32[32,256]{1,0:T(8,128)S(1)} %shard_map.45.a_ref), channel_id=1, source_target_pairs={{0,4},{1,5},{2,6},{3,7},{4,0},{5,1},{6,2},{7,3},{8,12},{9,13},{10,... | collective-permute-start | bytes 98312 | tf_op jit(solution)/shard_map/ppermute | solution.py:14
  95.8 5.1 %collective-permute-start.21 = (f32[104,256]{1,0:T(8,128)S(1)}, f32[104,256]{1,0:T(8,128)S(1)}, u32[]{:S(2)}, u32[]{:S(2)}) collective-permute-start(f32[104,256]{1,0:T(8,128)S(1)} %shard_map.46.refs_0_), channel_id=1, source_target_pairs={{0,96},{16,112},{32,64},{48,80},{64,32},{80,48},{96,0},{112,16},{1... | collective-permute-start | bytes 319496 | tf_op jit(solution)/shard_map/ppermute | solution.py:14
  98.2 5.1 %collective-permute-start.20 = (f32[104,256]{1,0:T(8,128)S(1)}, f32[104,256]{1,0:T(8,128)S(1)}, u32[]{:S(2)}, u32[]{:S(2)}) collective-permute-start(f32[104,256]{1,0:T(8,128)S(1)} %shard_map.46.refs_0_), channel_id=1, source_target_pairs={{0,64},{16,80},{32,96},{48,112},{64,0},{80,16},{96,32},{112,48},{1... | collective-permute-start | bytes 319496 | tf_op jit(solution)/shard_map/ppermute | solution.py:14
  98.2 5.1 %collective-permute-start.19 = (f32[104,256]{1,0:T(8,128)S(1)}, f32[104,256]{1,0:T(8,128)S(1)}, u32[]{:S(2)}, u32[]{:S(2)}) collective-permute-start(f32[104,256]{1,0:T(8,128)S(1)} %shard_map.46.refs_0_), channel_id=1, source_target_pairs={{0,32},{16,48},{32,0},{48,16},{64,96},{80,112},{96,64},{112,80},{1... | collective-permute-start | bytes 319496 | tf_op jit(solution)/shard_map/ppermute | solution.py:14
  103.2 7.4 %collective-permute-start.22 = (f32[4,104,256]{2,1,0:T(8,128)S(1)}, f32[4,104,256]{2,1,0:T(8,128)S(1)}, u32[]{:S(2)}, u32[]{:S(2)}) collective-permute-start(f32[4,104,256]{2,1,0:T(8,128)S(1)} %shard_map.47.own_ref), channel_id=1, source_target_pairs={{0,16},{16,0},{32,48},{48,32},{64,80},{80,64},{96,112},{112,96},{1... | collective-permute-start | bytes 1277960 | tf_op jit(solution)/shard_map/ppermute | solution.py:14

commit v6 on v5

--- a/solution.py
+++ b/solution.py
@@ -320,9 +320,14 @@
         y, r, _, _ = lax.while_loop(go_on, refine, (y, r, bound, jnp.int32(0)))
         return y + multiply(y, r)
 
+    def quartic():
+        square = fast(rest, rest)
+        better = guess + near_full(halves(guess), halves(rest), ((1,), (0,)))
+        return better + fast(better, square)
+
     guess = lax.cond(
         size < 0.5,
-        lambda: finished(fast, guess, rest, size),
+        lambda: lax.cond(size < 0.05, quartic, lambda: finished(fast, guess, rest, size)),
         lambda: finished(full, start, one - full(scaled, start), jnp.float32(1.0)),
     )
     out_ref[...] = guess * down * across

time: 126 us -> 126 us (level)
  transfers between devices with their start and end apart: 25 -> 25, of which waited for: 16 -> 16; matrix products, arithmetic and copies ran while one was open for 4% -> 3% of each run, Pallas kernels for 13% -> 13%
where the time goes in v6:
time: 126 us; the launch traced here: 125 us
  starting transfers between devices  62.7 us (50%)
  waiting for transfers between devices  34.5 us (27%)
  Pallas kernels  21.3 us (17%)
  other arithmetic  3.29 us (3%)
  local copies, waits for them, and re-layouts  3.14 us (2%)
    ppermute x21, starting transfers between devices, to_xor(): return lax.ppermute(value, axis, [(i, i ^ bits) for i in range(size)])  35.1 us
    ppermute x21, waiting for transfers between devices, to_xor(): return lax.ppermute(value, axis, [(i, i ^ bits) for i in range(size)])  20.8 us
    all_to_all x2, starting transfers between devices, to_plane(): lax.all_to_all(sent, 'col', 0, 0, tiled=True).reshape(-1, block.shape[-1])  16.1 us
    ppermute x2, waiting for transfers between devices, to_place(): lax.ppermute(value, ('row', 'col'), [(i, owner(i)) for i in range(128)])  13.7 us
    ppermute x2, starting transfers between devices, to_place(): lax.ppermute(value, ('row', 'col'), [(i, owner(i)) for i in range(128)])  11.5 us
    pallas_call x1, Pallas kernels, inverse_of(): pl.pallas_call(invert_kernel, out_shape=pltpu.VMEM((n, n), jnp.float32),...  10.1 us
    pallas_call x1, Pallas kernels, update(): pl.pallas_call(update_kernel, out_shape=pltpu.HBM(cov.shape, jnp.float32)...  3.91 us
    another operation x4, other arithmetic, side(): return jnp.stack([first, second])  3.29 us
  transfers between devices with their start and end apart: 25, of which 16 were waited for; matrix products, arithmetic and copies ran while one was open for 3% of the time, Pallas kernels for 13%

profile of v6, /device:TPU:1, one launch (start us, length us, event | category | flops | bytes accessed | tf_op | source)
XLA Modules:
  0.0 125.3 jit_solution(4809671771008868001)
XLA Ops:
  1.9 7.6 %all-to-all-start = ((f32[16,72,256]{2,1,0:T(8,128)}), f32[16,72,256]{2,1,0:T(8,128)}, u32[]{:S(2)}, u32[]{:S(2)}) async-start(f32[16,72,256]{2,1,0:T(8,128)} %broadcast_in_dim.4), calls=%async_computation | async-start | bytes 2359296 | tf_op jit(solution)/shard_map/all_to_all | solution.py:40
  9.5 5.8 %collective-permute-start.5 = (f32[72,256]{1,0:T(8,128)S(1)}, f32[72,256]{1,0:T(8,128)S(1)}, u32[]{:S(2)}, u32[]{:S(2)}) collective-permute-start(f32[72,256]{1,0:T(8,128)S(1)} %shard_map.38), channel_id=1, source_target_pairs={{0,0},{1,32},{2,64},{3,96},{4,16},{5,48},{6,80},{7,112},{8,1},{9,3... | collective-permute-start | bytes 221192 | tf_op jit(solution)/shard_map/ppermute | solution.py:18
  15.4 11.3 %collective-permute-done.5 = f32[72,256]{1,0:T(8,128)S(1)} collective-permute-done((f32[72,256]{1,0:T(8,128)S(1)}, f32[72,256]{1,0:T(8,128)S(1)}, u32[]{:S(2)}, u32[]{:S(2)}) %collective-permute-start.5) | collective-permute-done | bytes 73760 | tf_op jit(solution)/shard_map/ppermute | solution.py:18
  26.7 2.8 %collective-permute-start.6 = (f32[72,256]{1,0:T(8,128)S(1)}, f32[72,256]{1,0:T(8,128)S(1)}, u32[]{:S(2)}, u32[]{:S(2)}) collective-permute-start(f32[72,256]{1,0:T(8,128)S(1)} %collective-permute-done.5), channel_id=1, source_target_pairs={{0,32},{16,48},{32,0},{48,16},{64,96},{80,112},{96,64},{112,80},{1... | collective-permute-start | bytes 221192 | tf_op jit(solution)/shard_map/ppermute | solution.py:14
  29.6 1.7 %shard_map.37.cov_ref = f32[576,1152]{1,0:T(8,128)S(1)} custom-call(f32[576,1152]{1,0:T(8,128)} %bitcast.23), custom_call_target="tpu_custom_call" | custom-call | tf_op jit(solution)/shard_map/pallas_call | solution.py:265
  32.5 1.6 %pad_maximum_fusion.1 = f32[2,72,256]{2,1,0:T(8,128)} fusion(f32[1,72,256]{2,1,0:T(8,128)} %get-tuple-element.32, f32[1,72,256]{2,1,0:T(8,128)} %get-tuple-element.31), kind=kLoop, calls=%fused_computation.1 | loop fusion | flops 36864 | bytes 294912 | tf_op jit(solution)/shard_map/stack | solution.py:24
  34.1 3.7 %collective-permute-start.7 = (f32[2,72,256]{2,1,0:T(8,128)}, f32[2,72,256]{2,1,0:T(8,128)}, u32[]{:S(2)}, u32[]{:S(2)}) collective-permute-start(f32[2,72,256]{2,1,0:T(8,128)} %pad_maximum_fusion.1), channel_id=1, source_target_pairs={{0,96},{16,112},{32,64},{48,80},{64,32},{80,48},{96,0},{112,16},{1... | collective-permute-start | bytes 442376 | tf_op jit(solution)/shard_map/ppermute | solution.py:14
  37.8 2.6 %shard_map.39 = (f32[4,72,256]{2,1,0:T(8,128)S(1)}, f32[4,72,256]{2,1,0:T(8,128)S(1)}) custom-call(s32[1]{0:T(128)} %bitcast.2.core_ref, f32[576,1152]{1,0:T(8,128)S(1)} %shard_map.37.cov_ref, f32[1152,256]{1,0:T(8,128)} %bitcast.3.rows_ref), custom_call_target="tpu_custom_call" | custom-call | flops 1019215872 | bytes 2654208 | tf_op jit(solution)/shard_map/pallas_call | solution.py:89
  40.5 1.6 %collective-permute-done.7 = f32[2,72,256]{2,1,0:T(8,128)} collective-permute-done((f32[2,72,256]{2,1,0:T(8,128)}, f32[2,72,256]{2,1,0:T(8,128)}, u32[]{:S(2)}, u32[]{:S(2)}) %collective-permute-start.7) | collective-permute-done | bytes 147488 | tf_op jit(solution)/shard_map/ppermute | solution.py:14
  44.2 2.4 %collective-permute-start.2 = (f32[72,256]{1,0:T(8,128)S(1)}, f32[72,256]{1,0:T(8,128)S(1)}, u32[]{:S(2)}, u32[]{:S(2)}) collective-permute-start(f32[72,256]{1,0:T(8,128)S(1)} %get-tuple-element.21), channel_id=1, source_target_pairs={{0,64},{16,80},{32,96},{48,112},{64,0},{80,16},{96,32},{112,48},{1... | collective-permute-start | bytes 221192 | tf_op jit(solution)/shard_map/ppermute | solution.py:14
  47.1 1.7 %collective-permute-start.8 = (f32[288,256]{1,0:T(8,128)S(1)}, f32[288,256]{1,0:T(8,128)}, u32[]{:S(2)}, u32[]{:S(2)}) collective-permute-start(f32[288,256]{1,0:T(8,128)S(1)} %bitcast.18), channel_id=1, source_target_pairs={{0,16},{16,0},{32,48},{48,32},{64,80},{80,64},{96,112},{112,96},{1... | collective-permute-start | bytes 884744 | tf_op jit(solution)/shard_map/ppermute | solution.py:14
  48.8 1.6 %collective-permute-done.2.c_ref = f32[72,256]{1,0:T(8,128)S(1)} collective-permute-done((f32[72,256]{1,0:T(8,128)S(1)}, f32[72,256]{1,0:T(8,128)S(1)}, u32[]{:S(2)}, u32[]{:S(2)}) %collective-permute-start.2) | collective-permute-done | bytes 73760 | tf_op jit(solution)/shard_map/ppermute | solution.py:14
  50.5 1.5 %collective-permute-done.3.d_ref = f32[72,256]{1,0:T(8,128)S(1)} collective-permute-done((f32[72,256]{1,0:T(8,128)S(1)}, f32[72,256]{1,0:T(8,128)S(1)}, u32[]{:S(2)}, u32[]{:S(2)}) %collective-permute-start.3) | collective-permute-done | bytes 73760 | tf_op jit(solution)/shard_map/ppermute | solution.py:14
  52.0 5.6 %collective-permute-start.4 = (f32[72,256]{1,0:T(8,128)S(1)}, f32[72,256]{1,0:T(8,128)S(1)}, u32[]{:S(2)}, u32[]{:S(2)}) collective-permute-start(f32[72,256]{1,0:T(8,128)S(1)} %shard_map.41.product_ref), channel_id=1, source_target_pairs={{0,0},{1,8},{2,16},{3,24},{4,32},{5,40},{6,48},{7,56},{8,64},{9,72... | collective-permute-start | bytes 221192 | tf_op jit(solution)/shard_map/ppermute | solution.py:18
  57.6 2.3 %collective-permute-done.4 = f32[72,256]{1,0:T(8,128)S(1)} collective-permute-done((f32[72,256]{1,0:T(8,128)S(1)}, f32[72,256]{1,0:T(8,128)S(1)}, u32[]{:S(2)}, u32[]{:S(2)}) %collective-permute-start.4) | collective-permute-done | bytes 73760 | tf_op jit(solution)/shard_map/ppermute | solution.py:18
  61.0 8.5 %all-to-all-start.1 = ((f32[16,72,256]{2,1,0:T(8,128)}), f32[16,72,256]{2,1,0:T(8,128)}, u32[]{:S(2)}, u32[]{:S(2)}) async-start(f32[16,72,256]{2,1,0:T(8,128)} %broadcast_in_dim.5), calls=%async_computation.1 | async-start | bytes 2359296 | tf_op jit(solution)/shard_map/all_to_all | solution.py:40
  70.5 1.6 %shard_map.42 = (f32[4,32,256]{2,1,0:T(8,128)S(1)}, f32[4,32,256]{2,1,0:T(8,128)S(1)}) custom-call(s32[1]{0:T(128)} %bitcast.2.core_ref, f32[288,256]{1,0:T(8,128)S(1)} %bitcast.20, f32[288,256]{1,0:T(8,128)S(1)} %bitcast.21, f32[288,256]{1,0:T(8,128)S(1)} %bitcast.19, f32[288,256]{1,0:T(8,128)} %collective-permute-done.8.other_ref), custom_call_target="tpu_custom_call" | custom-call | flops 226492416 | bytes 1179648 | tf_op jit(solution)/shard_map/pallas_call | solution.py:106
  72.1 2.6 %collective-permute-start.9 = (f32[4,32,256]{2,1,0:T(8,128)S(1)}, f32[4,32,256]{2,1,0:T(8,128)S(1)}, u32[]{:S(2)}, u32[]{:S(2)}) collective-permute-start(f32[4,32,256]{2,1,0:T(8,128)S(1)} %get-tuple-element.24), channel_id=1, source_target_pairs={{0,16},{16,0},{32,48},{48,32},{64,80},{80,64},{96,112},{112,96},{1... | collective-permute-start | bytes 393224 | tf_op jit(solution)/shard_map/ppermute | solution.py:14
  75.9 1.2 collective-permute-start.11
  77.1 2.6 %collective-permute-start.12 = (f32[32,256]{1,0:T(8,128)S(1)}, f32[32,256]{1,0:T(8,128)S(1)}, u32[]{:S(2)}, u32[]{:S(2)}) collective-permute-start(f32[32,256]{1,0:T(8,128)S(1)} %get-tuple-element.28), channel_id=1, source_target_pairs={{0,96},{16,112},{32,64},{48,80},{64,32},{80,48},{96,0},{112,16},{1... | collective-permute-start | bytes 98312 | tf_op jit(solution)/shard_map/ppermute | solution.py:14
  80.6 1.2 collective-permute-done.12.d_ref
  81.9 2.9 %collective-permute-start.15 = (f32[32,256]{1,0:T(8,128)S(1)}, f32[32,256]{1,0:T(8,128)S(1)}, u32[]{:S(2)}, u32[]{:S(2)}) collective-permute-start(f32[32,256]{1,0:T(8,128)S(1)} %shard_map.44.a_ref), channel_id=1, source_target_pairs={{0,3},{1,2},{2,1},{3,0},{4,7},{5,6},{6,5},{7,4},{8,11},{9,10},{10,... | collective-permute-start | bytes 98312 | tf_op jit(solution)/shard_map/ppermute | solution.py:14
  85.4 3.3 %collective-permute-done.15.d_ref = f32[32,256]{1,0:T(8,128)S(1)} collective-permute-done((f32[32,256]{1,0:T(8,128)S(1)}, f32[32,256]{1,0:T(8,128)S(1)}, u32[]{:S(2)}, u32[]{:S(2)}) %collective-permute-start.15) | collective-permute-done | bytes 32800 | tf_op jit(solution)/shard_map/ppermute | solution.py:14
  89.1 2.5 %collective-permute-start.18 = (f32[32,256]{1,0:T(8,128)S(1)}, f32[32,256]{1,0:T(8,128)S(1)}, u32[]{:S(2)}, u32[]{:S(2)}) collective-permute-start(f32[32,256]{1,0:T(8,128)S(1)} %shard_map.45.a_ref), channel_id=1, source_target_pairs={{0,12},{1,13},{2,14},{3,15},{4,8},{5,9},{6,10},{7,11},{8,4},{9,5},... | collective-permute-start | bytes 98312 | tf_op jit(solution)/shard_map/ppermute | solution.py:14
  93.1 2.7 %collective-permute-done.17.c_ref = f32[32,256]{1,0:T(8,128)S(1)} collective-permute-done((f32[32,256]{1,0:T(8,128)S(1)}, f32[32,256]{1,0:T(8,128)S(1)}, u32[]{:S(2)}, u32[]{:S(2)}) %collective-permute-start.17) | collective-permute-done | bytes 32800 | tf_op jit(solution)/shard_map/ppermute | solution.py:14
  95.8 2.3 %collective-permute-start.21 = (f32[104,256]{1,0:T(8,128)S(1)}, f32[104,256]{1,0:T(8,128)S(1)}, u32[]{:S(2)}, u32[]{:S(2)}) collective-permute-start(f32[104,256]{1,0:T(8,128)S(1)} %shard_map.46.refs_0_), channel_id=1, source_target_pairs={{0,96},{16,112},{32,64},{48,80},{64,32},{80,48},{96,0},{112,16},{1... | collective-permute-start | bytes 319496 | tf_op jit(solution)/shard_map/ppermute | solution.py:14
  99.2 1.8 %collective-permute-done.21.refs_3_ = f32[104,256]{1,0:T(8,128)S(1)} collective-permute-done((f32[104,256]{1,0:T(8,128)S(1)}, f32[104,256]{1,0:T(8,128)S(1)}, u32[]{:S(2)}, u32[]{:S(2)}) %collective-permute-start.21) | collective-permute-done | bytes 106528 | tf_op jit(solution)/shard_map/ppermute | solution.py:14
  100.9 2.3 %collective-permute-done.20.refs_2_ = f32[104,256]{1,0:T(8,128)S(1)} collective-permute-done((f32[104,256]{1,0:T(8,128)S(1)}, f32[104,256]{1,0:T(8,128)S(1)}, u32[]{:S(2)}, u32[]{:S(2)}) %collective-permute-start.20) | collective-permute-done | bytes 106528 | tf_op jit(solution)/shard_map/ppermute | solution.py:14
  103.2 6.0 %collective-permute-start.22 = (f32[4,104,256]{2,1,0:T(8,128)S(1)}, f32[4,104,256]{2,1,0:T(8,128)S(1)}, u32[]{:S(2)}, u32[]{:S(2)}) collective-permute-start(f32[4,104,256]{2,1,0:T(8,128)S(1)} %shard_map.47.own_ref), channel_id=1, source_target_pairs={{0,16},{16,0},{32,48},{48,32},{64,80},{80,64},{96,112},{112,96},{1... | collective-permute-start | bytes 1277960 | tf_op jit(solution)/shard_map/ppermute | solution.py:14
  109.3 1.4 %collective-permute-done.22.other_ref = f32[4,104,256]{2,1,0:T(8,128)S(1)} collective-permute-done((f32[4,104,256]{2,1,0:T(8,128)S(1)}, f32[4,104,256]{2,1,0:T(8,128)S(1)}, u32[]{:S(2)}, u32[]{:S(2)}) %collective-permute-start.22) | collective-permute-done | bytes 426016 | tf_op jit(solution)/shard_map/ppermute | solution.py:14
  110.7 10.1 %shard_map.48.inv_ref = f32[256,256]{1,0:T(8,128)S(1)} custom-call(s32[1]{0:T(128)} %bitcast.2.core_ref, f32[4,104,256]{2,1,0:T(8,128)S(1)} %shard_map.47.own_ref, f32[4,104,256]{2,1,0:T(8,128)S(1)} %collective-permute-done.22.other_ref, f32[1,256]{1,0:T(1,128)S(1)} %bitcast.22), custom_call_target="tpu_custom_call" | custom-call | flops 1342177280 | bytes 786432 | tf_op jit(solution)/shard_map/pallas_call | solution.py:338
  121.2 3.9 %shard_map.50 = f32[576,1152]{1,0:T(8,128)} custom-call(f32[576,1152]{1,0:T(8,128)S(1)} %shard_map.37.cov_ref, f32[1152,256]{1,0:T(8,128)} %bitcast.4.rows_ref, f32[576,256]{1,0:T(8,128)S(1)} %shard_map.49.gain_ref), custom_call_target="tpu_custom_call" | custom-call | flops 1019215872 | bytes 2654208 | tf_op jit(solution)/shard_map/pallas_call | solution.py:219
  (44 shorter events, 13.9 us)
Async XLA Ops:
  1.9 35.9 %all-to-all-start = ((f32[16,72,256]{2,1,0:T(8,128)}), f32[16,72,256]{2,1,0:T(8,128)}, u32[]{:S(2)}, u32[]{:S(2)}) async-start(f32[16,72,256]{2,1,0:T(8,128)} %broadcast_in_dim.4), calls=%async_computation | async-start | bytes 2359296 | tf_op jit(solution)/shard_map/all_to_all | solution.py:40
  9.5 17.2 %collective-permute-start.5 = (f32[72,256]{1,0:T(8,128)S(1)}, f32[72,256]{1,0:T(8,128)S(1)}, u32[]{:S(2)}, u32[]{:S(2)}) collective-permute-start(f32[72,256]{1,0:T(8,128)S(1)} %shard_map.38), channel_id=1, source_target_pairs={{0,0},{1,32},{2,64},{3,96},{4,16},{5,48},{6,80},{7,112},{8,1},{9,3... | collective-permute-start | bytes 221192 | tf_op jit(solution)/shard_map/ppermute | solution.py:18
  26.7 5.1 %collective-permute-start.6 = (f32[72,256]{1,0:T(8,128)S(1)}, f32[72,256]{1,0:T(8,128)S(1)}, u32[]{:S(2)}, u32[]{:S(2)}) collective-permute-start(f32[72,256]{1,0:T(8,128)S(1)} %collective-permute-done.5), channel_id=1, source_target_pairs={{0,32},{16,48},{32,0},{48,16},{64,96},{80,112},{96,64},{112,80},{1... | collective-permute-start | bytes 221192 | tf_op jit(solution)/shard_map/ppermute | solution.py:14
  34.1 8.0 %collective-permute-start.7 = (f32[2,72,256]{2,1,0:T(8,128)}, f32[2,72,256]{2,1,0:T(8,128)}, u32[]{:S(2)}, u32[]{:S(2)}) collective-permute-start(f32[2,72,256]{2,1,0:T(8,128)} %pad_maximum_fusion.1), channel_id=1, source_target_pairs={{0,96},{16,112},{32,64},{48,80},{64,32},{80,48},{96,0},{112,16},{1... | collective-permute-start | bytes 442376 | tf_op jit(solution)/shard_map/ppermute | solution.py:14
  40.4 11.6 %copy-start = (f32[4,72,256]{2,1,0:T(8,128)}, f32[4,72,256]{2,1,0:T(8,128)S(1)}, u32[]{:S(2)}) copy-start(f32[4,72,256]{2,1,0:T(8,128)S(1)} %get-tuple-element.18) | copy-start | bytes 884740
  40.4 2.7 %collective-permute-start = (f32[4,72,256]{2,1,0:T(8,128)S(1)}, f32[4,72,256]{2,1,0:T(8,128)S(1)}, u32[]{:S(2)}, u32[]{:S(2)}) collective-permute-start(f32[4,72,256]{2,1,0:T(8,128)S(1)} %get-tuple-element.18), channel_id=1, source_target_pairs={{0,16},{16,0},{32,48},{48,32},{64,80},{80,64},{96,112},{112,96},{1... | collective-permute-start | bytes 884744 | tf_op jit(solution)/shard_map/ppermute | solution.py:14
  43.2 5.7 %collective-permute-start.1 = (f32[72,256]{1,0:T(8,128)S(1)}, f32[72,256]{1,0:T(8,128)S(1)}, u32[]{:S(2)}, u32[]{:S(2)}) collective-permute-start(f32[72,256]{1,0:T(8,128)S(1)} %get-tuple-element.20), channel_id=1, source_target_pairs={{0,32},{16,48},{32,0},{48,16},{64,96},{80,112},{96,64},{112,80},{1... | collective-permute-start | bytes 221192 | tf_op jit(solution)/shard_map/ppermute | solution.py:14
  44.2 6.3 %collective-permute-start.2 = (f32[72,256]{1,0:T(8,128)S(1)}, f32[72,256]{1,0:T(8,128)S(1)}, u32[]{:S(2)}, u32[]{:S(2)}) collective-permute-start(f32[72,256]{1,0:T(8,128)S(1)} %get-tuple-element.21), channel_id=1, source_target_pairs={{0,64},{16,80},{32,96},{48,112},{64,0},{80,16},{96,32},{112,48},{1... | collective-permute-start | bytes 221192 | tf_op jit(solution)/shard_map/ppermute | solution.py:14
  46.6 5.4 %collective-permute-start.3 = (f32[72,256]{1,0:T(8,128)S(1)}, f32[72,256]{1,0:T(8,128)S(1)}, u32[]{:S(2)}, u32[]{:S(2)}) collective-permute-start(f32[72,256]{1,0:T(8,128)S(1)} %get-tuple-element.22), channel_id=1, source_target_pairs={{0,96},{16,112},{32,64},{48,80},{64,32},{80,48},{96,0},{112,16},{1... | collective-permute-start | bytes 221192 | tf_op jit(solution)/shard_map/ppermute | solution.py:14
  47.1 22.4 %collective-permute-start.8 = (f32[288,256]{1,0:T(8,128)S(1)}, f32[288,256]{1,0:T(8,128)}, u32[]{:S(2)}, u32[]{:S(2)}) collective-permute-start(f32[288,256]{1,0:T(8,128)S(1)} %bitcast.18), channel_id=1, source_target_pairs={{0,16},{16,0},{32,48},{48,32},{64,80},{80,64},{96,112},{112,96},{1... | collective-permute-start | bytes 884744 | tf_op jit(solution)/shard_map/ppermute | solution.py:14
  52.0 8.0 %collective-permute-start.4 = (f32[72,256]{1,0:T(8,128)S(1)}, f32[72,256]{1,0:T(8,128)S(1)}, u32[]{:S(2)}, u32[]{:S(2)}) collective-permute-start(f32[72,256]{1,0:T(8,128)S(1)} %shard_map.41.product_ref), channel_id=1, source_target_pairs={{0,0},{1,8},{2,16},{3,24},{4,32},{5,40},{6,48},{7,56},{8,64},{9,72... | collective-permute-start | bytes 221192 | tf_op jit(solution)/shard_map/ppermute | solution.py:18
  61.0 60.1 %all-to-all-start.1 = ((f32[16,72,256]{2,1,0:T(8,128)}), f32[16,72,256]{2,1,0:T(8,128)}, u32[]{:S(2)}, u32[]{:S(2)}) async-start(f32[16,72,256]{2,1,0:T(8,128)} %broadcast_in_dim.5), calls=%async_computation.1 | async-start | bytes 2359296 | tf_op jit(solution)/shard_map/all_to_all | solution.py:40
  69.6 1.0 copy-start.1
  70.5 40.2 %copy-start.2 = (f32[2,128]{1,0:T(2,128)S(1)}, f32[2,128]{1,0:T(2,128)}, u32[]{:S(2)}) copy-start(f32[2,128]{1,0:T(2,128)} %param.5) | copy-start | bytes 3076
  72.1 3.6 %collective-permute-start.9 = (f32[4,32,256]{2,1,0:T(8,128)S(1)}, f32[4,32,256]{2,1,0:T(8,128)S(1)}, u32[]{:S(2)}, u32[]{:S(2)}) collective-permute-start(f32[4,32,256]{2,1,0:T(8,128)S(1)} %get-tuple-element.24), channel_id=1, source_target_pairs={{0,16},{16,0},{32,48},{48,32},{64,80},{80,64},{96,112},{112,96},{1... | collective-permute-start | bytes 393224 | tf_op jit(solution)/shard_map/ppermute | solution.py:14
  75.8 3.9 %collective-permute-start.10 = (f32[32,256]{1,0:T(8,128)S(1)}, f32[32,256]{1,0:T(8,128)S(1)}, u32[]{:S(2)}, u32[]{:S(2)}) collective-permute-start(f32[32,256]{1,0:T(8,128)S(1)} %get-tuple-element.26), channel_id=1, source_target_pairs={{0,32},{16,48},{32,0},{48,16},{64,96},{80,112},{96,64},{112,80},{1... | collective-permute-start | bytes 98312 | tf_op jit(solution)/shard_map/ppermute | solution.py:14
  75.9 4.7 %collective-permute-start.11 = (f32[32,256]{1,0:T(8,128)S(1)}, f32[32,256]{1,0:T(8,128)S(1)}, u32[]{:S(2)}, u32[]{:S(2)}) collective-permute-start(f32[32,256]{1,0:T(8,128)S(1)} %get-tuple-element.27), channel_id=1, source_target_pairs={{0,64},{16,80},{32,96},{48,112},{64,0},{80,16},{96,32},{112,48},{1... | collective-permute-start | bytes 98312 | tf_op jit(solution)/shard_map/ppermute | solution.py:14
  77.1 4.7 %collective-permute-start.12 = (f32[32,256]{1,0:T(8,128)S(1)}, f32[32,256]{1,0:T(8,128)S(1)}, u32[]{:S(2)}, u32[]{:S(2)}) collective-permute-start(f32[32,256]{1,0:T(8,128)S(1)} %get-tuple-element.28), channel_id=1, source_target_pairs={{0,96},{16,112},{32,64},{48,80},{64,32},{80,48},{96,0},{112,16},{1... | collective-permute-start | bytes 98312 | tf_op jit(solution)/shard_map/ppermute | solution.py:14
  81.9 6.8 %collective-permute-start.15 = (f32[32,256]{1,0:T(8,128)S(1)}, f32[32,256]{1,0:T(8,128)S(1)}, u32[]{:S(2)}, u32[]{:S(2)}) collective-permute-start(f32[32,256]{1,0:T(8,128)S(1)} %shard_map.44.a_ref), channel_id=1, source_target_pairs={{0,3},{1,2},{2,1},{3,0},{4,7},{5,6},{6,5},{7,4},{8,11},{9,10},{10,... | collective-permute-start | bytes 98312 | tf_op jit(solution)/shard_map/ppermute | solution.py:14
  84.8 4.3 %collective-permute-start.14 = (f32[32,256]{1,0:T(8,128)S(1)}, f32[32,256]{1,0:T(8,128)S(1)}, u32[]{:S(2)}, u32[]{:S(2)}) collective-permute-start(f32[32,256]{1,0:T(8,128)S(1)} %shard_map.44.a_ref), channel_id=1, source_target_pairs={{0,2},{1,3},{2,0},{3,1},{4,6},{5,7},{6,4},{7,5},{8,10},{9,11},{10,... | collective-permute-start | bytes 98312 | tf_op jit(solution)/shard_map/ppermute | solution.py:14
  85.4 3.6 %collective-permute-start.13 = (f32[32,256]{1,0:T(8,128)S(1)}, f32[32,256]{1,0:T(8,128)S(1)}, u32[]{:S(2)}, u32[]{:S(2)}) collective-permute-start(f32[32,256]{1,0:T(8,128)S(1)} %shard_map.44.a_ref), channel_id=1, source_target_pairs={{0,1},{1,0},{2,3},{3,2},{4,5},{5,4},{6,7},{7,6},{8,9},{9,8},{10,11... | collective-permute-start | bytes 98312 | tf_op jit(solution)/shard_map/ppermute | solution.py:14
  89.1 4.1 %collective-permute-start.18 = (f32[32,256]{1,0:T(8,128)S(1)}, f32[32,256]{1,0:T(8,128)S(1)}, u32[]{:S(2)}, u32[]{:S(2)}) collective-permute-start(f32[32,256]{1,0:T(8,128)S(1)} %shard_map.45.a_ref), channel_id=1, source_target_pairs={{0,12},{1,13},{2,14},{3,15},{4,8},{5,9},{6,10},{7,11},{8,4},{9,5},... | collective-permute-start | bytes 98312 | tf_op jit(solution)/shard_map/ppermute | solution.py:14
  91.5 4.3 %collective-permute-start.17 = (f32[32,256]{1,0:T(8,128)S(1)}, f32[32,256]{1,0:T(8,128)S(1)}, u32[]{:S(2)}, u32[]{:S(2)}) collective-permute-start(f32[32,256]{1,0:T(8,128)S(1)} %shard_map.45.a_ref), channel_id=1, source_target_pairs={{0,8},{1,9},{2,10},{3,11},{4,12},{5,13},{6,14},{7,15},{8,0},{9,1},... | collective-permute-start | bytes 98312 | tf_op jit(solution)/shard_map/ppermute | solution.py:14
  92.1 3.7 %collective-permute-start.16 = (f32[32,256]{1,0:T(8,128)S(1)}, f32[32,256]{1,0:T(8,128)S(1)}, u32[]{:S(2)}, u32[]{:S(2)}) collective-permute-start(f32[32,256]{1,0:T(8,128)S(1)} %shard_map.45.a_ref), channel_id=1, source_target_pairs={{0,4},{1,5},{2,6},{3,7},{4,0},{5,1},{6,2},{7,3},{8,12},{9,13},{10,... | collective-permute-start | bytes 98312 | tf_op jit(solution)/shard_map/ppermute | solution.py:14
  95.8 5.1 %collective-permute-start.21 = (f32[104,256]{1,0:T(8,128)S(1)}, f32[104,256]{1,0:T(8,128)S(1)}, u32[]{:S(2)}, u32[]{:S(2)}) collective-permute-start(f32[104,256]{1,0:T(8,128)S(1)} %shard_map.46.refs_0_), channel_id=1, source_target_pairs={{0,96},{16,112},{32,64},{48,80},{64,32},{80,48},{96,0},{112,16},{1... | collective-permute-start | bytes 319496 | tf_op jit(solution)/shard_map/ppermute | solution.py:14
  98.1 5.1 %collective-permute-start.20 = (f32[104,256]{1,0:T(8,128)S(1)}, f32[104,256]{1,0:T(8,128)S(1)}, u32[]{:S(2)}, u32[]{:S(2)}) collective-permute-start(f32[104,256]{1,0:T(8,128)S(1)} %shard_map.46.refs_0_), channel_id=1, source_target_pairs={{0,64},{16,80},{32,96},{48,112},{64,0},{80,16},{96,32},{112,48},{1... | collective-permute-start | bytes 319496 | tf_op jit(solution)/shard_map/ppermute | solution.py:14
  98.2 5.1 %collective-permute-start.19 = (f32[104,256]{1,0:T(8,128)S(1)}, f32[104,256]{1,0:T(8,128)S(1)}, u32[]{:S(2)}, u32[]{:S(2)}) collective-permute-start(f32[104,256]{1,0:T(8,128)S(1)} %shard_map.46.refs_0_), channel_id=1, source_target_pairs={{0,32},{16,48},{32,0},{48,16},{64,96},{80,112},{96,64},{112,80},{1... | collective-permute-start | bytes 319496 | tf_op jit(solution)/shard_map/ppermute | solution.py:14
  103.2 7.4 %collective-permute-start.22 = (f32[4,104,256]{2,1,0:T(8,128)S(1)}, f32[4,104,256]{2,1,0:T(8,128)S(1)}, u32[]{:S(2)}, u32[]{:S(2)}) collective-permute-start(f32[4,104,256]{2,1,0:T(8,128)S(1)} %shard_map.47.own_ref), channel_id=1, source_target_pairs={{0,16},{16,0},{32,48},{48,32},{64,80},{80,64},{96,112},{112,96},{1... | collective-permute-start | bytes 1277960 | tf_op jit(solution)/shard_map/ppermute | solution.py:14

commit v7 on v6

--- a/solution.py
+++ b/solution.py
@@ -227,25 +227,6 @@
         ),
         compiler_params=pltpu.CompilerParams(vmem_limit_bytes=20 << 20),
     )(cov, pltpu.with_memory_space_constraint(rows, pltpu.VMEM), gain)
-
-
-def gain_kernel(core_ref, own_ref, other_ref, inv_ref, out_ref):
-    block = out_ref.shape[0] // 8
-    inverse = halves(inv_ref[...])
-    for ref, at in ((own_ref, core_ref[0]), (other_ref, 1 - core_ref[0])):
-        for j in range(4):
-            out_ref[pl.ds(pl.multiple_of((4 * at + j) * block, 8), block), :] = ref[j, :block, :]
-    out_ref[...] = near_full(halves(out_ref[...]), inverse, ((1,), (0,)))
-
-
-def gain_of(core, own, other, inverse, block):
-    return pl.pallas_call(
-        gain_kernel,
-        out_shape=pltpu.VMEM((8 * block, own.shape[2]), jnp.float32),
-        in_specs=[SCALAR, VMEM, VMEM, VMEM],
-        out_specs=VMEM,
-        compiler_params=pltpu.CompilerParams(vmem_limit_bytes=6 << 20),
-    )(core.reshape(1), own, other, inverse)
 
 
 def hold_kernel(far_ref, near_ref, sems):
@@ -330,14 +311,19 @@
         lambda: lax.cond(size < 0.05, quartic, lambda: finished(fast, guess, rest, size)),
         lambda: finished(full, start, one - full(scaled, start), jnp.float32(1.0)),
     )
-    out_ref[...] = guess * down * across
-
-
-def inverse_of(core, own, other, noise):
+    inverse = halves(guess * down * across)
+    block = out_ref.shape[0] // 8
+    for ref, at in ((own_ref, core_ref[0]), (other_ref, 1 - core_ref[0])):
+        for j in range(4):
+            out_ref[pl.ds(pl.multiple_of((4 * at + j) * block, 8), block), :] = ref[j, :block, :]
+    out_ref[...] = near_full(halves(out_ref[...]), inverse, ((1,), (0,)))
+
+
+def gain_of(core, own, other, noise, block):
     n = noise.shape[1]
     return pl.pallas_call(
         invert_kernel,
-        out_shape=pltpu.VMEM((n, n), jnp.float32),
+        out_shape=pltpu.VMEM((8 * block, n), jnp.float32),
         in_specs=[SCALAR, VMEM, VMEM, VMEM],
         out_specs=VMEM,
         scratch_shapes=[pltpu.VMEM((n, n), jnp.float32)],
@@ -374,8 +360,7 @@
 
     product_rows = to_plane(to_place(product, product_place))
 
-    inverse = inverse_of(core, packed, mate, noise.reshape(1, width))
-    gain = gain_of(core, packed, mate, inverse, block)
+    gain = gain_of(core, packed, mate, noise.reshape(1, width), block)
     return update(turned, product_rows, gain).T
 
 

time: 126 us -> 126 us (level)
    pallas_call x2 -> x1, Pallas kernels: 10.5 us -> 10.5 us  [gain_of(): pl.pallas_call(invert_kernel, out_shape=pltpu.VMEM((8 * block, n), jnp.fl...]
where the time goes in v7:
time: 126 us; the launch traced here: 125 us
  starting transfers between devices  62.7 us (50%)
  waiting for transfers between devices  34.5 us (27%)
  Pallas kernels  21.3 us (17%)
  other arithmetic  3.29 us (3%)
  local copies, waits for them, and re-layouts  3.14 us (2%)
    ppermute x21, starting transfers between devices, to_xor(): return lax.ppermute(value, axis, [(i, i ^ bits) for i in range(size)])  35.1 us
    ppermute x21, waiting for transfers between devices, to_xor(): return lax.ppermute(value, axis, [(i, i ^ bits) for i in range(size)])  20.8 us
    all_to_all x2, starting transfers between devices, to_plane(): lax.all_to_all(sent, 'col', 0, 0, tiled=True).reshape(-1, block.shape[-1])  16.1 us
    ppermute x2, waiting for transfers between devices, to_place(): lax.ppermute(value, ('row', 'col'), [(i, owner(i)) for i in range(128)])  13.7 us
    ppermute x2, starting transfers between devices, to_place(): lax.ppermute(value, ('row', 'col'), [(i, owner(i)) for i in range(128)])  11.5 us
    pallas_call x1, Pallas kernels, gain_of(): pl.pallas_call(invert_kernel, out_shape=pltpu.VMEM((8 * block, n), jnp.fl...  10.5 us
    pallas_call x1, Pallas kernels, update(): pl.pallas_call(update_kernel, out_shape=pltpu.HBM(cov.shape, jnp.float32)...  3.92 us
    another operation x4, other arithmetic, side(): return jnp.stack([first, second])  3.29 us
  transfers between devices with their start and end apart: 25, of which 16 were waited for; matrix products, arithmetic and copies ran while one was open for 3% of the time, Pallas kernels for 13%

profile of v7, /device:TPU:1, one launch (start us, length us, event | category | flops | bytes accessed | tf_op | source)
XLA Modules:
  0.0 125.3 jit_solution(5074898281924225512)
XLA Ops:
  1.9 7.6 %all-to-all-start = ((f32[16,72,256]{2,1,0:T(8,128)}), f32[16,72,256]{2,1,0:T(8,128)}, u32[]{:S(2)}, u32[]{:S(2)}) async-start(f32[16,72,256]{2,1,0:T(8,128)} %broadcast_in_dim.4), calls=%async_computation | async-start | bytes 2359296 | tf_op jit(solution)/shard_map/all_to_all | solution.py:40
  9.5 5.8 %collective-permute-start.5 = (f32[72,256]{1,0:T(8,128)S(1)}, f32[72,256]{1,0:T(8,128)S(1)}, u32[]{:S(2)}, u32[]{:S(2)}) collective-permute-start(f32[72,256]{1,0:T(8,128)S(1)} %shard_map.38), channel_id=1, source_target_pairs={{0,0},{1,32},{2,64},{3,96},{4,16},{5,48},{6,80},{7,112},{8,1},{9,3... | collective-permute-start | bytes 221192 | tf_op jit(solution)/shard_map/ppermute | solution.py:18
  15.4 11.3 %collective-permute-done.5 = f32[72,256]{1,0:T(8,128)S(1)} collective-permute-done((f32[72,256]{1,0:T(8,128)S(1)}, f32[72,256]{1,0:T(8,128)S(1)}, u32[]{:S(2)}, u32[]{:S(2)}) %collective-permute-start.5) | collective-permute-done | bytes 73760 | tf_op jit(solution)/shard_map/ppermute | solution.py:18
  26.7 2.8 %collective-permute-start.6 = (f32[72,256]{1,0:T(8,128)S(1)}, f32[72,256]{1,0:T(8,128)S(1)}, u32[]{:S(2)}, u32[]{:S(2)}) collective-permute-start(f32[72,256]{1,0:T(8,128)S(1)} %collective-permute-done.5), channel_id=1, source_target_pairs={{0,32},{16,48},{32,0},{48,16},{64,96},{80,112},{96,64},{112,80},{1... | collective-permute-start | bytes 221192 | tf_op jit(solution)/shard_map/ppermute | solution.py:14
  29.6 1.7 %shard_map.37.cov_ref = f32[576,1152]{1,0:T(8,128)S(1)} custom-call(f32[576,1152]{1,0:T(8,128)} %bitcast.23), custom_call_target="tpu_custom_call" | custom-call | tf_op jit(solution)/shard_map/pallas_call | solution.py:246
  32.5 1.6 %pad_maximum_fusion.1 = f32[2,72,256]{2,1,0:T(8,128)} fusion(f32[1,72,256]{2,1,0:T(8,128)} %get-tuple-element.32, f32[1,72,256]{2,1,0:T(8,128)} %get-tuple-element.31), kind=kLoop, calls=%fused_computation.1 | loop fusion | flops 36864 | bytes 294912 | tf_op jit(solution)/shard_map/stack | solution.py:24
  34.1 3.7 %collective-permute-start.7 = (f32[2,72,256]{2,1,0:T(8,128)}, f32[2,72,256]{2,1,0:T(8,128)}, u32[]{:S(2)}, u32[]{:S(2)}) collective-permute-start(f32[2,72,256]{2,1,0:T(8,128)} %pad_maximum_fusion.1), channel_id=1, source_target_pairs={{0,96},{16,112},{32,64},{48,80},{64,32},{80,48},{96,0},{112,16},{1... | collective-permute-start | bytes 442376 | tf_op jit(solution)/shard_map/ppermute | solution.py:14
  37.8 2.6 %shard_map.39 = (f32[4,72,256]{2,1,0:T(8,128)S(1)}, f32[4,72,256]{2,1,0:T(8,128)S(1)}) custom-call(s32[1]{0:T(128)} %bitcast.2.core_ref, f32[576,1152]{1,0:T(8,128)S(1)} %shard_map.37.cov_ref, f32[1152,256]{1,0:T(8,128)} %bitcast.3.rows_ref), custom_call_target="tpu_custom_call" | custom-call | flops 1019215872 | bytes 2654208 | tf_op jit(solution)/shard_map/pallas_call | solution.py:89
  40.5 1.6 %collective-permute-done.7 = f32[2,72,256]{2,1,0:T(8,128)} collective-permute-done((f32[2,72,256]{2,1,0:T(8,128)}, f32[2,72,256]{2,1,0:T(8,128)}, u32[]{:S(2)}, u32[]{:S(2)}) %collective-permute-start.7) | collective-permute-done | bytes 147488 | tf_op jit(solution)/shard_map/ppermute | solution.py:14
  44.2 2.4 %collective-permute-start.2 = (f32[72,256]{1,0:T(8,128)S(1)}, f32[72,256]{1,0:T(8,128)S(1)}, u32[]{:S(2)}, u32[]{:S(2)}) collective-permute-start(f32[72,256]{1,0:T(8,128)S(1)} %get-tuple-element.21), channel_id=1, source_target_pairs={{0,64},{16,80},{32,96},{48,112},{64,0},{80,16},{96,32},{112,48},{1... | collective-permute-start | bytes 221192 | tf_op jit(solution)/shard_map/ppermute | solution.py:14
  47.1 1.7 %collective-permute-start.8 = (f32[288,256]{1,0:T(8,128)S(1)}, f32[288,256]{1,0:T(8,128)}, u32[]{:S(2)}, u32[]{:S(2)}) collective-permute-start(f32[288,256]{1,0:T(8,128)S(1)} %bitcast.18), channel_id=1, source_target_pairs={{0,16},{16,0},{32,48},{48,32},{64,80},{80,64},{96,112},{112,96},{1... | collective-permute-start | bytes 884744 | tf_op jit(solution)/shard_map/ppermute | solution.py:14
  48.8 1.6 %collective-permute-done.2.c_ref = f32[72,256]{1,0:T(8,128)S(1)} collective-permute-done((f32[72,256]{1,0:T(8,128)S(1)}, f32[72,256]{1,0:T(8,128)S(1)}, u32[]{:S(2)}, u32[]{:S(2)}) %collective-permute-start.2) | collective-permute-done | bytes 73760 | tf_op jit(solution)/shard_map/ppermute | solution.py:14
  50.5 1.5 %collective-permute-done.3.d_ref = f32[72,256]{1,0:T(8,128)S(1)} collective-permute-done((f32[72,256]{1,0:T(8,128)S(1)}, f32[72,256]{1,0:T(8,128)S(1)}, u32[]{:S(2)}, u32[]{:S(2)}) %collective-permute-start.3) | collective-permute-done | bytes 73760 | tf_op jit(solution)/shard_map/ppermute | solution.py:14
  52.0 5.6 %collective-permute-start.4 = (f32[72,256]{1,0:T(8,128)S(1)}, f32[72,256]{1,0:T(8,128)S(1)}, u32[]{:S(2)}, u32[]{:S(2)}) collective-permute-start(f32[72,256]{1,0:T(8,128)S(1)} %shard_map.41.product_ref), channel_id=1, source_target_pairs={{0,0},{1,8},{2,16},{3,24},{4,32},{5,40},{6,48},{7,56},{8,64},{9,72... | collective-permute-start | bytes 221192 | tf_op jit(solution)/shard_map/ppermute | solution.py:18
  57.6 2.3 %collective-permute-done.4 = f32[72,256]{1,0:T(8,128)S(1)} collective-permute-done((f32[72,256]{1,0:T(8,128)S(1)}, f32[72,256]{1,0:T(8,128)S(1)}, u32[]{:S(2)}, u32[]{:S(2)}) %collective-permute-start.4) | collective-permute-done | bytes 73760 | tf_op jit(solution)/shard_map/ppermute | solution.py:18
  61.0 8.5 %all-to-all-start.1 = ((f32[16,72,256]{2,1,0:T(8,128)}), f32[16,72,256]{2,1,0:T(8,128)}, u32[]{:S(2)}, u32[]{:S(2)}) async-start(f32[16,72,256]{2,1,0:T(8,128)} %broadcast_in_dim.5), calls=%async_computation.1 | async-start | bytes 2359296 | tf_op jit(solution)/shard_map/all_to_all | solution.py:40
  70.5 1.6 %shard_map.42 = (f32[4,32,256]{2,1,0:T(8,128)S(1)}, f32[4,32,256]{2,1,0:T(8,128)S(1)}) custom-call(s32[1]{0:T(128)} %bitcast.2.core_ref, f32[288,256]{1,0:T(8,128)S(1)} %bitcast.20, f32[288,256]{1,0:T(8,128)S(1)} %bitcast.21, f32[288,256]{1,0:T(8,128)S(1)} %bitcast.19, f32[288,256]{1,0:T(8,128)} %collective-permute-done.8.other_ref), custom_call_target="tpu_custom_call" | custom-call | flops 226492416 | bytes 1179648 | tf_op jit(solution)/shard_map/pallas_call | solution.py:106
  72.1 2.6 %collective-permute-start.9 = (f32[4,32,256]{2,1,0:T(8,128)S(1)}, f32[4,32,256]{2,1,0:T(8,128)S(1)}, u32[]{:S(2)}, u32[]{:S(2)}) collective-permute-start(f32[4,32,256]{2,1,0:T(8,128)S(1)} %get-tuple-element.24), channel_id=1, source_target_pairs={{0,16},{16,0},{32,48},{48,32},{64,80},{80,64},{96,112},{112,96},{1... | collective-permute-start | bytes 393224 | tf_op jit(solution)/shard_map/ppermute | solution.py:14
  75.9 1.2 collective-permute-start.11
  77.1 2.6 %collective-permute-start.12 = (f32[32,256]{1,0:T(8,128)S(1)}, f32[32,256]{1,0:T(8,128)S(1)}, u32[]{:S(2)}, u32[]{:S(2)}) collective-permute-start(f32[32,256]{1,0:T(8,128)S(1)} %get-tuple-element.28), channel_id=1, source_target_pairs={{0,96},{16,112},{32,64},{48,80},{64,32},{80,48},{96,0},{112,16},{1... | collective-permute-start | bytes 98312 | tf_op jit(solution)/shard_map/ppermute | solution.py:14
  80.6 1.2 collective-permute-done.12.d_ref
  81.9 2.9 %collective-permute-start.15 = (f32[32,256]{1,0:T(8,128)S(1)}, f32[32,256]{1,0:T(8,128)S(1)}, u32[]{:S(2)}, u32[]{:S(2)}) collective-permute-start(f32[32,256]{1,0:T(8,128)S(1)} %shard_map.44.a_ref), channel_id=1, source_target_pairs={{0,3},{1,2},{2,1},{3,0},{4,7},{5,6},{6,5},{7,4},{8,11},{9,10},{10,... | collective-permute-start | bytes 98312 | tf_op jit(solution)/shard_map/ppermute | solution.py:14
  85.4 3.3 %collective-permute-done.15.d_ref = f32[32,256]{1,0:T(8,128)S(1)} collective-permute-done((f32[32,256]{1,0:T(8,128)S(1)}, f32[32,256]{1,0:T(8,128)S(1)}, u32[]{:S(2)}, u32[]{:S(2)}) %collective-permute-start.15) | collective-permute-done | bytes 32800 | tf_op jit(solution)/shard_map/ppermute | solution.py:14
  89.1 2.5 %collective-permute-start.18 = (f32[32,256]{1,0:T(8,128)S(1)}, f32[32,256]{1,0:T(8,128)S(1)}, u32[]{:S(2)}, u32[]{:S(2)}) collective-permute-start(f32[32,256]{1,0:T(8,128)S(1)} %shard_map.45.a_ref), channel_id=1, source_target_pairs={{0,12},{1,13},{2,14},{3,15},{4,8},{5,9},{6,10},{7,11},{8,4},{9,5},... | collective-permute-start | bytes 98312 | tf_op jit(solution)/shard_map/ppermute | solution.py:14
  93.1 2.7 %collective-permute-done.17.c_ref = f32[32,256]{1,0:T(8,128)S(1)} collective-permute-done((f32[32,256]{1,0:T(8,128)S(1)}, f32[32,256]{1,0:T(8,128)S(1)}, u32[]{:S(2)}, u32[]{:S(2)}) %collective-permute-start.17) | collective-permute-done | bytes 32800 | tf_op jit(solution)/shard_map/ppermute | solution.py:14
  95.8 2.3 %collective-permute-start.21 = (f32[104,256]{1,0:T(8,128)S(1)}, f32[104,256]{1,0:T(8,128)S(1)}, u32[]{:S(2)}, u32[]{:S(2)}) collective-permute-start(f32[104,256]{1,0:T(8,128)S(1)} %shard_map.46.refs_0_), channel_id=1, source_target_pairs={{0,96},{16,112},{32,64},{48,80},{64,32},{80,48},{96,0},{112,16},{1... | collective-permute-start | bytes 319496 | tf_op jit(solution)/shard_map/ppermute | solution.py:14
  99.2 1.8 %collective-permute-done.21.refs_3_ = f32[104,256]{1,0:T(8,128)S(1)} collective-permute-done((f32[104,256]{1,0:T(8,128)S(1)}, f32[104,256]{1,0:T(8,128)S(1)}, u32[]{:S(2)}, u32[]{:S(2)}) %collective-permute-start.21) | collective-permute-done | bytes 106528 | tf_op jit(solution)/shard_map/ppermute | solution.py:14
  100.9 2.3 %collective-permute-done.20.refs_2_ = f32[104,256]{1,0:T(8,128)S(1)} collective-permute-done((f32[104,256]{1,0:T(8,128)S(1)}, f32[104,256]{1,0:T(8,128)S(1)}, u32[]{:S(2)}, u32[]{:S(2)}) %collective-permute-start.20) | collective-permute-done | bytes 106528 | tf_op jit(solution)/shard_map/ppermute | solution.py:14
  103.2 6.0 %collective-permute-start.22 = (f32[4,104,256]{2,1,0:T(8,128)S(1)}, f32[4,104,256]{2,1,0:T(8,128)S(1)}, u32[]{:S(2)}, u32[]{:S(2)}) collective-permute-start(f32[4,104,256]{2,1,0:T(8,128)S(1)} %shard_map.47.own_ref), channel_id=1, source_target_pairs={{0,16},{16,0},{32,48},{48,32},{64,80},{80,64},{96,112},{112,96},{1... | collective-permute-start | bytes 1277960 | tf_op jit(solution)/shard_map/ppermute | solution.py:14
  109.3 1.4 %collective-permute-done.22.other_ref = f32[4,104,256]{2,1,0:T(8,128)S(1)} collective-permute-done((f32[4,104,256]{2,1,0:T(8,128)S(1)}, f32[4,104,256]{2,1,0:T(8,128)S(1)}, u32[]{:S(2)}, u32[]{:S(2)}) %collective-permute-start.22) | collective-permute-done | bytes 426016 | tf_op jit(solution)/shard_map/ppermute | solution.py:14
  110.7 10.5 %shard_map.48.gain_ref = f32[576,256]{1,0:T(8,128)S(1)} custom-call(s32[1]{0:T(128)} %bitcast.2.core_ref, f32[4,104,256]{2,1,0:T(8,128)S(1)} %shard_map.47.own_ref, f32[4,104,256]{2,1,0:T(8,128)S(1)} %collective-permute-done.22.other_ref, f32[1,256]{1,0:T(1,128)S(1)} %bitcast.22), custom_call_target="tpu_custom_call" | custom-call | flops 1342177280 | bytes 786432 | tf_op jit(solution)/shard_map/pallas_call | solution.py:324
  121.2 3.9 %shard_map.49 = f32[576,1152]{1,0:T(8,128)} custom-call(f32[576,1152]{1,0:T(8,128)S(1)} %shard_map.37.cov_ref, f32[1152,256]{1,0:T(8,128)} %bitcast.4.rows_ref, f32[576,256]{1,0:T(8,128)S(1)} %shard_map.48.gain_ref), custom_call_target="tpu_custom_call" | custom-call | flops 1019215872 | bytes 2654208 | tf_op jit(solution)/shard_map/pallas_call | solution.py:219
  (43 shorter events, 13.5 us)
Async XLA Ops:
  1.9 35.9 %all-to-all-start = ((f32[16,72,256]{2,1,0:T(8,128)}), f32[16,72,256]{2,1,0:T(8,128)}, u32[]{:S(2)}, u32[]{:S(2)}) async-start(f32[16,72,256]{2,1,0:T(8,128)} %broadcast_in_dim.4), calls=%async_computation | async-start | bytes 2359296 | tf_op jit(solution)/shard_map/all_to_all | solution.py:40
  9.5 17.2 %collective-permute-start.5 = (f32[72,256]{1,0:T(8,128)S(1)}, f32[72,256]{1,0:T(8,128)S(1)}, u32[]{:S(2)}, u32[]{:S(2)}) collective-permute-start(f32[72,256]{1,0:T(8,128)S(1)} %shard_map.38), channel_id=1, source_target_pairs={{0,0},{1,32},{2,64},{3,96},{4,16},{5,48},{6,80},{7,112},{8,1},{9,3... | collective-permute-start | bytes 221192 | tf_op jit(solution)/shard_map/ppermute | solution.py:18
  26.7 5.1 %collective-permute-start.6 = (f32[72,256]{1,0:T(8,128)S(1)}, f32[72,256]{1,0:T(8,128)S(1)}, u32[]{:S(2)}, u32[]{:S(2)}) collective-permute-start(f32[72,256]{1,0:T(8,128)S(1)} %collective-permute-done.5), channel_id=1, source_target_pairs={{0,32},{16,48},{32,0},{48,16},{64,96},{80,112},{96,64},{112,80},{1... | collective-permute-start | bytes 221192 | tf_op jit(solution)/shard_map/ppermute | solution.py:14
  34.1 8.0 %collective-permute-start.7 = (f32[2,72,256]{2,1,0:T(8,128)}, f32[2,72,256]{2,1,0:T(8,128)}, u32[]{:S(2)}, u32[]{:S(2)}) collective-permute-start(f32[2,72,256]{2,1,0:T(8,128)} %pad_maximum_fusion.1), channel_id=1, source_target_pairs={{0,96},{16,112},{32,64},{48,80},{64,32},{80,48},{96,0},{112,16},{1... | collective-permute-start | bytes 442376 | tf_op jit(solution)/shard_map/ppermute | solution.py:14
  40.4 11.6 %copy-start = (f32[4,72,256]{2,1,0:T(8,128)}, f32[4,72,256]{2,1,0:T(8,128)S(1)}, u32[]{:S(2)}) copy-start(f32[4,72,256]{2,1,0:T(8,128)S(1)} %get-tuple-element.18) | copy-start | bytes 884740
  40.4 2.7 %collective-permute-start = (f32[4,72,256]{2,1,0:T(8,128)S(1)}, f32[4,72,256]{2,1,0:T(8,128)S(1)}, u32[]{:S(2)}, u32[]{:S(2)}) collective-permute-start(f32[4,72,256]{2,1,0:T(8,128)S(1)} %get-tuple-element.18), channel_id=1, source_target_pairs={{0,16},{16,0},{32,48},{48,32},{64,80},{80,64},{96,112},{112,96},{1... | collective-permute-start | bytes 884744 | tf_op jit(solution)/shard_map/ppermute | solution.py:14
  43.2 5.7 %collective-permute-start.1 = (f32[72,256]{1,0:T(8,128)S(1)}, f32[72,256]{1,0:T(8,128)S(1)}, u32[]{:S(2)}, u32[]{:S(2)}) collective-permute-start(f32[72,256]{1,0:T(8,128)S(1)} %get-tuple-element.20), channel_id=1, source_target_pairs={{0,32},{16,48},{32,0},{48,16},{64,96},{80,112},{96,64},{112,80},{1... | collective-permute-start | bytes 221192 | tf_op jit(solution)/shard_map/ppermute | solution.py:14
  44.2 6.3 %collective-permute-start.2 = (f32[72,256]{1,0:T(8,128)S(1)}, f32[72,256]{1,0:T(8,128)S(1)}, u32[]{:S(2)}, u32[]{:S(2)}) collective-permute-start(f32[72,256]{1,0:T(8,128)S(1)} %get-tuple-element.21), channel_id=1, source_target_pairs={{0,64},{16,80},{32,96},{48,112},{64,0},{80,16},{96,32},{112,48},{1... | collective-permute-start | bytes 221192 | tf_op jit(solution)/shard_map/ppermute | solution.py:14
  46.6 5.4 %collective-permute-start.3 = (f32[72,256]{1,0:T(8,128)S(1)}, f32[72,256]{1,0:T(8,128)S(1)}, u32[]{:S(2)}, u32[]{:S(2)}) collective-permute-start(f32[72,256]{1,0:T(8,128)S(1)} %get-tuple-element.22), channel_id=1, source_target_pairs={{0,96},{16,112},{32,64},{48,80},{64,32},{80,48},{96,0},{112,16},{1... | collective-permute-start | bytes 221192 | tf_op jit(solution)/shard_map/ppermute | solution.py:14
  47.1 22.4 %collective-permute-start.8 = (f32[288,256]{1,0:T(8,128)S(1)}, f32[288,256]{1,0:T(8,128)}, u32[]{:S(2)}, u32[]{:S(2)}) collective-permute-start(f32[288,256]{1,0:T(8,128)S(1)} %bitcast.18), channel_id=1, source_target_pairs={{0,16},{16,0},{32,48},{48,32},{64,80},{80,64},{96,112},{112,96},{1... | collective-permute-start | bytes 884744 | tf_op jit(solution)/shard_map/ppermute | solution.py:14
  52.0 8.0 %collective-permute-start.4 = (f32[72,256]{1,0:T(8,128)S(1)}, f32[72,256]{1,0:T(8,128)S(1)}, u32[]{:S(2)}, u32[]{:S(2)}) collective-permute-start(f32[72,256]{1,0:T(8,128)S(1)} %shard_map.41.product_ref), channel_id=1, source_target_pairs={{0,0},{1,8},{2,16},{3,24},{4,32},{5,40},{6,48},{7,56},{8,64},{9,72... | collective-permute-start | bytes 221192 | tf_op jit(solution)/shard_map/ppermute | solution.py:18
  61.0 60.1 %all-to-all-start.1 = ((f32[16,72,256]{2,1,0:T(8,128)}), f32[16,72,256]{2,1,0:T(8,128)}, u32[]{:S(2)}, u32[]{:S(2)}) async-start(f32[16,72,256]{2,1,0:T(8,128)} %broadcast_in_dim.5), calls=%async_computation.1 | async-start | bytes 2359296 | tf_op jit(solution)/shard_map/all_to_all | solution.py:40
  69.6 1.0 copy-start.1
  70.5 40.2 %copy-start.2 = (f32[2,128]{1,0:T(2,128)S(1)}, f32[2,128]{1,0:T(2,128)}, u32[]{:S(2)}) copy-start(f32[2,128]{1,0:T(2,128)} %param.5) | copy-start | bytes 3076
  72.1 3.6 %collective-permute-start.9 = (f32[4,32,256]{2,1,0:T(8,128)S(1)}, f32[4,32,256]{2,1,0:T(8,128)S(1)}, u32[]{:S(2)}, u32[]{:S(2)}) collective-permute-start(f32[4,32,256]{2,1,0:T(8,128)S(1)} %get-tuple-element.24), channel_id=1, source_target_pairs={{0,16},{16,0},{32,48},{48,32},{64,80},{80,64},{96,112},{112,96},{1... | collective-permute-start | bytes 393224 | tf_op jit(solution)/shard_map/ppermute | solution.py:14
  75.8 3.9 %collective-permute-start.10 = (f32[32,256]{1,0:T(8,128)S(1)}, f32[32,256]{1,0:T(8,128)S(1)}, u32[]{:S(2)}, u32[]{:S(2)}) collective-permute-start(f32[32,256]{1,0:T(8,128)S(1)} %get-tuple-element.26), channel_id=1, source_target_pairs={{0,32},{16,48},{32,0},{48,16},{64,96},{80,112},{96,64},{112,80},{1... | collective-permute-start | bytes 98312 | tf_op jit(solution)/shard_map/ppermute | solution.py:14
  75.9 4.7 %collective-permute-start.11 = (f32[32,256]{1,0:T(8,128)S(1)}, f32[32,256]{1,0:T(8,128)S(1)}, u32[]{:S(2)}, u32[]{:S(2)}) collective-permute-start(f32[32,256]{1,0:T(8,128)S(1)} %get-tuple-element.27), channel_id=1, source_target_pairs={{0,64},{16,80},{32,96},{48,112},{64,0},{80,16},{96,32},{112,48},{1... | collective-permute-start | bytes 98312 | tf_op jit(solution)/shard_map/ppermute | solution.py:14
  77.1 4.7 %collective-permute-start.12 = (f32[32,256]{1,0:T(8,128)S(1)}, f32[32,256]{1,0:T(8,128)S(1)}, u32[]{:S(2)}, u32[]{:S(2)}) collective-permute-start(f32[32,256]{1,0:T(8,128)S(1)} %get-tuple-element.28), channel_id=1, source_target_pairs={{0,96},{16,112},{32,64},{48,80},{64,32},{80,48},{96,0},{112,16},{1... | collective-permute-start | bytes 98312 | tf_op jit(solution)/shard_map/ppermute | solution.py:14
  81.9 6.8 %collective-permute-start.15 = (f32[32,256]{1,0:T(8,128)S(1)}, f32[32,256]{1,0:T(8,128)S(1)}, u32[]{:S(2)}, u32[]{:S(2)}) collective-permute-start(f32[32,256]{1,0:T(8,128)S(1)} %shard_map.44.a_ref), channel_id=1, source_target_pairs={{0,3},{1,2},{2,1},{3,0},{4,7},{5,6},{6,5},{7,4},{8,11},{9,10},{10,... | collective-permute-start | bytes 98312 | tf_op jit(solution)/shard_map/ppermute | solution.py:14
  84.8 4.3 %collective-permute-start.14 = (f32[32,256]{1,0:T(8,128)S(1)}, f32[32,256]{1,0:T(8,128)S(1)}, u32[]{:S(2)}, u32[]{:S(2)}) collective-permute-start(f32[32,256]{1,0:T(8,128)S(1)} %shard_map.44.a_ref), channel_id=1, source_target_pairs={{0,2},{1,3},{2,0},{3,1},{4,6},{5,7},{6,4},{7,5},{8,10},{9,11},{10,... | collective-permute-start | bytes 98312 | tf_op jit(solution)/shard_map/ppermute | solution.py:14
  85.4 3.6 %collective-permute-start.13 = (f32[32,256]{1,0:T(8,128)S(1)}, f32[32,256]{1,0:T(8,128)S(1)}, u32[]{:S(2)}, u32[]{:S(2)}) collective-permute-start(f32[32,256]{1,0:T(8,128)S(1)} %shard_map.44.a_ref), channel_id=1, source_target_pairs={{0,1},{1,0},{2,3},{3,2},{4,5},{5,4},{6,7},{7,6},{8,9},{9,8},{10,11... | collective-permute-start | bytes 98312 | tf_op jit(solution)/shard_map/ppermute | solution.py:14
  89.1 4.1 %collective-permute-start.18 = (f32[32,256]{1,0:T(8,128)S(1)}, f32[32,256]{1,0:T(8,128)S(1)}, u32[]{:S(2)}, u32[]{:S(2)}) collective-permute-start(f32[32,256]{1,0:T(8,128)S(1)} %shard_map.45.a_ref), channel_id=1, source_target_pairs={{0,12},{1,13},{2,14},{3,15},{4,8},{5,9},{6,10},{7,11},{8,4},{9,5},... | collective-permute-start | bytes 98312 | tf_op jit(solution)/shard_map/ppermute | solution.py:14
  91.5 4.3 %collective-permute-start.17 = (f32[32,256]{1,0:T(8,128)S(1)}, f32[32,256]{1,0:T(8,128)S(1)}, u32[]{:S(2)}, u32[]{:S(2)}) collective-permute-start(f32[32,256]{1,0:T(8,128)S(1)} %shard_map.45.a_ref), channel_id=1, source_target_pairs={{0,8},{1,9},{2,10},{3,11},{4,12},{5,13},{6,14},{7,15},{8,0},{9,1},... | collective-permute-start | bytes 98312 | tf_op jit(solution)/shard_map/ppermute | solution.py:14
  92.1 3.7 %collective-permute-start.16 = (f32[32,256]{1,0:T(8,128)S(1)}, f32[32,256]{1,0:T(8,128)S(1)}, u32[]{:S(2)}, u32[]{:S(2)}) collective-permute-start(f32[32,256]{1,0:T(8,128)S(1)} %shard_map.45.a_ref), channel_id=1, source_target_pairs={{0,4},{1,5},{2,6},{3,7},{4,0},{5,1},{6,2},{7,3},{8,12},{9,13},{10,... | collective-permute-start | bytes 98312 | tf_op jit(solution)/shard_map/ppermute | solution.py:14
  95.8 5.1 %collective-permute-start.21 = (f32[104,256]{1,0:T(8,128)S(1)}, f32[104,256]{1,0:T(8,128)S(1)}, u32[]{:S(2)}, u32[]{:S(2)}) collective-permute-start(f32[104,256]{1,0:T(8,128)S(1)} %shard_map.46.refs_0_), channel_id=1, source_target_pairs={{0,96},{16,112},{32,64},{48,80},{64,32},{80,48},{96,0},{112,16},{1... | collective-permute-start | bytes 319496 | tf_op jit(solution)/shard_map/ppermute | solution.py:14
  98.1 5.1 %collective-permute-start.20 = (f32[104,256]{1,0:T(8,128)S(1)}, f32[104,256]{1,0:T(8,128)S(1)}, u32[]{:S(2)}, u32[]{:S(2)}) collective-permute-start(f32[104,256]{1,0:T(8,128)S(1)} %shard_map.46.refs_0_), channel_id=1, source_target_pairs={{0,64},{16,80},{32,96},{48,112},{64,0},{80,16},{96,32},{112,48},{1... | collective-permute-start | bytes 319496 | tf_op jit(solution)/shard_map/ppermute | solution.py:14
  98.2 5.1 %collective-permute-start.19 = (f32[104,256]{1,0:T(8,128)S(1)}, f32[104,256]{1,0:T(8,128)S(1)}, u32[]{:S(2)}, u32[]{:S(2)}) collective-permute-start(f32[104,256]{1,0:T(8,128)S(1)} %shard_map.46.refs_0_), channel_id=1, source_target_pairs={{0,32},{16,48},{32,0},{48,16},{64,96},{80,112},{96,64},{112,80},{1... | collective-permute-start | bytes 319496 | tf_op jit(solution)/shard_map/ppermute | solution.py:14
  103.2 7.4 %collective-permute-start.22 = (f32[4,104,256]{2,1,0:T(8,128)S(1)}, f32[4,104,256]{2,1,0:T(8,128)S(1)}, u32[]{:S(2)}, u32[]{:S(2)}) collective-permute-start(f32[4,104,256]{2,1,0:T(8,128)S(1)} %shard_map.47.own_ref), channel_id=1, source_target_pairs={{0,16},{16,0},{32,48},{48,32},{64,80},{80,64},{96,112},{112,96},{1... | collective-permute-start | bytes 1277960 | tf_op jit(solution)/shard_map/ppermute | solution.py:14
